TPU v7x, 512 devices: a whole 4x4x16 slice. The times are simulated.
512 devices in a mesh: gx: 8 (over y, core), gy: 16 (over x, z_lo), gz: 4 (over z_hi).
Axes of the slice: x: 4, y: 4, z: 16 (z_hi: 4, z_lo: 4; z = z_hi * 4 + z_lo), core: 2. Of those that a mesh axis runs over, the one named last changes fastest.
Arguments:
- right_side: float32 [128, 256, 1024], P('gz', 'gy', 'gx'), may hold values from -33 to 33
- initial: float32 [128, 256, 1024], P('gz', 'gy', 'gx'), may hold values from -4 to 4
- kappa_sq: float32 [128, 256, 1024], P('gz', 'gy', 'gx'), may hold values from 0.0004 to 4
Outputs:
- solution: float32 [128, 256, 1024], P('gz', 'gy', 'gx')
- residual: float32 [128, 256, 1024], P('gz', 'gy', 'gx')
All inputs are finite; a program needn't handle non-finite values.
Results may differ from a plain program's by a relative error of at most 0.0001.
Values sent between devices are 32-bit elements; how exact they have to be, the bound alone decides.
No kernel may reach another device: no remote copies, remote signals or barrier semaphores. Data moves between devices by JAX's collectives and lax.ppermute only.
A program may use at most 64 MiB of HBM per device.

v0:
```python
import jax
import jax.numpy as jnp
from jax import lax
from jax.sharding import PartitionSpec as P

ITERS = 2
SWEEPS = 3


cheb_high = 7.2
cheb_low = 0.072


def padded_2(x, sides, width):
    for axis, dim in sides:
        devices, length = (lax.axis_size(axis), x.shape[dim])
        up = [(i, (i + 1) % devices) for i in range(devices - 1)]
        down = [(j, i) for i, j in up]
        last = lax.slice_in_dim(x, length - width, length, axis=dim)
        first = lax.slice_in_dim(x, 0, width, axis=dim)
        before = lax.ppermute(last, axis, up)
        after = lax.ppermute(first, axis, down)
        x = jnp.concatenate([before, x, after], axis=dim)
    return x


def neighbours(padded):
    total = padded[2:, 1:-1, 1:-1] + padded[:-2, 1:-1, 1:-1]
    total = total + padded[1:-1, 2:, 1:-1] + padded[1:-1, :-2, 1:-1]
    total = total + padded[1:-1, 1:-1, 2:] + padded[1:-1, 1:-1, :-2]
    return total


def stencil_single(values, kappa_sq):
    padded = padded_2(values, (("gx", 2), ("gy", 1), ("gz", 0)), 1)
    return ((6.0 + kappa_sq) * values - neighbours(padded)) / 6.0


def precondition(source, apply_q):
    centre = (cheb_high + cheb_low) / 2.0
    half_width = (cheb_high - cheb_low) / 2.0
    ratio_sigma = centre / half_width
    weight_old = 1.0 / ratio_sigma
    update = source / centre
    result = update
    for sweep in range(SWEEPS - 1):
        defect = source - apply_q(result)
        weight_new = 1.0 / (2.0 * ratio_sigma - weight_old)
        update = weight_new * weight_old * update + 2.0 * weight_new / half_width * defect
        result = result + update
        weight_old = weight_new
    return result


def global_dot(first_field, second_field):
    return lax.psum(jnp.sum(first_field * second_field), ("gx", "gy", "gz"))


def body(right_side, initial, kappa_sq):

    def apply_q(values):
        return stencil_single(stencil_single(values, kappa_sq), kappa_sq)

    def precond_of(values):
        return precondition(values, apply_q)

    solution = initial
    residual = right_side - apply_q(initial)
    precond = precond_of(residual)
    direction = precond
    energy = global_dot(residual, precond)
    for step in range(ITERS):
        applied = apply_q(direction)
        step_size = energy / global_dot(direction, applied)
        solution = solution + step_size * direction
        residual = residual - step_size * applied
        if step + 1 < ITERS:
            precond = precond_of(residual)
            energy_new = global_dot(residual, precond)
            direction = precond + energy_new / energy * direction
            energy = energy_new
    return (solution, residual)


def solution(mesh):
    in_specs = (P("gz", "gy", "gx"), P("gz", "gy", "gx"), P("gz", "gy", "gx"))
    out_specs = (P("gz", "gy", "gx"), P("gz", "gy", "gx"))
    return jax.shard_map(body, mesh=mesh, in_specs=in_specs, out_specs=out_specs, check_vma=False)
```

profile of v0, /device:TPU:1, one launch (start us, length us, event | category | flops | bytes accessed | tf_op | source)
XLA Modules:
  0.0 797.2 jit_solution(1967811583596469259)
XLA Ops:
  1.9 8.7 %collective-permute-start.1 = (f32[32,16,1]{2,1,0:T(8,128)S(1)}, f32[32,16,1]{2,1,0:T(8,128)S(1)}, u32[]{:S(2)}, u32[]{:S(2)}) collective-permute-start(f32[32,16,1]{2,1,0:T(8,128)S(1)} %get-tuple-element.101), channel_id=1, source_target_pairs={{64,0},{128,64},{192,128},{256,192},{320,256},{384,320},{448,384},... | collective-permute-start | bytes 6152 | tf_op jit(solution)/shard_map/ppermute | solution.py:22
  12.6 3.3 collective-permute-done
  17.4 4.1 collective-permute-start.2
  24.0 7.9 collective-permute-start.5
  33.6 2.5 collective-permute-start.7
  36.1 6.1 collective-permute-start.6
  42.2 2.1 collective-permute-done.7
  47.1 4.7 collective-permute-start.8
  54.2 8.5 %collective-permute-start.11 = (f32[1,18,130]{2,1,0:T(8,128)S(1)}, f32[1,18,130]{2,1,0:T(8,128)S(1)}, u32[]{:S(2)}, u32[]{:S(2)}) collective-permute-start(f32[1,18,130]{2,1,0:T(8,128)S(1)} %get-tuple-element.44), channel_id=1, source_target_pairs={{0,1},{1,2},{2,3},{4,5},{5,6},{6,7},{8,9},{9,10},{10,11},{12,13},{... | collective-permute-start | bytes 28088 | tf_op jit(solution)/shard_map/ppermute | solution.py:21
  64.4 1.9 collective-permute-start.13
  66.4 6.1 collective-permute-start.12
  72.5 2.1 collective-permute-done.13
  77.3 4.6 collective-permute-start.14
  84.3 8.5 %collective-permute-start.17 = (f32[1,18,130]{2,1,0:T(8,128)S(1)}, f32[1,18,130]{2,1,0:T(8,128)S(1)}, u32[]{:S(2)}, u32[]{:S(2)}) collective-permute-start(f32[1,18,130]{2,1,0:T(8,128)S(1)} %get-tuple-element.42), channel_id=1, source_target_pairs={{0,1},{1,2},{2,3},{4,5},{5,6},{6,7},{8,9},{9,10},{10,11},{12,13},{... | collective-permute-start | bytes 28088 | tf_op jit(solution)/shard_map/ppermute | solution.py:21
  96.5 6.1 collective-permute-start.18
  102.6 2.1 collective-permute-done.19
  107.5 4.6 collective-permute-start.20
  114.4 8.7 %collective-permute-start.23 = (f32[1,18,130]{2,1,0:T(8,128)S(1)}, f32[1,18,130]{2,1,0:T(8,128)S(1)}, u32[]{:S(2)}, u32[]{:S(2)}) collective-permute-start(f32[1,18,130]{2,1,0:T(8,128)S(1)} %get-tuple-element.40), channel_id=1, source_target_pairs={{0,1},{1,2},{2,3},{4,5},{5,6},{6,7},{8,9},{9,10},{10,11},{12,13},{... | collective-permute-start | bytes 28088 | tf_op jit(solution)/shard_map/ppermute | solution.py:21
  126.9 6.1 collective-permute-start.24
  133.0 2.1 collective-permute-done.25
  137.8 5.7 collective-permute-start.26
  146.0 8.5 %collective-permute-start.29 = (f32[1,18,130]{2,1,0:T(8,128)S(1)}, f32[1,18,130]{2,1,0:T(8,128)S(1)}, u32[]{:S(2)}, u32[]{:S(2)}) collective-permute-start(f32[1,18,130]{2,1,0:T(8,128)S(1)} %get-tuple-element.38), channel_id=1, source_target_pairs={{0,1},{1,2},{2,3},{4,5},{5,6},{6,7},{8,9},{9,10},{10,11},{12,13},{... | collective-permute-start | bytes 28088 | tf_op jit(solution)/shard_map/ppermute | solution.py:21
  158.1 6.1 collective-permute-start.30
  164.2 2.1 collective-permute-done.31
  169.1 7.6 collective-permute-start.32
  179.0 8.5 %collective-permute-start.35 = (f32[1,18,130]{2,1,0:T(8,128)S(1)}, f32[1,18,130]{2,1,0:T(8,128)S(1)}, u32[]{:S(2)}, u32[]{:S(2)}) collective-permute-start(f32[1,18,130]{2,1,0:T(8,128)S(1)} %get-tuple-element.36), channel_id=1, source_target_pairs={{0,1},{1,2},{2,3},{4,5},{5,6},{6,7},{8,9},{9,10},{10,11},{12,13},{... | collective-permute-start | bytes 28088 | tf_op jit(solution)/shard_map/ppermute | solution.py:21
  191.3 6.1 collective-permute-start.36
  197.4 2.1 collective-permute-done.37
  202.3 7.3 collective-permute-start.38
  212.0 8.5 %collective-permute-start.41 = (f32[1,18,130]{2,1,0:T(8,128)S(1)}, f32[1,18,130]{2,1,0:T(8,128)S(1)}, u32[]{:S(2)}, u32[]{:S(2)}) collective-permute-start(f32[1,18,130]{2,1,0:T(8,128)S(1)} %get-tuple-element.34), channel_id=1, source_target_pairs={{0,1},{1,2},{2,3},{4,5},{5,6},{6,7},{8,9},{9,10},{10,11},{12,13},{... | collective-permute-start | bytes 28088 | tf_op jit(solution)/shard_map/ppermute | solution.py:21
  224.2 6.1 collective-permute-start.42
  230.3 2.1 collective-permute-done.43
  235.1 7.3 collective-permute-start.44
  244.8 8.6 %collective-permute-start.47 = (f32[1,18,130]{2,1,0:T(8,128)S(1)}, f32[1,18,130]{2,1,0:T(8,128)S(1)}, u32[]{:S(2)}, u32[]{:S(2)}) collective-permute-start(f32[1,18,130]{2,1,0:T(8,128)S(1)} %get-tuple-element.32), channel_id=1, source_target_pairs={{0,1},{1,2},{2,3},{4,5},{5,6},{6,7},{8,9},{9,10},{10,11},{12,13},{... | collective-permute-start | bytes 28088 | tf_op jit(solution)/shard_map/ppermute | solution.py:21
  255.5 125.1 %all-reduce = (f32[]{:T(128)}, f32[]{:T(128)}) all-reduce(f32[]{:T(128)} %get-tuple-element.3, f32[]{:T(128)} %get-tuple-element.2), channel_id=1, replica_groups=mesh['gx'=8,'gy'=16,'gz'=4] {'gx','gy','gz'}, use_global_device_ids=true, to_apply=%region_1.0 | all-reduce | flops 2 | bytes 16 | tf_op jit(solution)/shard_map/psum | solution.py:56
  382.2 2.9 collective-permute-start.49
  385.1 2.7 collective-permute-start.48
  387.8 2.1 collective-permute-done.49
  392.6 4.2 collective-permute-start.50
  399.2 7.9 collective-permute-start.53
  408.9 1.9 collective-permute-start.55
  410.8 6.4 collective-permute-start.54
  417.3 2.1 collective-permute-done.55
  422.1 4.6 collective-permute-start.56
  429.1 8.5 %collective-permute-start.59 = (f32[1,18,130]{2,1,0:T(8,128)S(1)}, f32[1,18,130]{2,1,0:T(8,128)S(1)}, u32[]{:S(2)}, u32[]{:S(2)}) collective-permute-start(f32[1,18,130]{2,1,0:T(8,128)S(1)} %get-tuple-element.28), channel_id=1, source_target_pairs={{0,1},{1,2},{2,3},{4,5},{5,6},{6,7},{8,9},{9,10},{10,11},{12,13},{... | collective-permute-start | bytes 28088 | tf_op jit(solution)/shard_map/ppermute | solution.py:21
  441.3 6.1 collective-permute-start.60
  447.4 2.1 collective-permute-done.61
  452.3 4.6 collective-permute-start.62
  459.2 8.5 %collective-permute-start.65 = (f32[1,18,130]{2,1,0:T(8,128)S(1)}, f32[1,18,130]{2,1,0:T(8,128)S(1)}, u32[]{:S(2)}, u32[]{:S(2)}) collective-permute-start(f32[1,18,130]{2,1,0:T(8,128)S(1)} %get-tuple-element.26), channel_id=1, source_target_pairs={{0,1},{1,2},{2,3},{4,5},{5,6},{6,7},{8,9},{9,10},{10,11},{12,13},{... | collective-permute-start | bytes 28088 | tf_op jit(solution)/shard_map/ppermute | solution.py:21
  471.4 6.1 collective-permute-start.66
  477.5 2.1 collective-permute-done.67
  482.4 4.6 collective-permute-start.68
  489.3 8.6 %collective-permute-start.71 = (f32[1,18,130]{2,1,0:T(8,128)S(1)}, f32[1,18,130]{2,1,0:T(8,128)S(1)}, u32[]{:S(2)}, u32[]{:S(2)}) collective-permute-start(f32[1,18,130]{2,1,0:T(8,128)S(1)} %get-tuple-element.24), channel_id=1, source_target_pairs={{0,1},{1,2},{2,3},{4,5},{5,6},{6,7},{8,9},{9,10},{10,11},{12,13},{... | collective-permute-start | bytes 28088 | tf_op jit(solution)/shard_map/ppermute | solution.py:21
  500.1 122.1 %psum.30 = f32[]{:T(128)} all-reduce(f32[]{:T(128)} %get-tuple-element.8), channel_id=1, replica_groups=mesh['gx'=8,'gy'=16,'gz'=4] {'gx','gy','gz'}, use_global_device_ids=true, to_apply=%region_5.0 | all-reduce | flops 1 | bytes 8 | tf_op jit(solution)/shard_map/psum | solution.py:56
  623.8 2.6 collective-permute-start.73
  626.4 3.0 collective-permute-start.72
  629.4 2.1 collective-permute-done.73
  634.2 4.0 collective-permute-start.74
  640.6 7.9 collective-permute-start.77
  652.2 6.7 collective-permute-start.78
  658.9 2.4 collective-permute-done.79
  663.7 4.6 collective-permute-start.80
  670.7 8.6 %collective-permute-start.83 = (f32[1,18,130]{2,1,0:T(8,128)S(1)}, f32[1,18,130]{2,1,0:T(8,128)S(1)}, u32[]{:S(2)}, u32[]{:S(2)}) collective-permute-start(f32[1,18,130]{2,1,0:T(8,128)S(1)} %get-tuple-element.20), channel_id=1, source_target_pairs={{0,1},{1,2},{2,3},{4,5},{5,6},{6,7},{8,9},{9,10},{10,11},{12,13},{... | collective-permute-start | bytes 28088 | tf_op jit(solution)/shard_map/ppermute | solution.py:21
  681.5 113.5 %psum.31 = f32[]{:T(128)} all-reduce(f32[]{:T(128)} %get-tuple-element.6), channel_id=1, replica_groups=mesh['gx'=8,'gy'=16,'gz'=4] {'gx','gy','gz'}, use_global_device_ids=true, to_apply=%region_7.0 | all-reduce | flops 1 | bytes 8 | tf_op jit(solution)/shard_map/psum | solution.py:56
  (172 shorter events, 115.5 us)
Async XLA Ops:
  1.9 10.7 %collective-permute-start.1 = (f32[32,16,1]{2,1,0:T(8,128)S(1)}, f32[32,16,1]{2,1,0:T(8,128)S(1)}, u32[]{:S(2)}, u32[]{:S(2)}) collective-permute-start(f32[32,16,1]{2,1,0:T(8,128)S(1)} %get-tuple-element.101), channel_id=1, source_target_pairs={{64,0},{128,64},{192,128},{256,192},{320,256},{384,320},{448,384},... | collective-permute-start | bytes 6152 | tf_op jit(solution)/shard_map/ppermute | solution.py:22
  22.7 9.2 %collective-permute-start.4 = (f32[1,18,130]{2,1,0:T(8,128)S(1)}, f32[1,18,130]{2,1,0:T(8,128)S(1)}, u32[]{:S(2)}, u32[]{:S(2)}) collective-permute-start(f32[1,18,130]{2,1,0:T(8,128)S(1)} %get-tuple-element.45), channel_id=1, source_target_pairs={{1,0},{2,1},{3,2},{5,4},{6,5},{7,6},{9,8},{10,9},{11,10},{13,12},{... | collective-permute-start | bytes 28088 | tf_op jit(solution)/shard_map/ppermute | solution.py:22
  24.0 8.8 %collective-permute-start.5 = (f32[1,18,130]{2,1,0:T(8,128)S(1)}, f32[1,18,130]{2,1,0:T(8,128)S(1)}, u32[]{:S(2)}, u32[]{:S(2)}) collective-permute-start(f32[1,18,130]{2,1,0:T(8,128)S(1)} %get-tuple-element.46), channel_id=1, source_target_pairs={{0,1},{1,2},{2,3},{4,5},{5,6},{6,7},{8,9},{9,10},{10,11},{12,13},{... | collective-permute-start | bytes 28088 | tf_op jit(solution)/shard_map/ppermute | solution.py:21
  33.6 10.7 %collective-permute-start.7 = (f32[32,16,1]{2,1,0:T(8,128)S(1)}, f32[32,16,1]{2,1,0:T(8,128)S(1)}, u32[]{:S(2)}, u32[]{:S(2)}) collective-permute-start(f32[32,16,1]{2,1,0:T(8,128)S(1)} %get-tuple-element.99), channel_id=1, source_target_pairs={{64,0},{128,64},{192,128},{256,192},{320,256},{384,320},{448,384},... | collective-permute-start | bytes 6152 | tf_op jit(solution)/shard_map/ppermute | solution.py:22
  36.1 9.4 %collective-permute-start.6 = (f32[32,16,1]{2,1,0:T(8,128)S(1)}, f32[32,16,1]{2,1,0:T(8,128)S(1)}, u32[]{:S(2)}, u32[]{:S(2)}) collective-permute-start(f32[32,16,1]{2,1,0:T(8,128)S(1)} %get-tuple-element.100), channel_id=1, source_target_pairs={{0,64},{64,128},{128,192},{192,256},{256,320},{320,384},{384,448},... | collective-permute-start | bytes 6152 | tf_op jit(solution)/shard_map/ppermute | solution.py:21
  45.8 6.0 collective-permute-start.9
  52.9 9.8 %collective-permute-start.10 = (f32[1,18,130]{2,1,0:T(8,128)S(1)}, f32[1,18,130]{2,1,0:T(8,128)S(1)}, u32[]{:S(2)}, u32[]{:S(2)}) collective-permute-start(f32[1,18,130]{2,1,0:T(8,128)S(1)} %get-tuple-element.43), channel_id=1, source_target_pairs={{1,0},{2,1},{3,2},{5,4},{6,5},{7,6},{9,8},{10,9},{11,10},{13,12},{... | collective-permute-start | bytes 28088 | tf_op jit(solution)/shard_map/ppermute | solution.py:22
  54.2 9.4 %collective-permute-start.11 = (f32[1,18,130]{2,1,0:T(8,128)S(1)}, f32[1,18,130]{2,1,0:T(8,128)S(1)}, u32[]{:S(2)}, u32[]{:S(2)}) collective-permute-start(f32[1,18,130]{2,1,0:T(8,128)S(1)} %get-tuple-element.44), channel_id=1, source_target_pairs={{0,1},{1,2},{2,3},{4,5},{5,6},{6,7},{8,9},{9,10},{10,11},{12,13},{... | collective-permute-start | bytes 28088 | tf_op jit(solution)/shard_map/ppermute | solution.py:21
  64.4 10.1 %collective-permute-start.13 = (f32[32,16,1]{2,1,0:T(8,128)S(1)}, f32[32,16,1]{2,1,0:T(8,128)S(1)}, u32[]{:S(2)}, u32[]{:S(2)}) collective-permute-start(f32[32,16,1]{2,1,0:T(8,128)S(1)} %get-tuple-element.97), channel_id=1, source_target_pairs={{64,0},{128,64},{192,128},{256,192},{320,256},{384,320},{448,384},... | collective-permute-start | bytes 6152 | tf_op jit(solution)/shard_map/ppermute | solution.py:22
  66.4 9.4 %collective-permute-start.12 = (f32[32,16,1]{2,1,0:T(8,128)S(1)}, f32[32,16,1]{2,1,0:T(8,128)S(1)}, u32[]{:S(2)}, u32[]{:S(2)}) collective-permute-start(f32[32,16,1]{2,1,0:T(8,128)S(1)} %get-tuple-element.98), channel_id=1, source_target_pairs={{0,64},{64,128},{128,192},{192,256},{256,320},{320,384},{384,448},... | collective-permute-start | bytes 6152 | tf_op jit(solution)/shard_map/ppermute | solution.py:21
  83.0 9.8 %collective-permute-start.16 = (f32[1,18,130]{2,1,0:T(8,128)S(1)}, f32[1,18,130]{2,1,0:T(8,128)S(1)}, u32[]{:S(2)}, u32[]{:S(2)}) collective-permute-start(f32[1,18,130]{2,1,0:T(8,128)S(1)} %get-tuple-element.41), channel_id=1, source_target_pairs={{1,0},{2,1},{3,2},{5,4},{6,5},{7,6},{9,8},{10,9},{11,10},{13,12},{... | collective-permute-start | bytes 28088 | tf_op jit(solution)/shard_map/ppermute | solution.py:22
  84.3 9.4 %collective-permute-start.17 = (f32[1,18,130]{2,1,0:T(8,128)S(1)}, f32[1,18,130]{2,1,0:T(8,128)S(1)}, u32[]{:S(2)}, u32[]{:S(2)}) collective-permute-start(f32[1,18,130]{2,1,0:T(8,128)S(1)} %get-tuple-element.42), channel_id=1, source_target_pairs={{0,1},{1,2},{2,3},{4,5},{5,6},{6,7},{8,9},{9,10},{10,11},{12,13},{... | collective-permute-start | bytes 28088 | tf_op jit(solution)/shard_map/ppermute | solution.py:21
  94.6 10.1 %collective-permute-start.19 = (f32[32,16,1]{2,1,0:T(8,128)S(1)}, f32[32,16,1]{2,1,0:T(8,128)S(1)}, u32[]{:S(2)}, u32[]{:S(2)}) collective-permute-start(f32[32,16,1]{2,1,0:T(8,128)S(1)} %get-tuple-element.95), channel_id=1, source_target_pairs={{64,0},{128,64},{192,128},{256,192},{320,256},{384,320},{448,384},... | collective-permute-start | bytes 6152 | tf_op jit(solution)/shard_map/ppermute | solution.py:22
  96.5 9.4 %collective-permute-start.18 = (f32[32,16,1]{2,1,0:T(8,128)S(1)}, f32[32,16,1]{2,1,0:T(8,128)S(1)}, u32[]{:S(2)}, u32[]{:S(2)}) collective-permute-start(f32[32,16,1]{2,1,0:T(8,128)S(1)} %get-tuple-element.96), channel_id=1, source_target_pairs={{0,64},{64,128},{128,192},{192,256},{256,320},{320,384},{384,448},... | collective-permute-start | bytes 6152 | tf_op jit(solution)/shard_map/ppermute | solution.py:21
  113.1 10.0 %collective-permute-start.22 = (f32[1,18,130]{2,1,0:T(8,128)S(1)}, f32[1,18,130]{2,1,0:T(8,128)S(1)}, u32[]{:S(2)}, u32[]{:S(2)}) collective-permute-start(f32[1,18,130]{2,1,0:T(8,128)S(1)} %get-tuple-element.39), channel_id=1, source_target_pairs={{1,0},{2,1},{3,2},{5,4},{6,5},{7,6},{9,8},{10,9},{11,10},{13,12},{... | collective-permute-start | bytes 28088 | tf_op jit(solution)/shard_map/ppermute | solution.py:22
  114.4 9.7 %collective-permute-start.23 = (f32[1,18,130]{2,1,0:T(8,128)S(1)}, f32[1,18,130]{2,1,0:T(8,128)S(1)}, u32[]{:S(2)}, u32[]{:S(2)}) collective-permute-start(f32[1,18,130]{2,1,0:T(8,128)S(1)} %get-tuple-element.40), channel_id=1, source_target_pairs={{0,1},{1,2},{2,3},{4,5},{5,6},{6,7},{8,9},{9,10},{10,11},{12,13},{... | collective-permute-start | bytes 28088 | tf_op jit(solution)/shard_map/ppermute | solution.py:21
  124.9 10.1 %collective-permute-start.25 = (f32[32,16,1]{2,1,0:T(8,128)S(1)}, f32[32,16,1]{2,1,0:T(8,128)S(1)}, u32[]{:S(2)}, u32[]{:S(2)}) collective-permute-start(f32[32,16,1]{2,1,0:T(8,128)S(1)} %get-tuple-element.93), channel_id=1, source_target_pairs={{64,0},{128,64},{192,128},{256,192},{320,256},{384,320},{448,384},... | collective-permute-start | bytes 6152 | tf_op jit(solution)/shard_map/ppermute | solution.py:22
  126.9 9.4 %collective-permute-start.24 = (f32[32,16,1]{2,1,0:T(8,128)S(1)}, f32[32,16,1]{2,1,0:T(8,128)S(1)}, u32[]{:S(2)}, u32[]{:S(2)}) collective-permute-start(f32[32,16,1]{2,1,0:T(8,128)S(1)} %get-tuple-element.94), channel_id=1, source_target_pairs={{0,64},{64,128},{128,192},{192,256},{256,320},{320,384},{384,448},... | collective-permute-start | bytes 6152 | tf_op jit(solution)/shard_map/ppermute | solution.py:21
  136.5 7.0 collective-permute-start.27
  137.8 6.7 collective-permute-start.26
  144.7 9.8 %collective-permute-start.28 = (f32[1,18,130]{2,1,0:T(8,128)S(1)}, f32[1,18,130]{2,1,0:T(8,128)S(1)}, u32[]{:S(2)}, u32[]{:S(2)}) collective-permute-start(f32[1,18,130]{2,1,0:T(8,128)S(1)} %get-tuple-element.37), channel_id=1, source_target_pairs={{1,0},{2,1},{3,2},{5,4},{6,5},{7,6},{9,8},{10,9},{11,10},{13,12},{... | collective-permute-start | bytes 28088 | tf_op jit(solution)/shard_map/ppermute | solution.py:22
  146.0 9.4 %collective-permute-start.29 = (f32[1,18,130]{2,1,0:T(8,128)S(1)}, f32[1,18,130]{2,1,0:T(8,128)S(1)}, u32[]{:S(2)}, u32[]{:S(2)}) collective-permute-start(f32[1,18,130]{2,1,0:T(8,128)S(1)} %get-tuple-element.38), channel_id=1, source_target_pairs={{0,1},{1,2},{2,3},{4,5},{5,6},{6,7},{8,9},{9,10},{10,11},{12,13},{... | collective-permute-start | bytes 28088 | tf_op jit(solution)/shard_map/ppermute | solution.py:21
  156.2 10.1 %collective-permute-start.31 = (f32[32,16,1]{2,1,0:T(8,128)S(1)}, f32[32,16,1]{2,1,0:T(8,128)S(1)}, u32[]{:S(2)}, u32[]{:S(2)}) collective-permute-start(f32[32,16,1]{2,1,0:T(8,128)S(1)} %get-tuple-element.91), channel_id=1, source_target_pairs={{64,0},{128,64},{192,128},{256,192},{320,256},{384,320},{448,384},... | collective-permute-start | bytes 6152 | tf_op jit(solution)/shard_map/ppermute | solution.py:22
  158.1 9.4 %collective-permute-start.30 = (f32[32,16,1]{2,1,0:T(8,128)S(1)}, f32[32,16,1]{2,1,0:T(8,128)S(1)}, u32[]{:S(2)}, u32[]{:S(2)}) collective-permute-start(f32[32,16,1]{2,1,0:T(8,128)S(1)} %get-tuple-element.92), channel_id=1, source_target_pairs={{0,64},{64,128},{128,192},{192,256},{256,320},{320,384},{384,448},... | collective-permute-start | bytes 6152 | tf_op jit(solution)/shard_map/ppermute | solution.py:21
  167.8 8.9 %collective-permute-start.33 = (f32[32,1,130]{2,1,0:T(1,128)S(1)}, f32[32,1,130]{2,1,0:T(1,128)S(1)}, u32[]{:S(2)}, u32[]{:S(2)}) collective-permute-start(f32[32,1,130]{2,1,0:T(1,128)S(1)} %get-tuple-element.63), channel_id=1, source_target_pairs={{4,0},{8,4},{12,8},{16,12},{20,16},{24,20},{28,24},{32,28},{36,32}... | collective-permute-start | bytes 49928 | tf_op jit(solution)/shard_map/ppermute | solution.py:22
  169.1 8.6 %collective-permute-start.32 = (f32[32,1,130]{2,1,0:T(1,128)S(1)}, f32[32,1,130]{2,1,0:T(1,128)S(1)}, u32[]{:S(2)}, u32[]{:S(2)}) collective-permute-start(f32[32,1,130]{2,1,0:T(1,128)S(1)} %get-tuple-element.64), channel_id=1, source_target_pairs={{0,4},{4,8},{8,12},{12,16},{16,20},{20,24},{24,28},{28,32},{32,36}... | collective-permute-start | bytes 49928 | tf_op jit(solution)/shard_map/ppermute | solution.py:21
  177.7 9.8 %collective-permute-start.34 = (f32[1,18,130]{2,1,0:T(8,128)S(1)}, f32[1,18,130]{2,1,0:T(8,128)S(1)}, u32[]{:S(2)}, u32[]{:S(2)}) collective-permute-start(f32[1,18,130]{2,1,0:T(8,128)S(1)} %get-tuple-element.35), channel_id=1, source_target_pairs={{1,0},{2,1},{3,2},{5,4},{6,5},{7,6},{9,8},{10,9},{11,10},{13,12},{... | collective-permute-start | bytes 28088 | tf_op jit(solution)/shard_map/ppermute | solution.py:22
  179.0 9.5 %collective-permute-start.35 = (f32[1,18,130]{2,1,0:T(8,128)S(1)}, f32[1,18,130]{2,1,0:T(8,128)S(1)}, u32[]{:S(2)}, u32[]{:S(2)}) collective-permute-start(f32[1,18,130]{2,1,0:T(8,128)S(1)} %get-tuple-element.36), channel_id=1, source_target_pairs={{0,1},{1,2},{2,3},{4,5},{5,6},{6,7},{8,9},{9,10},{10,11},{12,13},{... | collective-permute-start | bytes 28088 | tf_op jit(solution)/shard_map/ppermute | solution.py:21
  189.4 10.1 %collective-permute-start.37 = (f32[32,16,1]{2,1,0:T(8,128)S(1)}, f32[32,16,1]{2,1,0:T(8,128)S(1)}, u32[]{:S(2)}, u32[]{:S(2)}) collective-permute-start(f32[32,16,1]{2,1,0:T(8,128)S(1)} %get-tuple-element.89), channel_id=1, source_target_pairs={{64,0},{128,64},{192,128},{256,192},{320,256},{384,320},{448,384},... | collective-permute-start | bytes 6152 | tf_op jit(solution)/shard_map/ppermute | solution.py:22
  191.3 9.4 %collective-permute-start.36 = (f32[32,16,1]{2,1,0:T(8,128)S(1)}, f32[32,16,1]{2,1,0:T(8,128)S(1)}, u32[]{:S(2)}, u32[]{:S(2)}) collective-permute-start(f32[32,16,1]{2,1,0:T(8,128)S(1)} %get-tuple-element.90), channel_id=1, source_target_pairs={{0,64},{64,128},{128,192},{192,256},{256,320},{320,384},{384,448},... | collective-permute-start | bytes 6152 | tf_op jit(solution)/shard_map/ppermute | solution.py:21
  201.0 8.6 %collective-permute-start.39 = (f32[32,1,130]{2,1,0:T(1,128)S(1)}, f32[32,1,130]{2,1,0:T(1,128)S(1)}, u32[]{:S(2)}, u32[]{:S(2)}) collective-permute-start(f32[32,1,130]{2,1,0:T(1,128)S(1)} %get-tuple-element.61), channel_id=1, source_target_pairs={{4,0},{8,4},{12,8},{16,12},{20,16},{24,20},{28,24},{32,28},{36,32}... | collective-permute-start | bytes 49928 | tf_op jit(solution)/shard_map/ppermute | solution.py:22
  202.3 8.3 %collective-permute-start.38 = (f32[32,1,130]{2,1,0:T(1,128)S(1)}, f32[32,1,130]{2,1,0:T(1,128)S(1)}, u32[]{:S(2)}, u32[]{:S(2)}) collective-permute-start(f32[32,1,130]{2,1,0:T(1,128)S(1)} %get-tuple-element.62), channel_id=1, source_target_pairs={{0,4},{4,8},{8,12},{12,16},{16,20},{20,24},{24,28},{28,32},{32,36}... | collective-permute-start | bytes 49928 | tf_op jit(solution)/shard_map/ppermute | solution.py:21
  210.7 9.8 %collective-permute-start.40 = (f32[1,18,130]{2,1,0:T(8,128)S(1)}, f32[1,18,130]{2,1,0:T(8,128)S(1)}, u32[]{:S(2)}, u32[]{:S(2)}) collective-permute-start(f32[1,18,130]{2,1,0:T(8,128)S(1)} %get-tuple-element.33), channel_id=1, source_target_pairs={{1,0},{2,1},{3,2},{5,4},{6,5},{7,6},{9,8},{10,9},{11,10},{13,12},{... | collective-permute-start | bytes 28088 | tf_op jit(solution)/shard_map/ppermute | solution.py:22
  212.0 9.4 %collective-permute-start.41 = (f32[1,18,130]{2,1,0:T(8,128)S(1)}, f32[1,18,130]{2,1,0:T(8,128)S(1)}, u32[]{:S(2)}, u32[]{:S(2)}) collective-permute-start(f32[1,18,130]{2,1,0:T(8,128)S(1)} %get-tuple-element.34), channel_id=1, source_target_pairs={{0,1},{1,2},{2,3},{4,5},{5,6},{6,7},{8,9},{9,10},{10,11},{12,13},{... | collective-permute-start | bytes 28088 | tf_op jit(solution)/shard_map/ppermute | solution.py:21
  222.2 10.1 %collective-permute-start.43 = (f32[32,16,1]{2,1,0:T(8,128)S(1)}, f32[32,16,1]{2,1,0:T(8,128)S(1)}, u32[]{:S(2)}, u32[]{:S(2)}) collective-permute-start(f32[32,16,1]{2,1,0:T(8,128)S(1)} %get-tuple-element.87), channel_id=1, source_target_pairs={{64,0},{128,64},{192,128},{256,192},{320,256},{384,320},{448,384},... | collective-permute-start | bytes 6152 | tf_op jit(solution)/shard_map/ppermute | solution.py:22
  224.2 9.4 %collective-permute-start.42 = (f32[32,16,1]{2,1,0:T(8,128)S(1)}, f32[32,16,1]{2,1,0:T(8,128)S(1)}, u32[]{:S(2)}, u32[]{:S(2)}) collective-permute-start(f32[32,16,1]{2,1,0:T(8,128)S(1)} %get-tuple-element.88), channel_id=1, source_target_pairs={{0,64},{64,128},{128,192},{192,256},{256,320},{320,384},{384,448},... | collective-permute-start | bytes 6152 | tf_op jit(solution)/shard_map/ppermute | solution.py:21
  233.8 8.6 %collective-permute-start.45 = (f32[32,1,130]{2,1,0:T(1,128)S(1)}, f32[32,1,130]{2,1,0:T(1,128)S(1)}, u32[]{:S(2)}, u32[]{:S(2)}) collective-permute-start(f32[32,1,130]{2,1,0:T(1,128)S(1)} %get-tuple-element.59), channel_id=1, source_target_pairs={{4,0},{8,4},{12,8},{16,12},{20,16},{24,20},{28,24},{32,28},{36,32}... | collective-permute-start | bytes 49928 | tf_op jit(solution)/shard_map/ppermute | solution.py:22
  235.1 8.3 %collective-permute-start.44 = (f32[32,1,130]{2,1,0:T(1,128)S(1)}, f32[32,1,130]{2,1,0:T(1,128)S(1)}, u32[]{:S(2)}, u32[]{:S(2)}) collective-permute-start(f32[32,1,130]{2,1,0:T(1,128)S(1)} %get-tuple-element.60), channel_id=1, source_target_pairs={{0,4},{4,8},{8,12},{12,16},{16,20},{20,24},{24,28},{28,32},{32,36}... | collective-permute-start | bytes 49928 | tf_op jit(solution)/shard_map/ppermute | solution.py:21
  243.5 10.0 %collective-permute-start.46 = (f32[1,18,130]{2,1,0:T(8,128)S(1)}, f32[1,18,130]{2,1,0:T(8,128)S(1)}, u32[]{:S(2)}, u32[]{:S(2)}) collective-permute-start(f32[1,18,130]{2,1,0:T(8,128)S(1)} %get-tuple-element.31), channel_id=1, source_target_pairs={{1,0},{2,1},{3,2},{5,4},{6,5},{7,6},{9,8},{10,9},{11,10},{13,12},{... | collective-permute-start | bytes 28088 | tf_op jit(solution)/shard_map/ppermute | solution.py:22
  244.8 9.4 %collective-permute-start.47 = (f32[1,18,130]{2,1,0:T(8,128)S(1)}, f32[1,18,130]{2,1,0:T(8,128)S(1)}, u32[]{:S(2)}, u32[]{:S(2)}) collective-permute-start(f32[1,18,130]{2,1,0:T(8,128)S(1)} %get-tuple-element.32), channel_id=1, source_target_pairs={{0,1},{1,2},{2,3},{4,5},{5,6},{6,7},{8,9},{9,10},{10,11},{12,13},{... | collective-permute-start | bytes 28088 | tf_op jit(solution)/shard_map/ppermute | solution.py:21
  382.2 7.7 collective-permute-start.49
  385.1 6.0 collective-permute-start.48
  397.9 9.2 %collective-permute-start.52 = (f32[1,18,130]{2,1,0:T(8,128)S(1)}, f32[1,18,130]{2,1,0:T(8,128)S(1)}, u32[]{:S(2)}, u32[]{:S(2)}) collective-permute-start(f32[1,18,130]{2,1,0:T(8,128)S(1)} %get-tuple-element.29), channel_id=1, source_target_pairs={{1,0},{2,1},{3,2},{5,4},{6,5},{7,6},{9,8},{10,9},{11,10},{13,12},{... | collective-permute-start | bytes 28088 | tf_op jit(solution)/shard_map/ppermute | solution.py:22
  399.2 8.8 %collective-permute-start.53 = (f32[1,18,130]{2,1,0:T(8,128)S(1)}, f32[1,18,130]{2,1,0:T(8,128)S(1)}, u32[]{:S(2)}, u32[]{:S(2)}) collective-permute-start(f32[1,18,130]{2,1,0:T(8,128)S(1)} %get-tuple-element.30), channel_id=1, source_target_pairs={{0,1},{1,2},{2,3},{4,5},{5,6},{6,7},{8,9},{9,10},{10,11},{12,13},{... | collective-permute-start | bytes 28088 | tf_op jit(solution)/shard_map/ppermute | solution.py:21
  408.9 10.5 %collective-permute-start.55 = (f32[32,16,1]{2,1,0:T(8,128)S(1)}, f32[32,16,1]{2,1,0:T(8,128)S(1)}, u32[]{:S(2)}, u32[]{:S(2)}) collective-permute-start(f32[32,16,1]{2,1,0:T(8,128)S(1)} %get-tuple-element.83), channel_id=1, source_target_pairs={{64,0},{128,64},{192,128},{256,192},{320,256},{384,320},{448,384},... | collective-permute-start | bytes 6152 | tf_op jit(solution)/shard_map/ppermute | solution.py:22
  410.8 9.7 %collective-permute-start.54 = (f32[32,16,1]{2,1,0:T(8,128)S(1)}, f32[32,16,1]{2,1,0:T(8,128)S(1)}, u32[]{:S(2)}, u32[]{:S(2)}) collective-permute-start(f32[32,16,1]{2,1,0:T(8,128)S(1)} %get-tuple-element.84), channel_id=1, source_target_pairs={{0,64},{64,128},{128,192},{192,256},{256,320},{320,384},{384,448},... | collective-permute-start | bytes 6152 | tf_op jit(solution)/shard_map/ppermute | solution.py:21
  427.8 9.8 %collective-permute-start.58 = (f32[1,18,130]{2,1,0:T(8,128)S(1)}, f32[1,18,130]{2,1,0:T(8,128)S(1)}, u32[]{:S(2)}, u32[]{:S(2)}) collective-permute-start(f32[1,18,130]{2,1,0:T(8,128)S(1)} %get-tuple-element.27), channel_id=1, source_target_pairs={{1,0},{2,1},{3,2},{5,4},{6,5},{7,6},{9,8},{10,9},{11,10},{13,12},{... | collective-permute-start | bytes 28088 | tf_op jit(solution)/shard_map/ppermute | solution.py:22
  429.1 9.4 %collective-permute-start.59 = (f32[1,18,130]{2,1,0:T(8,128)S(1)}, f32[1,18,130]{2,1,0:T(8,128)S(1)}, u32[]{:S(2)}, u32[]{:S(2)}) collective-permute-start(f32[1,18,130]{2,1,0:T(8,128)S(1)} %get-tuple-element.28), channel_id=1, source_target_pairs={{0,1},{1,2},{2,3},{4,5},{5,6},{6,7},{8,9},{9,10},{10,11},{12,13},{... | collective-permute-start | bytes 28088 | tf_op jit(solution)/shard_map/ppermute | solution.py:21
  439.3 10.1 %collective-permute-start.61 = (f32[32,16,1]{2,1,0:T(8,128)S(1)}, f32[32,16,1]{2,1,0:T(8,128)S(1)}, u32[]{:S(2)}, u32[]{:S(2)}) collective-permute-start(f32[32,16,1]{2,1,0:T(8,128)S(1)} %get-tuple-element.81), channel_id=1, source_target_pairs={{64,0},{128,64},{192,128},{256,192},{320,256},{384,320},{448,384},... | collective-permute-start | bytes 6152 | tf_op jit(solution)/shard_map/ppermute | solution.py:22
  441.3 9.4 %collective-permute-start.60 = (f32[32,16,1]{2,1,0:T(8,128)S(1)}, f32[32,16,1]{2,1,0:T(8,128)S(1)}, u32[]{:S(2)}, u32[]{:S(2)}) collective-permute-start(f32[32,16,1]{2,1,0:T(8,128)S(1)} %get-tuple-element.82), channel_id=1, source_target_pairs={{0,64},{64,128},{128,192},{192,256},{256,320},{320,384},{384,448},... | collective-permute-start | bytes 6152 | tf_op jit(solution)/shard_map/ppermute | solution.py:21
  457.9 9.8 %collective-permute-start.64 = (f32[1,18,130]{2,1,0:T(8,128)S(1)}, f32[1,18,130]{2,1,0:T(8,128)S(1)}, u32[]{:S(2)}, u32[]{:S(2)}) collective-permute-start(f32[1,18,130]{2,1,0:T(8,128)S(1)} %get-tuple-element.25), channel_id=1, source_target_pairs={{1,0},{2,1},{3,2},{5,4},{6,5},{7,6},{9,8},{10,9},{11,10},{13,12},{... | collective-permute-start | bytes 28088 | tf_op jit(solution)/shard_map/ppermute | solution.py:22
  459.2 9.4 %collective-permute-start.65 = (f32[1,18,130]{2,1,0:T(8,128)S(1)}, f32[1,18,130]{2,1,0:T(8,128)S(1)}, u32[]{:S(2)}, u32[]{:S(2)}) collective-permute-start(f32[1,18,130]{2,1,0:T(8,128)S(1)} %get-tuple-element.26), channel_id=1, source_target_pairs={{0,1},{1,2},{2,3},{4,5},{5,6},{6,7},{8,9},{9,10},{10,11},{12,13},{... | collective-permute-start | bytes 28088 | tf_op jit(solution)/shard_map/ppermute | solution.py:21
  469.5 10.1 %collective-permute-start.67 = (f32[32,16,1]{2,1,0:T(8,128)S(1)}, f32[32,16,1]{2,1,0:T(8,128)S(1)}, u32[]{:S(2)}, u32[]{:S(2)}) collective-permute-start(f32[32,16,1]{2,1,0:T(8,128)S(1)} %get-tuple-element.79), channel_id=1, source_target_pairs={{64,0},{128,64},{192,128},{256,192},{320,256},{384,320},{448,384},... | collective-permute-start | bytes 6152 | tf_op jit(solution)/shard_map/ppermute | solution.py:22
  471.4 9.4 %collective-permute-start.66 = (f32[32,16,1]{2,1,0:T(8,128)S(1)}, f32[32,16,1]{2,1,0:T(8,128)S(1)}, u32[]{:S(2)}, u32[]{:S(2)}) collective-permute-start(f32[32,16,1]{2,1,0:T(8,128)S(1)} %get-tuple-element.80), channel_id=1, source_target_pairs={{0,64},{64,128},{128,192},{192,256},{256,320},{320,384},{384,448},... | collective-permute-start | bytes 6152 | tf_op jit(solution)/shard_map/ppermute | solution.py:21
  488.0 9.9 %collective-permute-start.70 = (f32[1,18,130]{2,1,0:T(8,128)S(1)}, f32[1,18,130]{2,1,0:T(8,128)S(1)}, u32[]{:S(2)}, u32[]{:S(2)}) collective-permute-start(f32[1,18,130]{2,1,0:T(8,128)S(1)} %get-tuple-element.23), channel_id=1, source_target_pairs={{1,0},{2,1},{3,2},{5,4},{6,5},{7,6},{9,8},{10,9},{11,10},{13,12},{... | collective-permute-start | bytes 28088 | tf_op jit(solution)/shard_map/ppermute | solution.py:22
  489.3 9.5 %collective-permute-start.71 = (f32[1,18,130]{2,1,0:T(8,128)S(1)}, f32[1,18,130]{2,1,0:T(8,128)S(1)}, u32[]{:S(2)}, u32[]{:S(2)}) collective-permute-start(f32[1,18,130]{2,1,0:T(8,128)S(1)} %get-tuple-element.24), channel_id=1, source_target_pairs={{0,1},{1,2},{2,3},{4,5},{5,6},{6,7},{8,9},{9,10},{10,11},{12,13},{... | collective-permute-start | bytes 28088 | tf_op jit(solution)/shard_map/ppermute | solution.py:21
  623.8 7.7 collective-permute-start.73
  626.4 6.3 collective-permute-start.72
  639.3 9.2 %collective-permute-start.76 = (f32[1,18,130]{2,1,0:T(8,128)S(1)}, f32[1,18,130]{2,1,0:T(8,128)S(1)}, u32[]{:S(2)}, u32[]{:S(2)}) collective-permute-start(f32[1,18,130]{2,1,0:T(8,128)S(1)} %get-tuple-element.21), channel_id=1, source_target_pairs={{1,0},{2,1},{3,2},{5,4},{6,5},{7,6},{9,8},{10,9},{11,10},{13,12},{... | collective-permute-start | bytes 28088 | tf_op jit(solution)/shard_map/ppermute | solution.py:22
  640.6 8.8 %collective-permute-start.77 = (f32[1,18,130]{2,1,0:T(8,128)S(1)}, f32[1,18,130]{2,1,0:T(8,128)S(1)}, u32[]{:S(2)}, u32[]{:S(2)}) collective-permute-start(f32[1,18,130]{2,1,0:T(8,128)S(1)} %get-tuple-element.22), channel_id=1, source_target_pairs={{0,1},{1,2},{2,3},{4,5},{5,6},{6,7},{8,9},{9,10},{10,11},{12,13},{... | collective-permute-start | bytes 28088 | tf_op jit(solution)/shard_map/ppermute | solution.py:21
  650.3 11.0 %collective-permute-start.79 = (f32[32,16,1]{2,1,0:T(8,128)S(1)}, f32[32,16,1]{2,1,0:T(8,128)S(1)}, u32[]{:S(2)}, u32[]{:S(2)}) collective-permute-start(f32[32,16,1]{2,1,0:T(8,128)S(1)} %get-tuple-element.75), channel_id=1, source_target_pairs={{64,0},{128,64},{192,128},{256,192},{320,256},{384,320},{448,384},... | collective-permute-start | bytes 6152 | tf_op jit(solution)/shard_map/ppermute | solution.py:22
  652.2 10.0 %collective-permute-start.78 = (f32[32,16,1]{2,1,0:T(8,128)S(1)}, f32[32,16,1]{2,1,0:T(8,128)S(1)}, u32[]{:S(2)}, u32[]{:S(2)}) collective-permute-start(f32[32,16,1]{2,1,0:T(8,128)S(1)} %get-tuple-element.76), channel_id=1, source_target_pairs={{0,64},{64,128},{128,192},{192,256},{256,320},{320,384},{384,448},... | collective-permute-start | bytes 6152 | tf_op jit(solution)/shard_map/ppermute | solution.py:21
  669.4 9.9 %collective-permute-start.82 = (f32[1,18,130]{2,1,0:T(8,128)S(1)}, f32[1,18,130]{2,1,0:T(8,128)S(1)}, u32[]{:S(2)}, u32[]{:S(2)}) collective-permute-start(f32[1,18,130]{2,1,0:T(8,128)S(1)} %get-tuple-element.19), channel_id=1, source_target_pairs={{1,0},{2,1},{3,2},{5,4},{6,5},{7,6},{9,8},{10,9},{11,10},{13,12},{... | collective-permute-start | bytes 28088 | tf_op jit(solution)/shard_map/ppermute | solution.py:22
  670.7 9.5 %collective-permute-start.83 = (f32[1,18,130]{2,1,0:T(8,128)S(1)}, f32[1,18,130]{2,1,0:T(8,128)S(1)}, u32[]{:S(2)}, u32[]{:S(2)}) collective-permute-start(f32[1,18,130]{2,1,0:T(8,128)S(1)} %get-tuple-element.20), channel_id=1, source_target_pairs={{0,1},{1,2},{2,3},{4,5},{5,6},{6,7},{8,9},{9,10},{10,11},{12,13},{... | collective-permute-start | bytes 28088 | tf_op jit(solution)/shard_map/ppermute | solution.py:21
  (23 other events, 158.5 us)
where the time goes:
time: 800 us; the launch traced here: 797 us
  blocking collectives  361 us (45%)
  starting transfers between devices  337 us (42%)
  waiting for transfers between devices  72.8 us (9%)
  other arithmetic  17.4 us (2%)
    psum x3, blocking collectives, global_dot(): return lax.psum(jnp.sum(first_field * second_field), ('gx', 'gy', 'gz'))  361 us
    ppermute x42, starting transfers between devices, padded_2(): before = lax.ppermute(last, axis, up)  265 us
    ppermute x42, starting transfers between devices, padded_2(): after = lax.ppermute(first, axis, down)  72.1 us
    ppermute x42, waiting for transfers between devices, padded_2(): before = lax.ppermute(last, axis, up)  44.9 us
    ppermute x42, waiting for transfers between devices, padded_2(): after = lax.ppermute(first, axis, down)  27.8 us
  transfers between devices with their start and end apart: 84, of which 55 were waited for; matrix products, arithmetic and copies ran while one was open for 0% of the time, Pallas kernels for 0%

commit v1 on v0

v1 whole, which is shorter than its diff:
```python
import jax
import jax.numpy as jnp
from jax import lax
from jax.experimental import pallas as pl
from jax.experimental.pallas import tpu as pltpu
from jax.sharding import PartitionSpec as P

SWEEPS = 3
HIGH = 7.2
LOW = 0.072

NZ, NY, NX = 32, 16, 128
G = 8
FZ, FY = NZ + 2 * G, NY + 2 * G
DEPTHS = (6, 4, 7)
OFFS = (0, 6, 10)
LAYERS = 17
PIECES = [(f, k) for f in range(3) for k in range(DEPTHS[f])]
MAIN_ROWS = LAYERS * NZ
PACK_ROWS = MAIN_ROWS + LAYERS * 16
Q_PACK = FZ // 16 * FY


def chebyshev():
    centre = (HIGH + LOW) / 2.0
    half = (HIGH - LOW) / 2.0
    sigma = centre / half
    rho = 1.0 / sigma
    d = [1.0 / centre, 0.0, 0.0]
    z = list(d)
    for _ in range(SWEEPS - 1):
        rho_new = 1.0 / (2.0 * sigma - rho)
        defect = [1.0, -z[0], -z[1]]
        d = [rho_new * rho * a + 2.0 * rho_new / half * b for a, b in zip(d, defect)]
        z = [a + b for a, b in zip(z, d)]
        rho = rho_new
    return z


C0, C1, C2 = chebyshev()
SQ = 36.0

f32 = jnp.float32
VM = pl.BlockSpec(memory_space=pltpu.VMEM)


def run(kernel, outs, args, scratch=(), name=None):
    return pl.pallas_call(
        kernel,
        out_shape=[jax.ShapeDtypeStruct(s, f32) for s in outs],
        in_specs=[VM] * len(args),
        out_specs=[VM] * len(outs),
        scratch_shapes=list(scratch),
        name=name,
    )(*args)


def shift(x, axis, step):
    n = lax.axis_size(axis)
    pairs = [(i, i + step) for i in range(n) if 0 <= i + step < n]
    return lax.ppermute(x, axis, pairs)


def exchange(down, up, axis):
    from_above = shift(down, axis, -1)
    from_below = shift(up, axis, 1)
    return from_below, from_above


def pack_y(x_ref, b_ref, k_ref, lo_ref, hi_ref, dn_ref, up_ref):
    fields = (x_ref, b_ref, k_ref)
    for i, (f, k) in enumerate(PIECES):
        d = DEPTHS[f]
        for out, row in ((dn_ref, k), (up_ref, NY - d + k)):
            out[i * NZ : (i + 1) * NZ, :] = fields[f][pl.ds(row, NZ, stride=NY), :]
            at = MAIN_ROWS + i * 16
            first = OFFS[f] * NY + row
            out[at : at + d, :] = lo_ref[pl.ds(first, d, stride=NY), :]
            out[at + 8 : at + 8 + d, :] = hi_ref[pl.ds(first, d, stride=NY), :]


def pack_lanes(read, dn_ref, up_ref, base):
    group = lax.broadcasted_iota(jnp.int32, (FY, NX), 1) // G
    for q in range(FZ // 16):
        dn = jnp.zeros((FY, NX), f32)
        up = jnp.zeros((FY, NX), f32)
        for g in range(16):
            v = read(16 * q + g)
            a = v if g == 0 else pltpu.roll(v, G * g, 1)
            b = v if g == 15 else pltpu.roll(v, G * (g + 1), 1)
            dn = jnp.where(group == g, a, dn)
            up = jnp.where(group == g, b, up)
        dn_ref[base + q * FY : base + (q + 1) * FY, :] = dn
        up_ref[base + q * FY : base + (q + 1) * FY, :] = up


def unpack_lanes(lo_ref, hi_ref, base, write):
    right = lax.broadcasted_iota(jnp.int32, (FY, NX), 1) < NX // 2
    for q in range(FZ // 16):
        lo = lo_ref[base + q * FY : base + (q + 1) * FY, :]
        hi = hi_ref[base + q * FY : base + (q + 1) * FY, :]
        for g in range(16):
            a = hi if g == 0 else pltpu.roll(hi, NX - G * g, 1)
            b = lo if g == 15 else pltpu.roll(lo, NX - G - G * g, 1)
            write(16 * q + g, jnp.where(right, a, b))


def frame(x_ref, b_ref, k_ref, zlo, zhi, ylo, yhi, xe, be, ke, dn_ref, up_ref):
    fields = (x_ref, b_ref, k_ref)
    for f, out in enumerate((xe, be, ke)):
        d = DEPTHS[f]
        out[...] = jnp.zeros((FZ * FY, NX), f32)
        for z in range(NZ):
            at = (G + z) * FY + G
            out[at : at + NY, :] = fields[f][z * NY : (z + 1) * NY, :]
        for j in range(d):
            src = (OFFS[f] + j) * NY
            at = (G - d + j) * FY + G
            out[at : at + NY, :] = zlo[src : src + NY, :]
            at = (G + NZ + j) * FY + G
            out[at : at + NY, :] = zhi[src : src + NY, :]
        for k in range(d):
            i = OFFS[f] + k
            h = MAIN_ROWS + i * 16
            for src, row in ((ylo, G - d + k), (yhi, G + NY + k)):
                out[pl.ds(G * FY + row, NZ, stride=FY), :] = src[i * NZ : (i + 1) * NZ, :]
                out[pl.ds((G - d) * FY + row, d, stride=FY), :] = src[h : h + d, :]
                out[pl.ds((G + NZ) * FY + row, d, stride=FY), :] = src[h + 8 : h + 8 + d, :]
        pack_lanes(lambda z: out[z * FY : (z + 1) * FY, :], dn_ref, up_ref, f * Q_PACK)


def apply_k(src, dst, coef, mask, first, last, finish=None):
    lane = lax.broadcasted_iota(jnp.int32, (FY, NX), 1)
    s0, s1 = src
    c0, c1 = coef
    m0, m1 = mask

    def plane(z, _):
        v0, v1 = s0[z], s1[z]
        a0, a1 = pltpu.roll(v0, 1, 1), pltpu.roll(v1, 1, 1)
        b0, b1 = pltpu.roll(v0, NX - 1, 1), pltpu.roll(v1, NX - 1, 1)
        t0 = jnp.where(lane == 0, a1, a0) + jnp.where(lane == NX - 1, b1, b0)
        t1 = jnp.where(lane == 0, a0, a1) + jnp.where(lane == NX - 1, b0, b1)
        t0 = t0 + pltpu.roll(v0, 1, 0) + pltpu.roll(v0, FY - 1, 0) + s0[z - 1] + s0[z + 1]
        t1 = t1 + pltpu.roll(v1, 1, 0) + pltpu.roll(v1, FY - 1, 0) + s1[z - 1] + s1[z + 1]
        r0 = c0[z] * v0 - m0[z] * t0
        r1 = c1[z] * v1 - m1[z] * t1
        if finish is None:
            dst[0][z] = r0
            dst[1][z] = r1
        else:
            finish(z, r0, r1)
        return 0

    lax.fori_loop(first, last, plane, 0)


def span(radius):
    return G - radius, G + NZ + radius


def first_stage(xe, be, ke, lo, hi, r_out, w_out, wdn, wup, c0, c1, m0, m1, x1, b1, p0, p1, q0, q1):
    def put(ref):
        def write(z, v):
            ref[z] = v

        return write

    def put_coef(z, k1):
        k0 = ke[z]
        c0[z] = 6.0 + k0
        c1[z] = 6.0 + k1
        m0[z] = jnp.where(k0 > 0.0, 1.0, 0.0)
        m1[z] = jnp.where(k1 > 0.0, 1.0, 0.0)

    unpack_lanes(lo, hi, 0, put(x1))
    unpack_lanes(lo, hi, Q_PACK, put(b1))
    unpack_lanes(lo, hi, 2 * Q_PACK, put_coef)
    coef, mask, p, q, b = (c0, c1), (m0, m1), (p0, p1), (q0, q1), (be, b1)

    apply_k((xe, x1), p, coef, mask, *span(5))

    def to_residual(z, v0, v1):
        be[z] = be[z] - v0 * (1.0 / SQ)
        b1[z] = b1[z] - v1 * (1.0 / SQ)

    apply_k(p, None, coef, mask, *span(4), finish=to_residual)
    apply_k(b, p, coef, mask, *span(3))
    apply_k(p, q, coef, mask, *span(2))
    apply_k(q, p, coef, mask, *span(1))

    def to_precond(z, v0, v1):
        w = C0 * be[z] + (C1 / SQ) * q0[z] + (C2 / SQ**2) * v0
        w_out[z - G] = w[G : G + NY, :]
        r_out[z - G] = be[z][G : G + NY, :]

    apply_k(p, None, coef, mask, *span(0), finish=to_precond)
    wdn[...] = w_out[0:G]
    wup[...] = w_out[NZ - G : NZ]


def pack_y2(w_ref, lo_ref, hi_ref, dn_ref, up_ref):
    dn_ref[0:G] = lo_ref[:, 0:G, :]
    up_ref[0:G] = lo_ref[:, NY - G : NY, :]
    dn_ref[G : G + NZ] = w_ref[:, 0:G, :]
    up_ref[G : G + NZ] = w_ref[:, NY - G : NY, :]
    dn_ref[G + NZ : FZ] = hi_ref[:, 0:G, :]
    up_ref[G + NZ : FZ] = hi_ref[:, NY - G : NY, :]


def frame2(w_ref, zlo, zhi, ylo, yhi, we, dn_ref, up_ref):
    we[0:G, G : G + NY, :] = zlo[...]
    we[G : G + NZ, G : G + NY, :] = w_ref[...]
    we[G + NZ : FZ, G : G + NY, :] = zhi[...]
    we[:, 0:G, :] = ylo[...]
    we[:, G + NY : FY, :] = yhi[...]
    pack_lanes(lambda z: we[z], dn_ref, up_ref, 0)


def second_stage(we, lo, hi, r_ref, c0, c1, m0, m1, v1_out, v2_out, v3_out, dots, w1, p0, p1, q0, q1, s0, s1):
    def write(z, v):
        w1[z] = v

    unpack_lanes(lo, hi, 0, write)
    coef, mask, p, q, s = (c0, c1), (m0, m1), (p0, p1), (q0, q1), (s0, s1)
    apply_k((we, w1), p, coef, mask, *span(7))
    apply_k(p, q, coef, mask, *span(6))
    apply_k(q, p, coef, mask, *span(5))
    apply_k(p, s, coef, mask, *span(4))
    apply_k(s, p, coef, mask, *span(3))

    def to_w2(z, a0, a1):
        s0[z] = C0 * q0[z] + (C1 / SQ) * s0[z] + (C2 / SQ**2) * a0
        s1[z] = C0 * q1[z] + (C1 / SQ) * s1[z] + (C2 / SQ**2) * a1

    apply_k(p, None, coef, mask, *span(2), finish=to_w2)
    apply_k(s, p, coef, mask, *span(1))
    dots[...] = jnp.zeros((32, NX), f32)

    def to_w3(z, a0, a1):
        rows = slice(G, G + NY)
        w = we[z][rows]
        u1 = q0[z][rows]
        u2 = s0[z][rows]
        u3 = a0[rows]
        v1_out[z - G] = u1
        v2_out[z - G] = u2
        v3_out[z - G] = u3
        for i, t in enumerate((r_ref[z - G] * w, w * u1, u1 * u2, u2 * u3)):
            dots[8 * i : 8 * i + 8, :] += t[0:8] + t[8:16]

    apply_k(p, None, coef, mask, *span(0), finish=to_w3)


def finish(x_ref, r_ref, w_ref, v1, v2, v3, dots, x_out, r_out):
    def total(i, scale):
        return jnp.sum(dots[8 * i : 8 * i + 8, :], keepdims=True) * (1.0 / scale)

    e0 = total(0, 1.0)
    g0 = total(1, SQ)
    h = total(2, SQ**2)
    k = total(3, SQ**3)
    a0 = e0 / g0
    e1 = a0 * a0 * h - e0
    beta = 1.0 + e1 / e0
    a1 = e1 / (beta * beta * g0 - 2.0 * beta * a0 * h + a0 * a0 * k)
    near = a0 + a1 * beta
    far = a1 * a0
    x_out[...] = x_ref[...] + near[None] * w_ref[...] - (far * (1.0 / SQ))[None] * v2[...]
    r_out[...] = r_ref[...] - (near * (1.0 / SQ))[None] * v1[...] + (far * (1.0 / SQ**2))[None] * v3[...]


def all_sum(x):
    for axis in ("gx", "gy"):
        n = lax.axis_size(axis)
        copies = jnp.broadcast_to(x[None], (n, *x.shape))
        x = jnp.sum(lax.all_to_all(copies, axis, 0, 0), axis=0)
    return lax.psum(x, "gz")


def body(right_side, initial, kappa_sq):
    fields = (initial, right_side, kappa_sq)
    flat = [v.reshape(NZ * NY, NX) for v in fields]
    down = jnp.concatenate([v[:d] for v, d in zip(fields, DEPTHS)], axis=0)
    up = jnp.concatenate([v[NZ - d :] for v, d in zip(fields, DEPTHS)], axis=0)
    zlo, zhi = exchange(down, up, "gz")
    zlo, zhi = zlo.reshape(LAYERS * NY, NX), zhi.reshape(LAYERS * NY, NX)
    down, up = run(pack_y, [(PACK_ROWS, NX)] * 2, (*flat, zlo, zhi), name="pack_y")
    ylo, yhi = exchange(down, up, "gy")
    frame_shape = (FZ, FY, NX)
    xe, be, ke, down, up = run(
        frame, [(FZ * FY, NX)] * 3 + [(3 * Q_PACK, NX)] * 2, (*flat, zlo, zhi, ylo, yhi), name="frame"
    )
    xlo, xhi = exchange(down, up, "gx")
    xe, be, ke = (v.reshape(frame_shape) for v in (xe, be, ke))
    tile = pltpu.VMEM(frame_shape, f32)
    block = (NZ, NY, NX)
    slab = (G, NY, NX)

    def stage1(xe, be_in, *rest):
        be = rest[-1]
        be[...] = be_in[...]
        first_stage(xe, be, *rest[:-1])

    r0, w0, down, up, c0, c1, m0, m1 = run(
        stage1,
        [block, block, slab, slab, frame_shape, frame_shape, frame_shape, frame_shape],
        (xe, be, ke, xlo, xhi),
        scratch=[tile] * 7,
        name="first_stage",
    )
    zlo, zhi = exchange(down, up, "gz")
    down, up = run(pack_y2, [(FZ, G, NX)] * 2, (w0, zlo, zhi), name="pack_y2")
    ylo, yhi = exchange(down, up, "gy")
    we, down, up = run(frame2, [frame_shape, (Q_PACK, NX), (Q_PACK, NX)], (w0, zlo, zhi, ylo, yhi), name="frame2")
    xlo, xhi = exchange(down, up, "gx")
    v1, v2, v3, dots = run(
        second_stage,
        [block, block, block, (32, NX)],
        (we, xlo, xhi, r0, c0, c1, m0, m1),
        scratch=[tile] * 7,
        name="second_stage",
    )
    dots = all_sum(dots)
    x, r = run(finish, [block, block], (initial, r0, w0, v1, v2, v3, dots), name="finish")
    return x, r


def solution(mesh):
    spec = P("gz", "gy", "gx")
    return jax.shard_map(body, mesh=mesh, in_specs=(spec,) * 3, out_specs=(spec,) * 2, check_vma=False)
```

time: 800 us -> 234 us (0.29)
  blocking collectives: 361 us -> 42.9 us
  starting transfers between devices: 337 us -> 39.8 us
  Pallas kernels: 0 us -> 70.6 us
  other arithmetic: 17.4 us -> 0.06 us
    psum x3 -> x1, blocking collectives: 361 us -> 18.3 us  [all_sum(): return lax.psum(x, 'gz')]
    ppermute x84 -> x12, starting transfers between devices: 337 us -> 39.8 us  [shift(): return lax.ppermute(x, axis, pairs)]
    pallas_call x0 -> x7, Pallas kernels: none -> 70.6 us  [run(): pl.pallas_call(kernel, out_shape=[jax.ShapeDtypeStruct(s, f32) for s in o...]
    all_to_all x0 -> x2, blocking collectives: none -> 24.6 us  [all_sum(): x = jnp.sum(lax.all_to_all(copies, axis, 0, 0), axis=0)]
    ppermute x84 -> x12, waiting for transfers between devices: 72.8 us -> 68.9 us  [shift(): return lax.ppermute(x, axis, pairs)]
  transfers between devices with their start and end apart: 84 -> 12, of which waited for: 55 -> 11; matrix products, arithmetic and copies ran while one was open for 0% -> 0% of each run, Pallas kernels for 0% -> 0%
where the time goes in v1:
time: 234 us; the launch traced here: 230 us
  Pallas kernels  70.6 us (30%)
  waiting for transfers between devices  68.9 us (29%)
  blocking collectives  42.9 us (18%)
  starting transfers between devices  39.8 us (17%)
  local copies, waits for them, and re-layouts  7.22 us (3%)
    pallas_call x7, Pallas kernels, run(): pl.pallas_call(kernel, out_shape=[jax.ShapeDtypeStruct(s, f32) for s in o...  70.6 us
    ppermute x12, waiting for transfers between devices, shift(): return lax.ppermute(x, axis, pairs)  68.9 us
    ppermute x12, starting transfers between devices, shift(): return lax.ppermute(x, axis, pairs)  39.8 us
    all_to_all x2, blocking collectives, all_sum(): x = jnp.sum(lax.all_to_all(copies, axis, 0, 0), axis=0)  24.6 us
    psum x1, blocking collectives, all_sum(): return lax.psum(x, 'gz')  18.3 us
  transfers between devices with their start and end apart: 12, of which 11 were waited for; matrix products, arithmetic and copies ran while one was open for 0% of the time, Pallas kernels for 0%

profile of v1, /device:TPU:1, one launch (start us, length us, event | category | flops | bytes accessed | tf_op | source)
XLA Modules:
  0.0 230.3 jit_solution(5789131203181724108)
XLA Ops:
  0.6 0.8 fusion.1
  1.4 0.8 fusion
  2.2 0.9 fusion.2
  3.1 9.6 %collective-permute-start = (f32[17,16,128]{2,1,0:T(8,128)S(1)}, f32[17,16,128]{2,1,0:T(8,128)S(1)}, u32[]{:S(2)}, u32[]{:S(2)}) collective-permute-start(f32[17,16,128]{2,1,0:T(8,128)S(1)} %pad_maximum_fusion), channel_id=1, source_target_pairs={{0,1},{1,2},{2,3},{4,5},{5,6},{6,7},{8,9},{9,10},{10,11},{12,13},{... | collective-permute-start | bytes 417800 | tf_op jit(solution)/shard_map/ppermute | solution.py:61
  12.8 1.3 collective-permute-start.1
  14.1 1.0 collective-permute-done
  15.1 0.0 copy-start
  15.1 19.1 %collective-permute-done.1 = f32[17,16,128]{2,1,0:T(8,128)S(1)} collective-permute-done((f32[17,16,128]{2,1,0:T(8,128)S(1)}, f32[17,16,128]{2,1,0:T(8,128)S(1)}, u32[]{:S(2)}, u32[]{:S(2)}) %collective-permute-start.1) | collective-permute-done | bytes 139296 | tf_op jit(solution)/shard_map/ppermute | solution.py:61
  34.2 0.0 copy-start.1
  34.2 0.0 copy-done
  34.2 0.6 copy-done.1
  34.9 2.4 %pack_y.1 = (f32[816,128]{1,0:T(8,128)}, f32[816,128]{1,0:T(8,128)}) custom-call(f32[512,128]{1,0:T(8,128)} %bitcast.8, f32[512,128]{1,0:T(8,128)} %bitcast.12, f32[512,128]{1,0:T(8,128)} %bitcast.10, f32[272,128]{1,0:T(8,128)} %bitcast.17, f32[272,128]{1,0:T(8,128)} %bitcast.19), custom_call_target="tpu_custom_call" | custom-call | tf_op jit(solution)/shard_map/pack_y/pallas_call | solution.py:48
  37.2 1.3 collective-permute-start.2
  38.5 1.3 collective-permute-start.3
  39.8 7.3 %collective-permute-done.2.ylo = f32[816,128]{1,0:T(8,128)S(1)} collective-permute-done((f32[816,128]{1,0:T(8,128)}, f32[816,128]{1,0:T(8,128)S(1)}, u32[]{:S(2)}, u32[]{:S(2)}) %collective-permute-start.2) | collective-permute-done | bytes 417824 | tf_op jit(solution)/shard_map/ppermute | solution.py:61
  47.1 0.0 copy-start.2
  47.1 12.7 %collective-permute-done.3.yhi = f32[816,128]{1,0:T(8,128)S(1)} collective-permute-done((f32[816,128]{1,0:T(8,128)}, f32[816,128]{1,0:T(8,128)S(1)}, u32[]{:S(2)}, u32[]{:S(2)}) %collective-permute-start.3) | collective-permute-done | bytes 417824 | tf_op jit(solution)/shard_map/ppermute | solution.py:61
  59.8 0.0 copy-done.2
  59.8 0.0 copy-start.3
  59.8 0.8 copy-done.3
  60.6 3.8 %frame.1 = (f32[1536,128]{1,0:T(8,128)}, f32[1536,128]{1,0:T(8,128)}, f32[1536,128]{1,0:T(8,128)}, f32[288,128]{1,0:T(8,128)}, f32[288,128]{1,0:T(8,128)}) custom-call(f32[512,128]{1,0:T(8,128)} %bitcast.9, f32[512,128]{1,0:T(8,128)} %bitcast.13, f32[512,128]{1,0:T(8,128)} %bitcast.11, f32[272,128]{1,0:T(8,128)} %bitcast.18, f32[272,128]{1,0:T(8,128)} %bitcast.20, ...), custom_call_target="tpu_custom_call" | custom-call | tf_op jit(solution)/shard_map/frame/pallas_call | solution.py:48
  64.4 4.9 %collective-permute-start.4 = (f32[288,128]{1,0:T(8,128)}, f32[288,128]{1,0:T(8,128)S(1)}, u32[]{:S(2)}, u32[]{:S(2)}) collective-permute-start(f32[288,128]{1,0:T(8,128)} %get-tuple-element.31), channel_id=1, source_target_pairs={{0,64},{64,128},{128,192},{192,256},{256,320},{320,384},{384,448},... | collective-permute-start | bytes 442376 | tf_op jit(solution)/shard_map/ppermute | solution.py:61
  69.3 1.9 collective-permute-start.5
  71.2 0.5 collective-permute-done.4.rest_1_
  71.7 0.0 copy-start.8
  71.7 4.3 %collective-permute-done.5.rest_2_ = f32[288,128]{1,0:T(8,128)S(1)} collective-permute-done((f32[288,128]{1,0:T(8,128)}, f32[288,128]{1,0:T(8,128)S(1)}, u32[]{:S(2)}, u32[]{:S(2)}) %collective-permute-start.5) | collective-permute-done | bytes 147488 | tf_op jit(solution)/shard_map/ppermute | solution.py:61
  76.0 0.0 copy-start.9
  76.0 0.0 copy-done.8
  76.0 0.7 copy-done.9
  76.6 25.4 %first_stage.1 = (f32[32,16,128]{2,1,0:T(8,128)}, f32[32,16,128]{2,1,0:T(8,128)}, f32[8,16,128]{2,1,0:T(8,128)}, f32[8,16,128]{2,1,0:T(8,128)}, f32[48,32,128]{2...) custom-call(f32[48,32,128]{2,1,0:T(8,128)} %bitcast.14, ...), custom_call_target="tpu_custom_call" | custom-call | tf_op jit(solution)/shard_map/first_stage/pallas_call | solution.py:48
  102.0 7.3 %collective-permute-start.6 = (f32[8,16,128]{2,1,0:T(8,128)}, f32[8,16,128]{2,1,0:T(8,128)S(1)}, u32[]{:S(2)}, u32[]{:S(2)}) collective-permute-start(f32[8,16,128]{2,1,0:T(8,128)} %get-tuple-element.35), channel_id=1, source_target_pairs={{0,1},{1,2},{2,3},{4,5},{5,6},{6,7},{8,9},{9,10},{10,11},{12,13},{... | collective-permute-start | bytes 196616 | tf_op jit(solution)/shard_map/ppermute | solution.py:61
  109.3 1.3 collective-permute-start.7
  110.6 0.3 collective-permute-done.6.lo_ref.zlo
  110.9 0.0 copy-start.4
  110.9 9.4 %collective-permute-done.7.hi_ref.zhi = f32[8,16,128]{2,1,0:T(8,128)S(1)} collective-permute-done((f32[8,16,128]{2,1,0:T(8,128)}, f32[8,16,128]{2,1,0:T(8,128)S(1)}, u32[]{:S(2)}, u32[]{:S(2)}) %collective-permute-start.7) | collective-permute-done | bytes 65568 | tf_op jit(solution)/shard_map/ppermute | solution.py:61
  120.3 0.0 copy-start.5
  120.3 0.0 copy-done.4
  120.3 0.6 copy-done.5
  120.9 1.8 pack_y2.1
  122.7 1.9 collective-permute-start.8
  124.5 1.3 collective-permute-start.9
  125.8 1.6 collective-permute-done.8.ylo
  127.4 0.0 copy-start.6
  127.4 9.0 %collective-permute-done.9.yhi = f32[48,8,128]{2,1,0:T(8,128)S(1)} collective-permute-done((f32[48,8,128]{2,1,0:T(8,128)}, f32[48,8,128]{2,1,0:T(8,128)S(1)}, u32[]{:S(2)}, u32[]{:S(2)}) %collective-permute-start.9) | collective-permute-done | bytes 196640 | tf_op jit(solution)/shard_map/ppermute | solution.py:61
  136.5 0.0 copy-done.6
  136.5 0.0 copy-start.7
  136.5 0.7 copy-done.7
  137.1 2.4 %frame2.1 = (f32[48,32,128]{2,1,0:T(8,128)}, f32[96,128]{1,0:T(8,128)}, f32[96,128]{1,0:T(8,128)}) custom-call(f32[32,16,128]{2,1,0:T(8,128)} %get-tuple-element.34.w_ref, f32[8,16,128]{2,1,0:T(8,128)} %copy-done.4, f32[8,16,128]{2,1,0:T(8,128)} %copy-done.5, f32[48,8,128]{2,1,0:T(8,128)} %copy-done.6, f32[48,8,128]{2,1,0:T(8,128)} %copy-done.7), custom_call_target="tpu_custom_call" | custom-call | tf_op jit(solution)/shard_map/frame2/pallas_call | solution.py:48
  139.5 5.9 %collective-permute-start.10 = (f32[96,128]{1,0:T(8,128)}, f32[96,128]{1,0:T(8,128)S(1)}, u32[]{:S(2)}, u32[]{:S(2)}) collective-permute-start(f32[96,128]{1,0:T(8,128)} %get-tuple-element.40), channel_id=1, source_target_pairs={{0,64},{64,128},{128,192},{192,256},{256,320},{320,384},{384,448},... | collective-permute-start | bytes 147464 | tf_op jit(solution)/shard_map/ppermute | solution.py:61
  145.4 1.9 collective-permute-start.11
  147.3 0.0 collective-permute-done.10.lo
  147.4 0.0 copy-start.10
  147.4 3.7 %collective-permute-done.11.hi = f32[96,128]{1,0:T(8,128)S(1)} collective-permute-done((f32[96,128]{1,0:T(8,128)}, f32[96,128]{1,0:T(8,128)S(1)}, u32[]{:S(2)}, u32[]{:S(2)}) %collective-permute-start.11) | collective-permute-done | bytes 49184 | tf_op jit(solution)/shard_map/ppermute | solution.py:61
  151.0 0.0 copy-start.11
  151.0 0.0 copy-done.10
  151.0 0.6 copy-done.11
  151.7 32.6 %second_stage.1 = (f32[32,16,128]{2,1,0:T(8,128)}, f32[32,16,128]{2,1,0:T(8,128)}, f32[32,16,128]{2,1,0:T(8,128)}, f32[32,128]{1,0:T(8,128)}) custom-call(f32[48,32,128]{2,1,0:T(8,128)} %get-tuple-element.39.we, f32[96,128]{1,0:T(8,128)} %copy-done.10, f32[96,128]{1,0:T(8,128)} %copy-done.11, f32[32,16,128]{2,1,0:T(8,128)} %get-tuple-element.33.r_ref, ...), custom_call_target="tpu_custom_call" | custom-call | tf_op jit(solution)/shard_map/second_stage/pallas_call | solution.py:48
  184.2 0.7 broadcast_in_dim.4
  185.0 8.4 %all_to_all.10 = f32[8,32,128]{2,1,0:T(8,128)S(1)} all-to-all(f32[8,32,128]{2,1,0:T(8,128)S(1)} %broadcast_in_dim.4), channel_id=1, replica_groups=mesh['gx'=8,'gy'=16,'gz'=4] {'gx'}, dimensions={0} | all-to-all | bytes 262144 | tf_op jit(solution)/shard_map/all_to_all | solution.py:277
  193.4 16.1 %all_to_all.11 = f32[16,32,128]{2,1,0:T(8,128)S(1)} all-to-all(f32[16,32,128]{2,1,0:T(8,128)S(1)} %broadcast_in_dim.5), channel_id=1, replica_groups=mesh['gx'=8,'gy'=16,'gz'=4] {'gy'}, dimensions={0} | all-to-all | bytes 524288 | tf_op jit(solution)/shard_map/all_to_all | solution.py:277
  209.6 18.3 %psum.7.dots = f32[32,128]{1,0:T(8,128)} all-reduce(f32[32,128]{1,0:T(8,128)S(1)} %reduce_sum.19), channel_id=1, replica_groups=mesh['gx'=8,'gy'=16,'gz'=4] {'gz'}, use_global_device_ids=true, to_apply=%region_2.0 | all-reduce | flops 4096 | bytes 32768 | tf_op jit(solution)/shard_map/psum | solution.py:278
  227.9 2.4 %finish.1 = (f32[32,16,128]{2,1,0:T(8,128)}, f32[32,16,128]{2,1,0:T(8,128)}) custom-call(f32[32,16,128]{2,1,0:T(8,128)} %x_ref.1, f32[32,16,128]{2,1,0:T(8,128)} %get-tuple-element.33.r_ref, f32[32,16,128]{2,1,0:T(8,128)} %get-tuple-element.34.w_ref, f32[32,16,128]{2,1,0:T(8,128)} %get-tuple-element.46.v1, f32[32,16,128]{2,1,0:T(8,128)} %get-tuple-element.47.v2, ...), custom_call_target="tpu_custom_call" | custom-call | tf_op jit(solution)/shard_map/finish/pallas_call | solution.py:48
  (5 shorter events, 0.1 us)
Async XLA Ops:
  3.1 12.0 %collective-permute-start = (f32[17,16,128]{2,1,0:T(8,128)S(1)}, f32[17,16,128]{2,1,0:T(8,128)S(1)}, u32[]{:S(2)}, u32[]{:S(2)}) collective-permute-start(f32[17,16,128]{2,1,0:T(8,128)S(1)} %pad_maximum_fusion), channel_id=1, source_target_pairs={{0,1},{1,2},{2,3},{4,5},{5,6},{6,7},{8,9},{9,10},{10,11},{12,13},{... | collective-permute-start | bytes 417800 | tf_op jit(solution)/shard_map/ppermute | solution.py:61
  12.8 21.4 %collective-permute-start.1 = (f32[17,16,128]{2,1,0:T(8,128)S(1)}, f32[17,16,128]{2,1,0:T(8,128)S(1)}, u32[]{:S(2)}, u32[]{:S(2)}) collective-permute-start(f32[17,16,128]{2,1,0:T(8,128)S(1)} %pad_maximum_fusion.1), channel_id=1, source_target_pairs={{1,0},{2,1},{3,2},{5,4},{6,5},{7,6},{9,8},{10,9},{11,10},{13,12},{... | collective-permute-start | bytes 417800 | tf_op jit(solution)/shard_map/ppermute | solution.py:61
  15.1 19.1 %copy-start = (f32[17,16,128]{2,1,0:T(8,128)}, f32[17,16,128]{2,1,0:T(8,128)S(1)}, u32[]{:S(2)}) copy-start(f32[17,16,128]{2,1,0:T(8,128)S(1)} %collective-permute-done) | copy-start | bytes 417796
  34.2 0.7 copy-start.1
  37.2 9.9 %collective-permute-start.2 = (f32[816,128]{1,0:T(8,128)}, f32[816,128]{1,0:T(8,128)S(1)}, u32[]{:S(2)}, u32[]{:S(2)}) collective-permute-start(f32[816,128]{1,0:T(8,128)} %get-tuple-element.26), channel_id=1, source_target_pairs={{0,4},{4,8},{8,12},{12,16},{16,20},{20,24},{24,28},{28,32},{32,36}... | collective-permute-start | bytes 1253384 | tf_op jit(solution)/shard_map/ppermute | solution.py:61
  38.5 21.3 %collective-permute-start.3 = (f32[816,128]{1,0:T(8,128)}, f32[816,128]{1,0:T(8,128)S(1)}, u32[]{:S(2)}, u32[]{:S(2)}) collective-permute-start(f32[816,128]{1,0:T(8,128)} %get-tuple-element.27), channel_id=1, source_target_pairs={{4,0},{8,4},{12,8},{16,12},{20,16},{24,20},{28,24},{32,28},{36,32}... | collective-permute-start | bytes 1253384 | tf_op jit(solution)/shard_map/ppermute | solution.py:61
  47.1 12.7 %copy-start.2 = (f32[816,128]{1,0:T(8,128)}, f32[816,128]{1,0:T(8,128)S(1)}, u32[]{:S(2)}) copy-start(f32[816,128]{1,0:T(8,128)S(1)} %collective-permute-done.2.ylo) | copy-start | bytes 1253380
  59.8 0.8 copy-start.3
  64.4 7.3 %collective-permute-start.4 = (f32[288,128]{1,0:T(8,128)}, f32[288,128]{1,0:T(8,128)S(1)}, u32[]{:S(2)}, u32[]{:S(2)}) collective-permute-start(f32[288,128]{1,0:T(8,128)} %get-tuple-element.31), channel_id=1, source_target_pairs={{0,64},{64,128},{128,192},{192,256},{256,320},{320,384},{384,448},... | collective-permute-start | bytes 442376 | tf_op jit(solution)/shard_map/ppermute | solution.py:61
  69.3 6.7 %collective-permute-start.5 = (f32[288,128]{1,0:T(8,128)}, f32[288,128]{1,0:T(8,128)S(1)}, u32[]{:S(2)}, u32[]{:S(2)}) collective-permute-start(f32[288,128]{1,0:T(8,128)} %get-tuple-element.32), channel_id=1, source_target_pairs={{64,0},{128,64},{192,128},{256,192},{320,256},{384,320},{448,384},... | collective-permute-start | bytes 442376 | tf_op jit(solution)/shard_map/ppermute | solution.py:61
  71.7 4.3 %copy-start.8 = (f32[288,128]{1,0:T(8,128)}, f32[288,128]{1,0:T(8,128)S(1)}, u32[]{:S(2)}) copy-start(f32[288,128]{1,0:T(8,128)S(1)} %collective-permute-done.4.rest_1_) | copy-start | bytes 442372
  76.0 0.7 copy-start.9
  102.0 8.9 %collective-permute-start.6 = (f32[8,16,128]{2,1,0:T(8,128)}, f32[8,16,128]{2,1,0:T(8,128)S(1)}, u32[]{:S(2)}, u32[]{:S(2)}) collective-permute-start(f32[8,16,128]{2,1,0:T(8,128)} %get-tuple-element.35), channel_id=1, source_target_pairs={{0,1},{1,2},{2,3},{4,5},{5,6},{6,7},{8,9},{9,10},{10,11},{12,13},{... | collective-permute-start | bytes 196616 | tf_op jit(solution)/shard_map/ppermute | solution.py:61
  109.3 11.0 %collective-permute-start.7 = (f32[8,16,128]{2,1,0:T(8,128)}, f32[8,16,128]{2,1,0:T(8,128)S(1)}, u32[]{:S(2)}, u32[]{:S(2)}) collective-permute-start(f32[8,16,128]{2,1,0:T(8,128)} %get-tuple-element.36), channel_id=1, source_target_pairs={{1,0},{2,1},{3,2},{5,4},{6,5},{7,6},{9,8},{10,9},{11,10},{13,12},{... | collective-permute-start | bytes 196616 | tf_op jit(solution)/shard_map/ppermute | solution.py:61
  110.9 9.4 %copy-start.4 = (f32[8,16,128]{2,1,0:T(8,128)}, f32[8,16,128]{2,1,0:T(8,128)S(1)}, u32[]{:S(2)}) copy-start(f32[8,16,128]{2,1,0:T(8,128)S(1)} %collective-permute-done.6.lo_ref.zlo) | copy-start | bytes 196612
  120.3 0.6 copy-start.5
  122.7 4.8 %collective-permute-start.8 = (f32[48,8,128]{2,1,0:T(8,128)}, f32[48,8,128]{2,1,0:T(8,128)S(1)}, u32[]{:S(2)}, u32[]{:S(2)}) collective-permute-start(f32[48,8,128]{2,1,0:T(8,128)} %get-tuple-element.37), channel_id=1, source_target_pairs={{0,4},{4,8},{8,12},{12,16},{16,20},{20,24},{24,28},{28,32},{32,36}... | collective-permute-start | bytes 589832 | tf_op jit(solution)/shard_map/ppermute | solution.py:61
  124.5 11.9 %collective-permute-start.9 = (f32[48,8,128]{2,1,0:T(8,128)}, f32[48,8,128]{2,1,0:T(8,128)S(1)}, u32[]{:S(2)}, u32[]{:S(2)}) collective-permute-start(f32[48,8,128]{2,1,0:T(8,128)} %get-tuple-element.38), channel_id=1, source_target_pairs={{4,0},{8,4},{12,8},{16,12},{20,16},{24,20},{28,24},{32,28},{36,32}... | collective-permute-start | bytes 589832 | tf_op jit(solution)/shard_map/ppermute | solution.py:61
  127.4 9.0 %copy-start.6 = (f32[48,8,128]{2,1,0:T(8,128)}, f32[48,8,128]{2,1,0:T(8,128)S(1)}, u32[]{:S(2)}) copy-start(f32[48,8,128]{2,1,0:T(8,128)S(1)} %collective-permute-done.8.ylo) | copy-start | bytes 589828
  136.5 0.7 copy-start.7
  139.5 7.8 %collective-permute-start.10 = (f32[96,128]{1,0:T(8,128)}, f32[96,128]{1,0:T(8,128)S(1)}, u32[]{:S(2)}, u32[]{:S(2)}) collective-permute-start(f32[96,128]{1,0:T(8,128)} %get-tuple-element.40), channel_id=1, source_target_pairs={{0,64},{64,128},{128,192},{192,256},{256,320},{320,384},{384,448},... | collective-permute-start | bytes 147464 | tf_op jit(solution)/shard_map/ppermute | solution.py:61
  145.4 5.6 %collective-permute-start.11 = (f32[96,128]{1,0:T(8,128)}, f32[96,128]{1,0:T(8,128)S(1)}, u32[]{:S(2)}, u32[]{:S(2)}) collective-permute-start(f32[96,128]{1,0:T(8,128)} %get-tuple-element.41), channel_id=1, source_target_pairs={{64,0},{128,64},{192,128},{256,192},{320,256},{384,320},{448,384},... | collective-permute-start | bytes 147464 | tf_op jit(solution)/shard_map/ppermute | solution.py:61
  147.4 3.7 %copy-start.10 = (f32[96,128]{1,0:T(8,128)}, f32[96,128]{1,0:T(8,128)S(1)}, u32[]{:S(2)}) copy-start(f32[96,128]{1,0:T(8,128)S(1)} %collective-permute-done.10.lo) | copy-start | bytes 147460
  151.0 0.6 copy-start.11

commit v2 on v1

--- a/solution.py
+++ b/solution.py
@@ -15,9 +15,28 @@
 DEPTHS = (6, 4, 7)
 OFFS = (0, 6, 10)
 LAYERS = 17
-PIECES = [(f, k) for f in range(3) for k in range(DEPTHS[f])]
+PIECES = [(f, t) for f in range(3) for t in range(1, DEPTHS[f] + 1)]
 MAIN_ROWS = LAYERS * NZ
-PACK_ROWS = MAIN_ROWS + LAYERS * 16
+
+
+def place_corners():
+    sizes = [(DEPTHS[f] - t, f, t, side) for f, t in PIECES for side in (0, 1)]
+    free, at = [], {}
+    for n, f, t, side in sorted(sizes, reverse=True):
+        if n == 0:
+            continue
+        for i, used in enumerate(free):
+            if used + n <= 8:
+                break
+        else:
+            free.append(0)
+            i = len(free) - 1
+        at[f, t, side] = MAIN_ROWS + 8 * i + free[i]
+        free[i] += n
+    return at, MAIN_ROWS + 8 * len(free)
+
+
+CORNERS, PACK_ROWS = place_corners()
 Q_PACK = FZ // 16 * FY
 
 
@@ -44,13 +63,14 @@
 VM = pl.BlockSpec(memory_space=pltpu.VMEM)
 
 
-def run(kernel, outs, args, scratch=(), name=None):
+def run(kernel, outs, args, scratch=(), name=None, mib=16):
     return pl.pallas_call(
         kernel,
         out_shape=[jax.ShapeDtypeStruct(s, f32) for s in outs],
         in_specs=[VM] * len(args),
         out_specs=[VM] * len(outs),
         scratch_shapes=list(scratch),
+        compiler_params=pltpu.CompilerParams(vmem_limit_bytes=mib << 20),
         name=name,
     )(*args)
 
@@ -69,14 +89,15 @@
 
 def pack_y(x_ref, b_ref, k_ref, lo_ref, hi_ref, dn_ref, up_ref):
     fields = (x_ref, b_ref, k_ref)
-    for i, (f, k) in enumerate(PIECES):
-        d = DEPTHS[f]
-        for out, row in ((dn_ref, k), (up_ref, NY - d + k)):
+    for i, (f, t) in enumerate(PIECES):
+        d, n = DEPTHS[f], DEPTHS[f] - t
+        for out, row in ((dn_ref, t - 1), (up_ref, NY - t)):
             out[i * NZ : (i + 1) * NZ, :] = fields[f][pl.ds(row, NZ, stride=NY), :]
-            at = MAIN_ROWS + i * 16
-            first = OFFS[f] * NY + row
-            out[at : at + d, :] = lo_ref[pl.ds(first, d, stride=NY), :]
-            out[at + 8 : at + 8 + d, :] = hi_ref[pl.ds(first, d, stride=NY), :]
+            if n:
+                at = CORNERS[f, t, 0]
+                out[at : at + n, :] = lo_ref[pl.ds((OFFS[f] + d - n) * NY + row, n, stride=NY), :]
+                at = CORNERS[f, t, 1]
+                out[at : at + n, :] = hi_ref[pl.ds(OFFS[f] * NY + row, n, stride=NY), :]
 
 
 def pack_lanes(read, dn_ref, up_ref, base):
@@ -119,40 +140,54 @@
             out[at : at + NY, :] = zlo[src : src + NY, :]
             at = (G + NZ + j) * FY + G
             out[at : at + NY, :] = zhi[src : src + NY, :]
-        for k in range(d):
-            i = OFFS[f] + k
-            h = MAIN_ROWS + i * 16
-            for src, row in ((ylo, G - d + k), (yhi, G + NY + k)):
+        for t in range(1, d + 1):
+            i, n = OFFS[f] + t - 1, d - t
+            for src, row in ((ylo, G - t), (yhi, G + NY + t - 1)):
                 out[pl.ds(G * FY + row, NZ, stride=FY), :] = src[i * NZ : (i + 1) * NZ, :]
-                out[pl.ds((G - d) * FY + row, d, stride=FY), :] = src[h : h + d, :]
-                out[pl.ds((G + NZ) * FY + row, d, stride=FY), :] = src[h + 8 : h + 8 + d, :]
+                if n:
+                    at = CORNERS[f, t, 0]
+                    out[pl.ds((G - n) * FY + row, n, stride=FY), :] = src[at : at + n, :]
+                    at = CORNERS[f, t, 1]
+                    out[pl.ds((G + NZ) * FY + row, n, stride=FY), :] = src[at : at + n, :]
         pack_lanes(lambda z: out[z * FY : (z + 1) * FY, :], dn_ref, up_ref, f * Q_PACK)
 
 
+PLANES = 4
+
+
 def apply_k(src, dst, coef, mask, first, last, finish=None):
-    lane = lax.broadcasted_iota(jnp.int32, (FY, NX), 1)
     s0, s1 = src
     c0, c1 = coef
     m0, m1 = mask
 
-    def plane(z, _):
-        v0, v1 = s0[z], s1[z]
-        a0, a1 = pltpu.roll(v0, 1, 1), pltpu.roll(v1, 1, 1)
-        b0, b1 = pltpu.roll(v0, NX - 1, 1), pltpu.roll(v1, NX - 1, 1)
+    def planes(z, n):
+        lane = lax.broadcasted_iota(jnp.int32, (n, FY, NX), 2)
+        here, below, above = pl.ds(z, n), pl.ds(z - 1, n), pl.ds(z + 1, n)
+        v0, v1 = s0[here], s1[here]
+        a0, a1 = pltpu.roll(v0, 1, 2), pltpu.roll(v1, 1, 2)
+        b0, b1 = pltpu.roll(v0, NX - 1, 2), pltpu.roll(v1, NX - 1, 2)
         t0 = jnp.where(lane == 0, a1, a0) + jnp.where(lane == NX - 1, b1, b0)
         t1 = jnp.where(lane == 0, a0, a1) + jnp.where(lane == NX - 1, b0, b1)
-        t0 = t0 + pltpu.roll(v0, 1, 0) + pltpu.roll(v0, FY - 1, 0) + s0[z - 1] + s0[z + 1]
-        t1 = t1 + pltpu.roll(v1, 1, 0) + pltpu.roll(v1, FY - 1, 0) + s1[z - 1] + s1[z + 1]
-        r0 = c0[z] * v0 - m0[z] * t0
-        r1 = c1[z] * v1 - m1[z] * t1
+        t0 = t0 + (pltpu.roll(v0, 1, 1) + pltpu.roll(v0, FY - 1, 1)) + (s0[below] + s0[above])
+        t1 = t1 + (pltpu.roll(v1, 1, 1) + pltpu.roll(v1, FY - 1, 1)) + (s1[below] + s1[above])
+        r0 = c0[here] * v0 - m0[here] * t0
+        r1 = c1[here] * v1 - m1[here] * t1
         if finish is None:
-            dst[0][z] = r0
-            dst[1][z] = r1
+            dst[0][here] = r0
+            dst[1][here] = r1
         else:
-            finish(z, r0, r1)
+            finish(z, n, r0, r1)
+
+    count = last - first
+    whole = count // PLANES
+
+    def step(i, _):
+        planes(first + i * PLANES, PLANES)
         return 0
 
-    lax.fori_loop(first, last, plane, 0)
+    lax.fori_loop(0, whole, step, 0)
+    if count % PLANES:
+        planes(first + whole * PLANES, count % PLANES)
 
 
 def span(radius):
@@ -180,19 +215,22 @@
 
     apply_k((xe, x1), p, coef, mask, *span(5))
 
-    def to_residual(z, v0, v1):
-        be[z] = be[z] - v0 * (1.0 / SQ)
-        b1[z] = b1[z] - v1 * (1.0 / SQ)
+    def to_residual(z, n, v0, v1):
+        at = pl.ds(z, n)
+        be[at] = be[at] - v0 * (1.0 / SQ)
+        b1[at] = b1[at] - v1 * (1.0 / SQ)
 
     apply_k(p, None, coef, mask, *span(4), finish=to_residual)
     apply_k(b, p, coef, mask, *span(3))
     apply_k(p, q, coef, mask, *span(2))
     apply_k(q, p, coef, mask, *span(1))
 
-    def to_precond(z, v0, v1):
-        w = C0 * be[z] + (C1 / SQ) * q0[z] + (C2 / SQ**2) * v0
-        w_out[z - G] = w[G : G + NY, :]
-        r_out[z - G] = be[z][G : G + NY, :]
+    def to_precond(z, n, v0, v1):
+        at = pl.ds(z, n)
+        r = be[at]
+        w = C0 * r + (C1 / SQ) * q0[at] + (C2 / SQ**2) * v0
+        w_out[pl.ds(z - G, n)] = w[:, G : G + NY, :]
+        r_out[pl.ds(z - G, n)] = r[:, G : G + NY, :]
 
     apply_k(p, None, coef, mask, *span(0), finish=to_precond)
     wdn[...] = w_out[0:G]
@@ -217,7 +255,7 @@
     pack_lanes(lambda z: we[z], dn_ref, up_ref, 0)
 
 
-def second_stage(we, lo, hi, r_ref, c0, c1, m0, m1, v1_out, v2_out, v3_out, dots, w1, p0, p1, q0, q1, s0, s1):
+def second_stage(we, lo, hi, r_ref, c0, c1, m0, m1, v1_out, v2_out, v3_out, dots, acc, w1, p0, p1, q0, q1, s0, s1):
     def write(z, v):
         w1[z] = v
 
@@ -229,32 +267,37 @@
     apply_k(p, s, coef, mask, *span(4))
     apply_k(s, p, coef, mask, *span(3))
 
-    def to_w2(z, a0, a1):
-        s0[z] = C0 * q0[z] + (C1 / SQ) * s0[z] + (C2 / SQ**2) * a0
-        s1[z] = C0 * q1[z] + (C1 / SQ) * s1[z] + (C2 / SQ**2) * a1
+    def to_w2(z, n, a0, a1):
+        at = pl.ds(z, n)
+        s0[at] = C0 * q0[at] + (C1 / SQ) * s0[at] + (C2 / SQ**2) * a0
+        s1[at] = C0 * q1[at] + (C1 / SQ) * s1[at] + (C2 / SQ**2) * a1
 
     apply_k(p, None, coef, mask, *span(2), finish=to_w2)
     apply_k(s, p, coef, mask, *span(1))
-    dots[...] = jnp.zeros((32, NX), f32)
-
-    def to_w3(z, a0, a1):
+    acc[...] = jnp.zeros((4, G, NX), f32)
+
+    def to_w3(z, n, a0, a1):
+        at, to = pl.ds(z, n), pl.ds(z - G, n)
         rows = slice(G, G + NY)
-        w = we[z][rows]
-        u1 = q0[z][rows]
-        u2 = s0[z][rows]
-        u3 = a0[rows]
-        v1_out[z - G] = u1
-        v2_out[z - G] = u2
-        v3_out[z - G] = u3
-        for i, t in enumerate((r_ref[z - G] * w, w * u1, u1 * u2, u2 * u3)):
-            dots[8 * i : 8 * i + 8, :] += t[0:8] + t[8:16]
+        w = we[at][:, rows]
+        u1 = q0[at][:, rows]
+        u2 = s0[at][:, rows]
+        u3 = a0[:, rows]
+        v1_out[to] = u1
+        v2_out[to] = u2
+        v3_out[to] = u3
+        for i, t in enumerate((r_ref[to] * w, w * u1, u1 * u2, u2 * u3)):
+            acc[i] += jnp.sum(t[:, 0:8] + t[:, 8:16], axis=0)
 
     apply_k(p, None, coef, mask, *span(0), finish=to_w3)
+    dots[...] = jnp.zeros((G, NX), f32)
+    for i in range(4):
+        dots[i : i + 1, :] = jnp.sum(acc[i], axis=0, keepdims=True)
 
 
 def finish(x_ref, r_ref, w_ref, v1, v2, v3, dots, x_out, r_out):
     def total(i, scale):
-        return jnp.sum(dots[8 * i : 8 * i + 8, :], keepdims=True) * (1.0 / scale)
+        return jnp.sum(dots[i : i + 1, :], axis=1, keepdims=True) * (1.0 / scale)
 
     e0 = total(0, 1.0)
     g0 = total(1, SQ)
@@ -316,9 +359,9 @@
     xlo, xhi = exchange(down, up, "gx")
     v1, v2, v3, dots = run(
         second_stage,
-        [block, block, block, (32, NX)],
+        [block, block, block, (G, NX)],
         (we, xlo, xhi, r0, c0, c1, m0, m1),
-        scratch=[tile] * 7,
+        scratch=[pltpu.VMEM((4, G, NX), f32)] + [tile] * 7,
         name="second_stage",
     )
     dots = all_sum(dots)

time: 234 us -> 166 us (0.71)
  Pallas kernels: 70.6 us -> 25.9 us
  blocking collectives: 42.9 us -> 31.9 us
  local copies, waits for them, and re-layouts: 7.22 us -> 1.69 us
  waiting for transfers between devices: 68.9 us -> 63.7 us
    pallas_call x7, Pallas kernels: 70.6 us -> 25.9 us  [run(): pl.pallas_call(kernel, out_shape=[jax.ShapeDtypeStruct(s, f32) for s in o...]
    psum x1, blocking collectives: 18.3 us -> 10.7 us  [all_sum(): return lax.psum(x, 'gz')]
    ppermute x12, waiting for transfers between devices: 68.9 us -> 63.7 us  [shift(): return lax.ppermute(x, axis, pairs)]
    unnamed x24 -> x6, local copies, waits for them, and re-layouts: 4.01 us -> 0.02 us
    all_to_all x2, blocking collectives: 24.6 us -> 21.2 us  [all_sum(): x = jnp.sum(lax.all_to_all(copies, axis, 0, 0), axis=0)]
  transfers between devices with their start and end apart: 12 -> 12, of which waited for: 11 -> 10; matrix products, arithmetic and copies ran while one was open for 0% -> 0% of each run, Pallas kernels for 0% -> 0%
where the time goes in v2:
time: 166 us; the launch traced here: 164 us
  waiting for transfers between devices  63.7 us (38%)
  starting transfers between devices  39.7 us (24%)
  blocking collectives  31.9 us (19%)
  Pallas kernels  25.9 us (16%)
  local copies, waits for them, and re-layouts  1.69 us (1%)
    ppermute x12, waiting for transfers between devices, shift(): return lax.ppermute(x, axis, pairs)  63.7 us
    ppermute x12, starting transfers between devices, shift(): return lax.ppermute(x, axis, pairs)  39.7 us
    pallas_call x7, Pallas kernels, run(): pl.pallas_call(kernel, out_shape=[jax.ShapeDtypeStruct(s, f32) for s in o...  25.9 us
    all_to_all x2, blocking collectives, all_sum(): x = jnp.sum(lax.all_to_all(copies, axis, 0, 0), axis=0)  21.2 us
    psum x1, blocking collectives, all_sum(): return lax.psum(x, 'gz')  10.7 us
  transfers between devices with their start and end apart: 12, of which 10 were waited for; matrix products, arithmetic and copies ran while one was open for 0% of the time, Pallas kernels for 0%

profile of v2, /device:TPU:1, one launch (start us, length us, event | category | flops | bytes accessed | tf_op | source)
XLA Modules:
  0.0 163.7 jit_solution(4400317004321566785)
XLA Ops:
  0.6 0.0 copy-start.1
  0.6 0.8 fusion.1
  1.5 0.8 fusion
  2.3 0.0 copy-done.1
  2.3 0.0 copy-start
  2.3 0.0 copy-start.2
  2.4 9.8 %collective-permute-start = (f32[17,16,128]{2,1,0:T(8,128)S(1)}, f32[17,16,128]{2,1,0:T(8,128)S(1)}, u32[]{:S(2)}, u32[]{:S(2)}) collective-permute-start(f32[17,16,128]{2,1,0:T(8,128)S(1)} %pad_maximum_fusion), channel_id=1, source_target_pairs={{0,1},{1,2},{2,3},{4,5},{5,6},{6,7},{8,9},{9,10},{10,11},{12,13},{... | collective-permute-start | bytes 417800 | tf_op jit(solution)/shard_map/ppermute | solution.py:81
  12.2 1.3 collective-permute-start.1
  13.5 1.0 collective-permute-done
  14.5 19.1 %collective-permute-done.1 = f32[17,16,128]{2,1,0:T(8,128)S(1)} collective-permute-done((f32[17,16,128]{2,1,0:T(8,128)S(1)}, f32[17,16,128]{2,1,0:T(8,128)S(1)}, u32[]{:S(2)}, u32[]{:S(2)}) %collective-permute-start.1) | collective-permute-done | bytes 139296 | tf_op jit(solution)/shard_map/ppermute | solution.py:81
  33.6 0.0 copy-done
  33.6 0.0 copy-done.2
  33.6 0.2 pack_y.1
  33.8 1.3 collective-permute-start.2
  35.1 1.3 collective-permute-start.3
  36.4 5.0 %collective-permute-done.2.ylo = f32[632,128]{1,0:T(8,128)S(1)} collective-permute-done((f32[632,128]{1,0:T(8,128)S(1)}, f32[632,128]{1,0:T(8,128)S(1)}, u32[]{:S(2)}, u32[]{:S(2)}) %collective-permute-start.2) | collective-permute-done | bytes 323616 | tf_op jit(solution)/shard_map/ppermute | solution.py:81
  41.4 10.8 %collective-permute-done.3.yhi = f32[632,128]{1,0:T(8,128)S(1)} collective-permute-done((f32[632,128]{1,0:T(8,128)S(1)}, f32[632,128]{1,0:T(8,128)S(1)}, u32[]{:S(2)}, u32[]{:S(2)}) %collective-permute-start.3) | collective-permute-done | bytes 323616 | tf_op jit(solution)/shard_map/ppermute | solution.py:81
  52.2 1.4 frame.1
  53.6 4.9 %collective-permute-start.4 = (f32[288,128]{1,0:T(8,128)S(1)}, f32[288,128]{1,0:T(8,128)S(1)}, u32[]{:S(2)}, u32[]{:S(2)}) collective-permute-start(f32[288,128]{1,0:T(8,128)S(1)} %get-tuple-element.31), channel_id=1, source_target_pairs={{0,64},{64,128},{128,192},{192,256},{256,320},{320,384},{384,448},... | collective-permute-start | bytes 442376 | tf_op jit(solution)/shard_map/ppermute | solution.py:81
  58.5 1.9 %collective-permute-start.5 = (f32[288,128]{1,0:T(8,128)S(1)}, f32[288,128]{1,0:T(8,128)S(1)}, u32[]{:S(2)}, u32[]{:S(2)}) collective-permute-start(f32[288,128]{1,0:T(8,128)S(1)} %get-tuple-element.32), channel_id=1, source_target_pairs={{64,0},{128,64},{192,128},{256,192},{320,256},{384,320},{448,384},... | collective-permute-start | bytes 442376 | tf_op jit(solution)/shard_map/ppermute | solution.py:81
  60.4 0.2 collective-permute-done.4.rest_1_
  60.6 4.4 %collective-permute-done.5.rest_2_ = f32[288,128]{1,0:T(8,128)S(1)} collective-permute-done((f32[288,128]{1,0:T(8,128)S(1)}, f32[288,128]{1,0:T(8,128)S(1)}, u32[]{:S(2)}, u32[]{:S(2)}) %collective-permute-start.5) | collective-permute-done | bytes 147488 | tf_op jit(solution)/shard_map/ppermute | solution.py:81
  64.9 10.0 %first_stage.1 = (f32[32,16,128]{2,1,0:T(8,128)S(1)}, f32[32,16,128]{2,1,0:T(8,128)S(1)}, f32[8,16,128]{2,1,0:T(8,128)S(1)}, f32[8,16,128]{2,1,0:T(8,128)S(1)}, ...) custom-call(f32[48,32,128]{2,1,0:T(8,128)S(1)} %bitcast.14, ...), custom_call_target="tpu_custom_call" | custom-call | tf_op jit(solution)/shard_map/first_stage/pallas_call | solution.py:67
  75.0 7.3 %collective-permute-start.6 = (f32[8,16,128]{2,1,0:T(8,128)S(1)}, f32[8,16,128]{2,1,0:T(8,128)S(1)}, u32[]{:S(2)}, u32[]{:S(2)}) collective-permute-start(f32[8,16,128]{2,1,0:T(8,128)S(1)} %get-tuple-element.35), channel_id=1, source_target_pairs={{0,1},{1,2},{2,3},{4,5},{5,6},{6,7},{8,9},{9,10},{10,11},{12,13},{... | collective-permute-start | bytes 196616 | tf_op jit(solution)/shard_map/ppermute | solution.py:81
  82.2 1.3 collective-permute-start.7
  83.5 0.0 collective-permute-done.6.lo_ref.zlo
  83.6 9.4 %collective-permute-done.7.hi_ref.zhi = f32[8,16,128]{2,1,0:T(8,128)S(1)} collective-permute-done((f32[8,16,128]{2,1,0:T(8,128)S(1)}, f32[8,16,128]{2,1,0:T(8,128)S(1)}, u32[]{:S(2)}, u32[]{:S(2)}) %collective-permute-start.7) | collective-permute-done | bytes 65568 | tf_op jit(solution)/shard_map/ppermute | solution.py:81
  93.0 1.9 %collective-permute-start.8 = (f32[48,8,128]{2,1,0:T(8,128)S(1)}, f32[48,8,128]{2,1,0:T(8,128)S(1)}, u32[]{:S(2)}, u32[]{:S(2)}) collective-permute-start(f32[48,8,128]{2,1,0:T(8,128)S(1)} %get-tuple-element.37), channel_id=1, source_target_pairs={{0,4},{4,8},{8,12},{12,16},{16,20},{20,24},{24,28},{28,32},{32,36}... | collective-permute-start | bytes 589832 | tf_op jit(solution)/shard_map/ppermute | solution.py:81
  94.8 1.3 collective-permute-start.9
  96.1 1.3 collective-permute-done.8.ylo
  97.4 9.2 %collective-permute-done.9.yhi = f32[48,8,128]{2,1,0:T(8,128)S(1)} collective-permute-done((f32[48,8,128]{2,1,0:T(8,128)S(1)}, f32[48,8,128]{2,1,0:T(8,128)S(1)}, u32[]{:S(2)}, u32[]{:S(2)}) %collective-permute-start.9) | collective-permute-done | bytes 196640 | tf_op jit(solution)/shard_map/ppermute | solution.py:81
  106.6 0.4 frame2.1
  107.0 5.6 %collective-permute-start.10 = (f32[96,128]{1,0:T(8,128)S(1)}, f32[96,128]{1,0:T(8,128)S(1)}, u32[]{:S(2)}, u32[]{:S(2)}) collective-permute-start(f32[96,128]{1,0:T(8,128)S(1)} %get-tuple-element.40), channel_id=1, source_target_pairs={{0,64},{64,128},{128,192},{192,256},{256,320},{320,384},{384,448},... | collective-permute-start | bytes 147464 | tf_op jit(solution)/shard_map/ppermute | solution.py:81
  112.6 1.9 %collective-permute-start.11 = (f32[96,128]{1,0:T(8,128)S(1)}, f32[96,128]{1,0:T(8,128)S(1)}, u32[]{:S(2)}, u32[]{:S(2)}) collective-permute-start(f32[96,128]{1,0:T(8,128)S(1)} %get-tuple-element.41), channel_id=1, source_target_pairs={{64,0},{128,64},{192,128},{256,192},{320,256},{384,320},{448,384},... | collective-permute-start | bytes 147464 | tf_op jit(solution)/shard_map/ppermute | solution.py:81
  114.5 0.0 collective-permute-done.10.lo
  114.6 3.5 %collective-permute-done.11.hi = f32[96,128]{1,0:T(8,128)S(1)} collective-permute-done((f32[96,128]{1,0:T(8,128)S(1)}, f32[96,128]{1,0:T(8,128)S(1)}, u32[]{:S(2)}, u32[]{:S(2)}) %collective-permute-start.11) | collective-permute-done | bytes 49184 | tf_op jit(solution)/shard_map/ppermute | solution.py:81
  118.0 12.8 %second_stage.1 = (f32[32,16,128]{2,1,0:T(8,128)S(1)}, f32[32,16,128]{2,1,0:T(8,128)S(1)}, f32[32,16,128]{2,1,0:T(8,128)S(1)}, f32[8,128]{1,0:T(8,128)S(1)}) custom-call(f32[48,32,128]{2,1,0:T(8,128)S(1)} %get-tuple-element.39.we, f32[96,128]{1,0:T(8,128)S(1)} %collective-permute-done.10.lo, f32[96,128]{1,0:T(8,128)S(1)} %collective-permute-done.11.hi, ...), custom_call_target="tpu_custom_call" | custom-call | tf_op jit(solution)/shard_map/second_stage/pallas_call | solution.py:67
  130.9 7.9 %all_to_all.10 = f32[8,8,128]{2,1,0:T(8,128)S(1)} all-to-all(f32[8,8,128]{2,1,0:T(8,128)S(1)} %broadcast_in_dim.4), channel_id=1, replica_groups=mesh['gx'=8,'gy'=16,'gz'=4] {'gx'}, dimensions={0} | all-to-all | bytes 65536 | tf_op jit(solution)/shard_map/all_to_all | solution.py:320
  138.8 13.3 %all_to_all.11 = f32[16,8,128]{2,1,0:T(8,128)S(1)} all-to-all(f32[16,8,128]{2,1,0:T(8,128)S(1)} %broadcast_in_dim.5), channel_id=1, replica_groups=mesh['gx'=8,'gy'=16,'gz'=4] {'gy'}, dimensions={0} | all-to-all | bytes 131072 | tf_op jit(solution)/shard_map/all_to_all | solution.py:320
  152.1 10.7 %psum.7.dots = f32[8,128]{1,0:T(8,128)S(1)} all-reduce(f32[8,128]{1,0:T(8,128)S(1)} %reduce_sum.19), channel_id=1, replica_groups=mesh['gx'=8,'gy'=16,'gz'=4] {'gz'}, use_global_device_ids=true, to_apply=%region_2.0 | all-reduce | flops 1024 | bytes 8192 | tf_op jit(solution)/shard_map/psum | solution.py:321
  162.8 1.0 finish.1
  (8 shorter events, 0.1 us)
Async XLA Ops:
  0.6 1.7 %copy-start.1 = (f32[32,16,128]{2,1,0:T(8,128)S(1)}, f32[32,16,128]{2,1,0:T(8,128)}, u32[]{:S(2)}) copy-start(f32[32,16,128]{2,1,0:T(8,128)} %param.5) | copy-start | bytes 786436
  2.3 31.3 %copy-start = (f32[32,16,128]{2,1,0:T(8,128)S(1)}, f32[32,16,128]{2,1,0:T(8,128)}, u32[]{:S(2)}) copy-start(f32[32,16,128]{2,1,0:T(8,128)} %x_ref.1) | copy-start | bytes 786436
  2.3 31.3 %copy-start.2 = (f32[32,16,128]{2,1,0:T(8,128)S(1)}, f32[32,16,128]{2,1,0:T(8,128)}, u32[]{:S(2)}) copy-start(f32[32,16,128]{2,1,0:T(8,128)} %param.3) | copy-start | bytes 786436
  2.4 12.1 %collective-permute-start = (f32[17,16,128]{2,1,0:T(8,128)S(1)}, f32[17,16,128]{2,1,0:T(8,128)S(1)}, u32[]{:S(2)}, u32[]{:S(2)}) collective-permute-start(f32[17,16,128]{2,1,0:T(8,128)S(1)} %pad_maximum_fusion), channel_id=1, source_target_pairs={{0,1},{1,2},{2,3},{4,5},{5,6},{6,7},{8,9},{9,10},{10,11},{12,13},{... | collective-permute-start | bytes 417800 | tf_op jit(solution)/shard_map/ppermute | solution.py:81
  12.2 21.4 %collective-permute-start.1 = (f32[17,16,128]{2,1,0:T(8,128)S(1)}, f32[17,16,128]{2,1,0:T(8,128)S(1)}, u32[]{:S(2)}, u32[]{:S(2)}) collective-permute-start(f32[17,16,128]{2,1,0:T(8,128)S(1)} %pad_maximum_fusion.1), channel_id=1, source_target_pairs={{1,0},{2,1},{3,2},{5,4},{6,5},{7,6},{9,8},{10,9},{11,10},{13,12},{... | collective-permute-start | bytes 417800 | tf_op jit(solution)/shard_map/ppermute | solution.py:81
  33.8 7.6 %collective-permute-start.2 = (f32[632,128]{1,0:T(8,128)S(1)}, f32[632,128]{1,0:T(8,128)S(1)}, u32[]{:S(2)}, u32[]{:S(2)}) collective-permute-start(f32[632,128]{1,0:T(8,128)S(1)} %get-tuple-element.26), channel_id=1, source_target_pairs={{0,4},{4,8},{8,12},{12,16},{16,20},{20,24},{24,28},{28,32},{32,36}... | collective-permute-start | bytes 970760 | tf_op jit(solution)/shard_map/ppermute | solution.py:81
  35.1 17.1 %collective-permute-start.3 = (f32[632,128]{1,0:T(8,128)S(1)}, f32[632,128]{1,0:T(8,128)S(1)}, u32[]{:S(2)}, u32[]{:S(2)}) collective-permute-start(f32[632,128]{1,0:T(8,128)S(1)} %get-tuple-element.27), channel_id=1, source_target_pairs={{4,0},{8,4},{12,8},{16,12},{20,16},{24,20},{28,24},{32,28},{36,32}... | collective-permute-start | bytes 970760 | tf_op jit(solution)/shard_map/ppermute | solution.py:81
  53.6 7.0 %collective-permute-start.4 = (f32[288,128]{1,0:T(8,128)S(1)}, f32[288,128]{1,0:T(8,128)S(1)}, u32[]{:S(2)}, u32[]{:S(2)}) collective-permute-start(f32[288,128]{1,0:T(8,128)S(1)} %get-tuple-element.31), channel_id=1, source_target_pairs={{0,64},{64,128},{128,192},{192,256},{256,320},{320,384},{384,448},... | collective-permute-start | bytes 442376 | tf_op jit(solution)/shard_map/ppermute | solution.py:81
  58.5 6.5 %collective-permute-start.5 = (f32[288,128]{1,0:T(8,128)S(1)}, f32[288,128]{1,0:T(8,128)S(1)}, u32[]{:S(2)}, u32[]{:S(2)}) collective-permute-start(f32[288,128]{1,0:T(8,128)S(1)} %get-tuple-element.32), channel_id=1, source_target_pairs={{64,0},{128,64},{192,128},{256,192},{320,256},{384,320},{448,384},... | collective-permute-start | bytes 442376 | tf_op jit(solution)/shard_map/ppermute | solution.py:81
  75.0 8.6 %collective-permute-start.6 = (f32[8,16,128]{2,1,0:T(8,128)S(1)}, f32[8,16,128]{2,1,0:T(8,128)S(1)}, u32[]{:S(2)}, u32[]{:S(2)}) collective-permute-start(f32[8,16,128]{2,1,0:T(8,128)S(1)} %get-tuple-element.35), channel_id=1, source_target_pairs={{0,1},{1,2},{2,3},{4,5},{5,6},{6,7},{8,9},{9,10},{10,11},{12,13},{... | collective-permute-start | bytes 196616 | tf_op jit(solution)/shard_map/ppermute | solution.py:81
  82.2 10.7 %collective-permute-start.7 = (f32[8,16,128]{2,1,0:T(8,128)S(1)}, f32[8,16,128]{2,1,0:T(8,128)S(1)}, u32[]{:S(2)}, u32[]{:S(2)}) collective-permute-start(f32[8,16,128]{2,1,0:T(8,128)S(1)} %get-tuple-element.36), channel_id=1, source_target_pairs={{1,0},{2,1},{3,2},{5,4},{6,5},{7,6},{9,8},{10,9},{11,10},{13,12},{... | collective-permute-start | bytes 196616 | tf_op jit(solution)/shard_map/ppermute | solution.py:81
  93.0 4.4 %collective-permute-start.8 = (f32[48,8,128]{2,1,0:T(8,128)S(1)}, f32[48,8,128]{2,1,0:T(8,128)S(1)}, u32[]{:S(2)}, u32[]{:S(2)}) collective-permute-start(f32[48,8,128]{2,1,0:T(8,128)S(1)} %get-tuple-element.37), channel_id=1, source_target_pairs={{0,4},{4,8},{8,12},{12,16},{16,20},{20,24},{24,28},{28,32},{32,36}... | collective-permute-start | bytes 589832 | tf_op jit(solution)/shard_map/ppermute | solution.py:81
  94.8 11.7 %collective-permute-start.9 = (f32[48,8,128]{2,1,0:T(8,128)S(1)}, f32[48,8,128]{2,1,0:T(8,128)S(1)}, u32[]{:S(2)}, u32[]{:S(2)}) collective-permute-start(f32[48,8,128]{2,1,0:T(8,128)S(1)} %get-tuple-element.38), channel_id=1, source_target_pairs={{4,0},{8,4},{12,8},{16,12},{20,16},{24,20},{28,24},{32,28},{36,32}... | collective-permute-start | bytes 589832 | tf_op jit(solution)/shard_map/ppermute | solution.py:81
  107.0 7.5 %collective-permute-start.10 = (f32[96,128]{1,0:T(8,128)S(1)}, f32[96,128]{1,0:T(8,128)S(1)}, u32[]{:S(2)}, u32[]{:S(2)}) collective-permute-start(f32[96,128]{1,0:T(8,128)S(1)} %get-tuple-element.40), channel_id=1, source_target_pairs={{0,64},{64,128},{128,192},{192,256},{256,320},{320,384},{384,448},... | collective-permute-start | bytes 147464 | tf_op jit(solution)/shard_map/ppermute | solution.py:81
  112.6 5.4 %collective-permute-start.11 = (f32[96,128]{1,0:T(8,128)S(1)}, f32[96,128]{1,0:T(8,128)S(1)}, u32[]{:S(2)}, u32[]{:S(2)}) collective-permute-start(f32[96,128]{1,0:T(8,128)S(1)} %get-tuple-element.41), channel_id=1, source_target_pairs={{64,0},{128,64},{192,128},{256,192},{320,256},{384,320},{448,384},... | collective-permute-start | bytes 147464 | tf_op jit(solution)/shard_map/ppermute | solution.py:81

commit v3 on v2

--- a/solution.py
+++ b/solution.py
@@ -19,24 +19,24 @@
 MAIN_ROWS = LAYERS * NZ
 
 
-def place_corners():
-    sizes = [(DEPTHS[f] - t, f, t, side) for f, t in PIECES for side in (0, 1)]
+def place_corners(depths):
+    sizes = [(d - t, f, t, side) for f, d in enumerate(depths) for t in range(1, d) for side in (0, 1)]
     free, at = [], {}
     for n, f, t, side in sorted(sizes, reverse=True):
-        if n == 0:
-            continue
         for i, used in enumerate(free):
             if used + n <= 8:
                 break
         else:
             free.append(0)
             i = len(free) - 1
-        at[f, t, side] = MAIN_ROWS + 8 * i + free[i]
+        at[f, t, side] = 8 * i + free[i]
         free[i] += n
-    return at, MAIN_ROWS + 8 * len(free)
-
-
-CORNERS, PACK_ROWS = place_corners()
+    return at, 8 * len(free)
+
+
+CORNERS, CORNER_ROWS = place_corners(DEPTHS)
+CORNERS2, CORNER_ROWS2 = place_corners((G,))
+MAIN_ROWS2 = G * NZ
 Q_PACK = FZ // 16 * FY
 
 
@@ -87,12 +87,22 @@
     return from_below, from_above
 
 
-def pack_y(x_ref, b_ref, k_ref, lo_ref, hi_ref, dn_ref, up_ref):
+def pack_block(x_ref, b_ref, k_ref, zdn, zup, ydn, yup):
     fields = (x_ref, b_ref, k_ref)
+    for f, field in enumerate(fields):
+        n = DEPTHS[f] * NY
+        at = OFFS[f] * NY
+        zdn[at : at + n, :] = field[0:n, :]
+        zup[at : at + n, :] = field[NZ * NY - n : NZ * NY, :]
     for i, (f, t) in enumerate(PIECES):
+        for out, row in ((ydn, t - 1), (yup, NY - t)):
+            out[i * NZ : (i + 1) * NZ, :] = fields[f][pl.ds(row, NZ, stride=NY), :]
+
+
+def pack_corners(lo_ref, hi_ref, dn_ref, up_ref):
+    for f, t in PIECES:
         d, n = DEPTHS[f], DEPTHS[f] - t
         for out, row in ((dn_ref, t - 1), (up_ref, NY - t)):
-            out[i * NZ : (i + 1) * NZ, :] = fields[f][pl.ds(row, NZ, stride=NY), :]
             if n:
                 at = CORNERS[f, t, 0]
                 out[at : at + n, :] = lo_ref[pl.ds((OFFS[f] + d - n) * NY + row, n, stride=NY), :]
@@ -126,7 +136,7 @@
             write(16 * q + g, jnp.where(right, a, b))
 
 
-def frame(x_ref, b_ref, k_ref, zlo, zhi, ylo, yhi, xe, be, ke, dn_ref, up_ref):
+def frame(x_ref, b_ref, k_ref, zlo, zhi, ylo, yhi, clo, chi, xe, be, ke, dn_ref, up_ref):
     fields = (x_ref, b_ref, k_ref)
     for f, out in enumerate((xe, be, ke)):
         d = DEPTHS[f]
@@ -142,17 +152,21 @@
             out[at : at + NY, :] = zhi[src : src + NY, :]
         for t in range(1, d + 1):
             i, n = OFFS[f] + t - 1, d - t
-            for src, row in ((ylo, G - t), (yhi, G + NY + t - 1)):
+            for src, corner, row in ((ylo, clo, G - t), (yhi, chi, G + NY + t - 1)):
                 out[pl.ds(G * FY + row, NZ, stride=FY), :] = src[i * NZ : (i + 1) * NZ, :]
                 if n:
                     at = CORNERS[f, t, 0]
-                    out[pl.ds((G - n) * FY + row, n, stride=FY), :] = src[at : at + n, :]
+                    out[pl.ds((G - n) * FY + row, n, stride=FY), :] = corner[at : at + n, :]
                     at = CORNERS[f, t, 1]
-                    out[pl.ds((G + NZ) * FY + row, n, stride=FY), :] = src[at : at + n, :]
+                    out[pl.ds((G + NZ) * FY + row, n, stride=FY), :] = corner[at : at + n, :]
         pack_lanes(lambda z: out[z * FY : (z + 1) * FY, :], dn_ref, up_ref, f * Q_PACK)
 
 
-PLANES = 4
+PLANES = 8
+
+
+def rows_of(z, n, shift=0):
+    return pl.ds(pl.multiple_of(z * FY, FY) + shift, n * FY)
 
 
 def apply_k(src, dst, coef, mask, first, last, finish=None):
@@ -160,23 +174,28 @@
     c0, c1 = coef
     m0, m1 = mask
 
-    def planes(z, n):
-        lane = lax.broadcasted_iota(jnp.int32, (n, FY, NX), 2)
-        here, below, above = pl.ds(z, n), pl.ds(z - 1, n), pl.ds(z + 1, n)
+    def plane(z):
+        lane = lax.broadcasted_iota(jnp.int32, (FY, NX), 1)
+
+        def around(ref, v, other):
+            x = pltpu.roll(jnp.where(lane == NX - 1, other, v), 1, 1)
+            x = x + pltpu.roll(jnp.where(lane == 0, other, v), NX - 1, 1)
+            y = ref[rows_of(z, 1, -1)] + ref[rows_of(z, 1, 1)]
+            return (y + (ref[rows_of(z, 1, -FY)] + ref[rows_of(z, 1, FY)])) + x
+
+        here = rows_of(z, 1)
         v0, v1 = s0[here], s1[here]
-        a0, a1 = pltpu.roll(v0, 1, 2), pltpu.roll(v1, 1, 2)
-        b0, b1 = pltpu.roll(v0, NX - 1, 2), pltpu.roll(v1, NX - 1, 2)
-        t0 = jnp.where(lane == 0, a1, a0) + jnp.where(lane == NX - 1, b1, b0)
-        t1 = jnp.where(lane == 0, a0, a1) + jnp.where(lane == NX - 1, b0, b1)
-        t0 = t0 + (pltpu.roll(v0, 1, 1) + pltpu.roll(v0, FY - 1, 1)) + (s0[below] + s0[above])
-        t1 = t1 + (pltpu.roll(v1, 1, 1) + pltpu.roll(v1, FY - 1, 1)) + (s1[below] + s1[above])
-        r0 = c0[here] * v0 - m0[here] * t0
-        r1 = c1[here] * v1 - m1[here] * t1
+        r0 = c0[here] * v0 - m0[here] * around(s0, v0, v1)
+        r1 = c1[here] * v1 - m1[here] * around(s1, v1, v0)
         if finish is None:
             dst[0][here] = r0
             dst[1][here] = r1
         else:
-            finish(z, n, r0, r1)
+            finish(z, 1, r0, r1)
+
+    def planes(z, n):
+        for k in range(n):
+            plane(z + k)
 
     count = last - first
     whole = count // PLANES
@@ -190,6 +209,10 @@
         planes(first + whole * PLANES, count % PLANES)
 
 
+def block_of(v, n):
+    return v.reshape(n, FY, NX)[:, G : G + NY]
+
+
 def span(radius):
     return G - radius, G + NZ + radius
 
@@ -197,16 +220,17 @@
 def first_stage(xe, be, ke, lo, hi, r_out, w_out, wdn, wup, c0, c1, m0, m1, x1, b1, p0, p1, q0, q1):
     def put(ref):
         def write(z, v):
-            ref[z] = v
+            ref[z * FY : (z + 1) * FY] = v
 
         return write
 
     def put_coef(z, k1):
-        k0 = ke[z]
-        c0[z] = 6.0 + k0
-        c1[z] = 6.0 + k1
-        m0[z] = jnp.where(k0 > 0.0, 1.0, 0.0)
-        m1[z] = jnp.where(k1 > 0.0, 1.0, 0.0)
+        at = slice(z * FY, (z + 1) * FY)
+        k0 = ke[at]
+        c0[at] = 6.0 + k0
+        c1[at] = 6.0 + k1
+        m0[at] = jnp.where(k0 > 0.0, 1.0, 0.0)
+        m1[at] = jnp.where(k1 > 0.0, 1.0, 0.0)
 
     unpack_lanes(lo, hi, 0, put(x1))
     unpack_lanes(lo, hi, Q_PACK, put(b1))
@@ -216,7 +240,7 @@
     apply_k((xe, x1), p, coef, mask, *span(5))
 
     def to_residual(z, n, v0, v1):
-        at = pl.ds(z, n)
+        at = rows_of(z, n)
         be[at] = be[at] - v0 * (1.0 / SQ)
         b1[at] = b1[at] - v1 * (1.0 / SQ)
 
@@ -226,11 +250,11 @@
     apply_k(q, p, coef, mask, *span(1))
 
     def to_precond(z, n, v0, v1):
-        at = pl.ds(z, n)
+        at = rows_of(z, n)
         r = be[at]
         w = C0 * r + (C1 / SQ) * q0[at] + (C2 / SQ**2) * v0
-        w_out[pl.ds(z - G, n)] = w[:, G : G + NY, :]
-        r_out[pl.ds(z - G, n)] = r[:, G : G + NY, :]
+        w_out[pl.ds(z - G, n)] = block_of(w, n)
+        r_out[pl.ds(z - G, n)] = block_of(r, n)
 
     apply_k(p, None, coef, mask, *span(0), finish=to_precond)
     wdn[...] = w_out[0:G]
@@ -238,26 +262,40 @@
 
 
 def pack_y2(w_ref, lo_ref, hi_ref, dn_ref, up_ref):
-    dn_ref[0:G] = lo_ref[:, 0:G, :]
-    up_ref[0:G] = lo_ref[:, NY - G : NY, :]
-    dn_ref[G : G + NZ] = w_ref[:, 0:G, :]
-    up_ref[G : G + NZ] = w_ref[:, NY - G : NY, :]
-    dn_ref[G + NZ : FZ] = hi_ref[:, 0:G, :]
-    up_ref[G + NZ : FZ] = hi_ref[:, NY - G : NY, :]
+    for t in range(1, G + 1):
+        n = G - t
+        for out, row in ((dn_ref, t - 1), (up_ref, NY - t)):
+            out[(t - 1) * NZ : t * NZ, :] = w_ref[pl.ds(row, NZ, stride=NY), :]
+            if n:
+                at = MAIN_ROWS2 + CORNERS2[0, t, 0]
+                out[at : at + n, :] = lo_ref[pl.ds(t * NY + row, n, stride=NY), :]
+                at = MAIN_ROWS2 + CORNERS2[0, t, 1]
+                out[at : at + n, :] = hi_ref[pl.ds(row, n, stride=NY), :]
 
 
 def frame2(w_ref, zlo, zhi, ylo, yhi, we, dn_ref, up_ref):
-    we[0:G, G : G + NY, :] = zlo[...]
-    we[G : G + NZ, G : G + NY, :] = w_ref[...]
-    we[G + NZ : FZ, G : G + NY, :] = zhi[...]
-    we[:, 0:G, :] = ylo[...]
-    we[:, G + NY : FY, :] = yhi[...]
-    pack_lanes(lambda z: we[z], dn_ref, up_ref, 0)
+    for z in range(FZ):
+        at = z * FY
+        src, k = (zlo, z) if z < G else (w_ref, z - G) if z < G + NZ else (zhi, z - G - NZ)
+        we[at + G : at + G + NY, :] = src[k * NY : (k + 1) * NY, :]
+        if z < G or z >= G + NZ:
+            we[at : at + G, :] = jnp.zeros((G, NX), f32)
+            we[at + G + NY : at + FY, :] = jnp.zeros((G, NX), f32)
+    for t in range(1, G + 1):
+        n = G - t
+        for src, row in ((ylo, G - t), (yhi, G + NY + t - 1)):
+            we[pl.ds(G * FY + row, NZ, stride=FY), :] = src[(t - 1) * NZ : t * NZ, :]
+            if n:
+                at = MAIN_ROWS2 + CORNERS2[0, t, 0]
+                we[pl.ds((G - n) * FY + row, n, stride=FY), :] = src[at : at + n, :]
+                at = MAIN_ROWS2 + CORNERS2[0, t, 1]
+                we[pl.ds((G + NZ) * FY + row, n, stride=FY), :] = src[at : at + n, :]
+    pack_lanes(lambda z: we[z * FY : (z + 1) * FY, :], dn_ref, up_ref, 0)
 
 
 def second_stage(we, lo, hi, r_ref, c0, c1, m0, m1, v1_out, v2_out, v3_out, dots, acc, w1, p0, p1, q0, q1, s0, s1):
     def write(z, v):
-        w1[z] = v
+        w1[z * FY : (z + 1) * FY] = v
 
     unpack_lanes(lo, hi, 0, write)
     coef, mask, p, q, s = (c0, c1), (m0, m1), (p0, p1), (q0, q1), (s0, s1)
@@ -268,7 +306,7 @@
     apply_k(s, p, coef, mask, *span(3))
 
     def to_w2(z, n, a0, a1):
-        at = pl.ds(z, n)
+        at = rows_of(z, n)
         s0[at] = C0 * q0[at] + (C1 / SQ) * s0[at] + (C2 / SQ**2) * a0
         s1[at] = C0 * q1[at] + (C1 / SQ) * s1[at] + (C2 / SQ**2) * a1
 
@@ -277,12 +315,8 @@
     acc[...] = jnp.zeros((4, G, NX), f32)
 
     def to_w3(z, n, a0, a1):
-        at, to = pl.ds(z, n), pl.ds(z - G, n)
-        rows = slice(G, G + NY)
-        w = we[at][:, rows]
-        u1 = q0[at][:, rows]
-        u2 = s0[at][:, rows]
-        u3 = a0[:, rows]
+        at, to = rows_of(z, n), pl.ds(z - G, n)
+        w, u1, u2, u3 = (block_of(v, n) for v in (we[at], q0[at], s0[at], a0))
         v1_out[to] = u1
         v2_out[to] = u2
         v3_out[to] = u3
@@ -322,20 +356,19 @@
 
 
 def body(right_side, initial, kappa_sq):
-    fields = (initial, right_side, kappa_sq)
-    flat = [v.reshape(NZ * NY, NX) for v in fields]
-    down = jnp.concatenate([v[:d] for v, d in zip(fields, DEPTHS)], axis=0)
-    up = jnp.concatenate([v[NZ - d :] for v, d in zip(fields, DEPTHS)], axis=0)
-    zlo, zhi = exchange(down, up, "gz")
-    zlo, zhi = zlo.reshape(LAYERS * NY, NX), zhi.reshape(LAYERS * NY, NX)
-    down, up = run(pack_y, [(PACK_ROWS, NX)] * 2, (*flat, zlo, zhi), name="pack_y")
-    ylo, yhi = exchange(down, up, "gy")
-    frame_shape = (FZ, FY, NX)
+    flat = [v.reshape(NZ * NY, NX) for v in (initial, right_side, kappa_sq)]
+    zdn, zup, ydn, yup = run(
+        pack_block, [(LAYERS * NY, NX)] * 2 + [(MAIN_ROWS, NX)] * 2, flat, name="pack_block"
+    )
+    ylo, yhi = exchange(ydn, yup, "gy")
+    zlo, zhi = exchange(zdn, zup, "gz")
+    down, up = run(pack_corners, [(CORNER_ROWS, NX)] * 2, (zlo, zhi), name="pack_corners")
+    clo, chi = exchange(down, up, "gy")
+    frame_shape = (FZ * FY, NX)
     xe, be, ke, down, up = run(
-        frame, [(FZ * FY, NX)] * 3 + [(3 * Q_PACK, NX)] * 2, (*flat, zlo, zhi, ylo, yhi), name="frame"
+        frame, [frame_shape] * 3 + [(3 * Q_PACK, NX)] * 2, (*flat, zlo, zhi, ylo, yhi, clo, chi), name="frame"
     )
     xlo, xhi = exchange(down, up, "gx")
-    xe, be, ke = (v.reshape(frame_shape) for v in (xe, be, ke))
     tile = pltpu.VMEM(frame_shape, f32)
     block = (NZ, NY, NX)
     slab = (G, NY, NX)
@@ -353,9 +386,10 @@
         name="first_stage",
     )
     zlo, zhi = exchange(down, up, "gz")
-    down, up = run(pack_y2, [(FZ, G, NX)] * 2, (w0, zlo, zhi), name="pack_y2")
+    w_flat, zlo, zhi = (v.reshape(-1, NX) for v in (w0, zlo, zhi))
+    down, up = run(pack_y2, [(MAIN_ROWS2 + CORNER_ROWS2, NX)] * 2, (w_flat, zlo, zhi), name="pack_y2")
     ylo, yhi = exchange(down, up, "gy")
-    we, down, up = run(frame2, [frame_shape, (Q_PACK, NX), (Q_PACK, NX)], (w0, zlo, zhi, ylo, yhi), name="frame2")
+    we, down, up = run(frame2, [frame_shape, (Q_PACK, NX), (Q_PACK, NX)], (w_flat, zlo, zhi, ylo, yhi), name="frame2")
     xlo, xhi = exchange(down, up, "gx")
     v1, v2, v3, dots = run(
         second_stage,

time: 166 us -> 157 us (0.946)
  waiting for transfers between devices: 63.7 us -> 38.5 us
  starting transfers between devices: 39.7 us -> 59.1 us
  Pallas kernels: 25.9 us -> 18.9 us
  blocking collectives: 31.9 us -> 34 us
    ppermute x12 -> x14, waiting for transfers between devices: 63.7 us -> 38.5 us  [shift(): return lax.ppermute(x, axis, pairs)]
    ppermute x12 -> x14, starting transfers between devices: 39.7 us -> 59.1 us  [shift(): return lax.ppermute(x, axis, pairs)]
    pallas_call x7 -> x8, Pallas kernels: 25.9 us -> 18.9 us  [run(): pl.pallas_call(kernel, out_shape=[jax.ShapeDtypeStruct(s, f32) for s in o...]
    unnamed x6 -> x10, local copies, waits for them, and re-layouts: 0.02 us -> 2.85 us
    slice x3 -> x0, local copies, waits for them, and re-layouts: 1.66 us -> none  [body(): down = jnp.concatenate([v[:d] for v, d in zip(fields, DEPTHS)], axis=0)]
  transfers between devices with their start and end apart: 12 -> 14, of which waited for: 10 -> 9; matrix products, arithmetic and copies ran while one was open for 0% -> 0% of each run, Pallas kernels for 0% -> 0%
where the time goes in v3:
time: 157 us; the launch traced here: 154 us
  starting transfers between devices  59.1 us (38%)
  waiting for transfers between devices  38.5 us (25%)
  blocking collectives  34 us (22%)
  Pallas kernels  18.9 us (12%)
  local copies, waits for them, and re-layouts  2.87 us (2%)
    ppermute x14, starting transfers between devices, shift(): return lax.ppermute(x, axis, pairs)  59.1 us
    ppermute x14, waiting for transfers between devices, shift(): return lax.ppermute(x, axis, pairs)  38.5 us
    all_to_all x2, blocking collectives, all_sum(): x = jnp.sum(lax.all_to_all(copies, axis, 0, 0), axis=0)  22.1 us
    pallas_call x8, Pallas kernels, run(): pl.pallas_call(kernel, out_shape=[jax.ShapeDtypeStruct(s, f32) for s in o...  18.9 us
    psum x1, blocking collectives, all_sum(): return lax.psum(x, 'gz')  11.9 us
  transfers between devices with their start and end apart: 14, of which 9 were waited for; matrix products, arithmetic and copies ran while one was open for 0% of the time, Pallas kernels for 0%

profile of v3, /device:TPU:1, one launch (start us, length us, event | category | flops | bytes accessed | tf_op | source)
XLA Modules:
  0.0 154.2 jit_solution(1676115737273388986)
XLA Ops:
  0.6 0.0 copy-start
  0.6 0.9 copy-done
  1.6 0.0 copy-start.2
  1.6 0.9 copy-done.2
  2.5 0.0 copy-start.4
  2.5 0.9 copy-done.4
  3.5 0.0 copy-start.3
  3.5 0.2 pack_block.1
  3.7 0.0 copy-start.1
  3.7 4.5 %collective-permute-start.2 = (f32[544,128]{1,0:T(8,128)S(1)}, f32[544,128]{1,0:T(8,128)S(1)}, u32[]{:S(2)}, u32[]{:S(2)}) collective-permute-start(f32[544,128]{1,0:T(8,128)S(1)} %get-tuple-element.32), channel_id=1, source_target_pairs={{0,4},{4,8},{8,12},{12,16},{16,20},{20,24},{24,28},{28,32},{32,36}... | collective-permute-start | bytes 835592 | tf_op jit(solution)/shard_map/ppermute | solution.py:81
  8.2 1.3 collective-permute-start.3
  9.5 8.8 %collective-permute-start = (f32[272,128]{1,0:T(8,128)S(1)}, f32[272,128]{1,0:T(8,128)S(1)}, u32[]{:S(2)}, u32[]{:S(2)}) collective-permute-start(f32[272,128]{1,0:T(8,128)S(1)} %get-tuple-element.30), channel_id=1, source_target_pairs={{0,1},{1,2},{2,3},{4,5},{5,6},{6,7},{8,9},{9,10},{10,11},{12,13},{... | collective-permute-start | bytes 417800 | tf_op jit(solution)/shard_map/ppermute | solution.py:81
  18.3 1.3 collective-permute-start.1
  19.6 0.7 collective-permute-done.lo_ref.zlo
  20.3 8.7 %collective-permute-done.1.hi_ref.zhi = f32[272,128]{1,0:T(8,128)S(1)} collective-permute-done((f32[272,128]{1,0:T(8,128)S(1)}, f32[272,128]{1,0:T(8,128)S(1)}, u32[]{:S(2)}, u32[]{:S(2)}) %collective-permute-start.1) | collective-permute-done | bytes 139296 | tf_op jit(solution)/shard_map/ppermute | solution.py:81
  29.1 15.7 %collective-permute-start.4 = (f32[88,128]{1,0:T(8,128)S(1)}, f32[88,128]{1,0:T(8,128)S(1)}, u32[]{:S(2)}, u32[]{:S(2)}) collective-permute-start(f32[88,128]{1,0:T(8,128)S(1)} %get-tuple-element.34), channel_id=1, source_target_pairs={{0,4},{4,8},{8,12},{12,16},{16,20},{20,24},{24,28},{28,32},{32,36}... | collective-permute-start | bytes 135176 | tf_op jit(solution)/shard_map/ppermute | solution.py:81
  44.8 1.3 collective-permute-start.5
  46.1 0.0 collective-permute-done.4.clo
  46.1 3.5 %collective-permute-done.5.chi = f32[88,128]{1,0:T(8,128)S(1)} collective-permute-done((f32[88,128]{1,0:T(8,128)S(1)}, f32[88,128]{1,0:T(8,128)S(1)}, u32[]{:S(2)}, u32[]{:S(2)}) %collective-permute-start.5) | collective-permute-done | bytes 45088 | tf_op jit(solution)/shard_map/ppermute | solution.py:81
  49.6 0.0 collective-permute-done.2.ylo
  49.6 0.0 collective-permute-done.3.yhi
  49.6 0.0 copy-done.3
  49.6 0.0 copy-done.1
  49.6 1.4 frame.1
  51.0 5.5 %collective-permute-start.6 = (f32[288,128]{1,0:T(8,128)S(1)}, f32[288,128]{1,0:T(8,128)S(1)}, u32[]{:S(2)}, u32[]{:S(2)}) collective-permute-start(f32[288,128]{1,0:T(8,128)S(1)} %get-tuple-element.39), channel_id=1, source_target_pairs={{0,64},{64,128},{128,192},{192,256},{256,320},{320,384},{384,448},... | collective-permute-start | bytes 442376 | tf_op jit(solution)/shard_map/ppermute | solution.py:81
  56.5 1.9 %collective-permute-start.7 = (f32[288,128]{1,0:T(8,128)S(1)}, f32[288,128]{1,0:T(8,128)S(1)}, u32[]{:S(2)}, u32[]{:S(2)}) collective-permute-start(f32[288,128]{1,0:T(8,128)S(1)} %get-tuple-element.40), channel_id=1, source_target_pairs={{64,0},{128,64},{192,128},{256,192},{320,256},{384,320},{448,384},... | collective-permute-start | bytes 442376 | tf_op jit(solution)/shard_map/ppermute | solution.py:81
  58.4 0.2 collective-permute-done.6.rest_1_
  58.6 4.4 %collective-permute-done.7.rest_2_ = f32[288,128]{1,0:T(8,128)S(1)} collective-permute-done((f32[288,128]{1,0:T(8,128)S(1)}, f32[288,128]{1,0:T(8,128)S(1)}, u32[]{:S(2)}, u32[]{:S(2)}) %collective-permute-start.7) | collective-permute-done | bytes 147488 | tf_op jit(solution)/shard_map/ppermute | solution.py:81
  62.9 7.0 %first_stage.1 = (f32[32,16,128]{2,1,0:T(8,128)S(1)}, f32[32,16,128]{2,1,0:T(8,128)S(1)}, f32[8,16,128]{2,1,0:T(8,128)S(1)}, f32[8,16,128]{2,1,0:T(8,128)S(1)}, ...) custom-call(f32[1536,128]{1,0:T(8,128)S(1)} %get-tuple-element.36.xe, ...), custom_call_target="tpu_custom_call" | custom-call | tf_op jit(solution)/shard_map/first_stage/pallas_call | solution.py:67
  69.9 6.9 %collective-permute-start.8 = (f32[8,16,128]{2,1,0:T(8,128)S(1)}, f32[8,16,128]{2,1,0:T(8,128)S(1)}, u32[]{:S(2)}, u32[]{:S(2)}) collective-permute-start(f32[8,16,128]{2,1,0:T(8,128)S(1)} %get-tuple-element.43), channel_id=1, source_target_pairs={{0,1},{1,2},{2,3},{4,5},{5,6},{6,7},{8,9},{9,10},{10,11},{12,13},{... | collective-permute-start | bytes 196616 | tf_op jit(solution)/shard_map/ppermute | solution.py:81
  76.8 1.3 collective-permute-start.9
  78.1 0.0 collective-permute-done.8
  78.1 8.0 %collective-permute-done.9 = f32[8,16,128]{2,1,0:T(8,128)S(1)} collective-permute-done((f32[8,16,128]{2,1,0:T(8,128)S(1)}, f32[8,16,128]{2,1,0:T(8,128)S(1)}, u32[]{:S(2)}, u32[]{:S(2)}) %collective-permute-start.9) | collective-permute-done | bytes 65568 | tf_op jit(solution)/shard_map/ppermute | solution.py:81
  86.1 0.1 pack_y2.1
  86.3 3.1 %collective-permute-start.10 = (f32[312,128]{1,0:T(8,128)S(1)}, f32[312,128]{1,0:T(8,128)S(1)}, u32[]{:S(2)}, u32[]{:S(2)}) collective-permute-start(f32[312,128]{1,0:T(8,128)S(1)} %get-tuple-element.45), channel_id=1, source_target_pairs={{0,4},{4,8},{8,12},{12,16},{16,20},{20,24},{24,28},{28,32},{32,36}... | collective-permute-start | bytes 479240 | tf_op jit(solution)/shard_map/ppermute | solution.py:81
  89.3 1.3 collective-permute-start.11
  90.6 0.9 collective-permute-done.10.ylo
  91.5 8.7 %collective-permute-done.11.yhi = f32[312,128]{1,0:T(8,128)S(1)} collective-permute-done((f32[312,128]{1,0:T(8,128)S(1)}, f32[312,128]{1,0:T(8,128)S(1)}, u32[]{:S(2)}, u32[]{:S(2)}) %collective-permute-start.11) | collective-permute-done | bytes 159776 | tf_op jit(solution)/shard_map/ppermute | solution.py:81
  100.2 0.6 frame2.1
  100.8 4.3 %collective-permute-start.12 = (f32[96,128]{1,0:T(8,128)S(1)}, f32[96,128]{1,0:T(8,128)S(1)}, u32[]{:S(2)}, u32[]{:S(2)}) collective-permute-start(f32[96,128]{1,0:T(8,128)S(1)} %get-tuple-element.48), channel_id=1, source_target_pairs={{0,64},{64,128},{128,192},{192,256},{256,320},{320,384},{384,448},... | collective-permute-start | bytes 147464 | tf_op jit(solution)/shard_map/ppermute | solution.py:81
  105.1 1.9 %collective-permute-start.13 = (f32[96,128]{1,0:T(8,128)S(1)}, f32[96,128]{1,0:T(8,128)S(1)}, u32[]{:S(2)}, u32[]{:S(2)}) collective-permute-start(f32[96,128]{1,0:T(8,128)S(1)} %get-tuple-element.49), channel_id=1, source_target_pairs={{64,0},{128,64},{192,128},{256,192},{320,256},{384,320},{448,384},... | collective-permute-start | bytes 147464 | tf_op jit(solution)/shard_map/ppermute | solution.py:81
  107.0 0.0 collective-permute-done.12.lo
  107.0 3.5 %collective-permute-done.13.hi = f32[96,128]{1,0:T(8,128)S(1)} collective-permute-done((f32[96,128]{1,0:T(8,128)S(1)}, f32[96,128]{1,0:T(8,128)S(1)}, u32[]{:S(2)}, u32[]{:S(2)}) %collective-permute-start.13) | collective-permute-done | bytes 49184 | tf_op jit(solution)/shard_map/ppermute | solution.py:81
  110.5 8.7 %second_stage.1 = (f32[32,16,128]{2,1,0:T(8,128)S(1)}, f32[32,16,128]{2,1,0:T(8,128)S(1)}, f32[32,16,128]{2,1,0:T(8,128)S(1)}, f32[8,128]{1,0:T(8,128)S(1)}) custom-call(f32[1536,128]{1,0:T(8,128)S(1)} %get-tuple-element.47.we, f32[96,128]{1,0:T(8,128)S(1)} %collective-permute-done.12.lo, f32[96,128]{1,0:T(8,128)S(1)} %collective-permute-done.13.hi, ...), custom_call_target="tpu_custom_call" | custom-call | tf_op jit(solution)/shard_map/second_stage/pallas_call | solution.py:67
  119.2 7.8 %all_to_all.10 = f32[8,8,128]{2,1,0:T(8,128)S(1)} all-to-all(f32[8,8,128]{2,1,0:T(8,128)S(1)} %broadcast_in_dim.4), channel_id=1, replica_groups=mesh['gx'=8,'gy'=16,'gz'=4] {'gx'}, dimensions={0} | all-to-all | bytes 65536 | tf_op jit(solution)/shard_map/all_to_all | solution.py:354
  127.0 14.3 %all_to_all.11 = f32[16,8,128]{2,1,0:T(8,128)S(1)} all-to-all(f32[16,8,128]{2,1,0:T(8,128)S(1)} %broadcast_in_dim.5), channel_id=1, replica_groups=mesh['gx'=8,'gy'=16,'gz'=4] {'gy'}, dimensions={0} | all-to-all | bytes 131072 | tf_op jit(solution)/shard_map/all_to_all | solution.py:354
  141.3 11.9 %psum.7.dots = f32[8,128]{1,0:T(8,128)S(1)} all-reduce(f32[8,128]{1,0:T(8,128)S(1)} %reduce_sum.19), channel_id=1, replica_groups=mesh['gx'=8,'gy'=16,'gz'=4] {'gz'}, use_global_device_ids=true, to_apply=%region_2.0 | all-reduce | flops 1024 | bytes 8192 | tf_op jit(solution)/shard_map/psum | solution.py:355
  153.2 1.0 finish.1
  (5 shorter events, 0.1 us)
Async XLA Ops:
  0.6 1.0 copy-start
  1.6 0.9 copy-start.2
  2.5 0.9 copy-start.4
  3.5 46.1 %copy-start.3 = (f32[32,16,128]{2,1,0:T(8,128)S(1)}, f32[32,16,128]{2,1,0:T(8,128)}, u32[]{:S(2)}) copy-start(f32[32,16,128]{2,1,0:T(8,128)} %param.3) | copy-start | bytes 786436
  3.7 45.9 %copy-start.1 = (f32[32,16,128]{2,1,0:T(8,128)S(1)}, f32[32,16,128]{2,1,0:T(8,128)}, u32[]{:S(2)}) copy-start(f32[32,16,128]{2,1,0:T(8,128)} %x_ref.1) | copy-start | bytes 786436
  3.7 45.9 %collective-permute-start.2 = (f32[544,128]{1,0:T(8,128)S(1)}, f32[544,128]{1,0:T(8,128)S(1)}, u32[]{:S(2)}, u32[]{:S(2)}) collective-permute-start(f32[544,128]{1,0:T(8,128)S(1)} %get-tuple-element.32), channel_id=1, source_target_pairs={{0,4},{4,8},{8,12},{12,16},{16,20},{20,24},{24,28},{28,32},{32,36}... | collective-permute-start | bytes 835592 | tf_op jit(solution)/shard_map/ppermute | solution.py:81
  8.2 41.4 %collective-permute-start.3 = (f32[544,128]{1,0:T(8,128)S(1)}, f32[544,128]{1,0:T(8,128)S(1)}, u32[]{:S(2)}, u32[]{:S(2)}) collective-permute-start(f32[544,128]{1,0:T(8,128)S(1)} %get-tuple-element.33), channel_id=1, source_target_pairs={{4,0},{8,4},{12,8},{16,12},{20,16},{24,20},{28,24},{32,28},{36,32}... | collective-permute-start | bytes 835592 | tf_op jit(solution)/shard_map/ppermute | solution.py:81
  9.5 10.8 %collective-permute-start = (f32[272,128]{1,0:T(8,128)S(1)}, f32[272,128]{1,0:T(8,128)S(1)}, u32[]{:S(2)}, u32[]{:S(2)}) collective-permute-start(f32[272,128]{1,0:T(8,128)S(1)} %get-tuple-element.30), channel_id=1, source_target_pairs={{0,1},{1,2},{2,3},{4,5},{5,6},{6,7},{8,9},{9,10},{10,11},{12,13},{... | collective-permute-start | bytes 417800 | tf_op jit(solution)/shard_map/ppermute | solution.py:81
  18.3 10.7 %collective-permute-start.1 = (f32[272,128]{1,0:T(8,128)S(1)}, f32[272,128]{1,0:T(8,128)S(1)}, u32[]{:S(2)}, u32[]{:S(2)}) collective-permute-start(f32[272,128]{1,0:T(8,128)S(1)} %get-tuple-element.31), channel_id=1, source_target_pairs={{1,0},{2,1},{3,2},{5,4},{6,5},{7,6},{9,8},{10,9},{11,10},{13,12},{... | collective-permute-start | bytes 417800 | tf_op jit(solution)/shard_map/ppermute | solution.py:81
  29.1 17.0 %collective-permute-start.4 = (f32[88,128]{1,0:T(8,128)S(1)}, f32[88,128]{1,0:T(8,128)S(1)}, u32[]{:S(2)}, u32[]{:S(2)}) collective-permute-start(f32[88,128]{1,0:T(8,128)S(1)} %get-tuple-element.34), channel_id=1, source_target_pairs={{0,4},{4,8},{8,12},{12,16},{16,20},{20,24},{24,28},{28,32},{32,36}... | collective-permute-start | bytes 135176 | tf_op jit(solution)/shard_map/ppermute | solution.py:81
  44.8 4.8 %collective-permute-start.5 = (f32[88,128]{1,0:T(8,128)S(1)}, f32[88,128]{1,0:T(8,128)S(1)}, u32[]{:S(2)}, u32[]{:S(2)}) collective-permute-start(f32[88,128]{1,0:T(8,128)S(1)} %get-tuple-element.35), channel_id=1, source_target_pairs={{4,0},{8,4},{12,8},{16,12},{20,16},{24,20},{28,24},{32,28},{36,32}... | collective-permute-start | bytes 135176 | tf_op jit(solution)/shard_map/ppermute | solution.py:81
  51.0 7.6 %collective-permute-start.6 = (f32[288,128]{1,0:T(8,128)S(1)}, f32[288,128]{1,0:T(8,128)S(1)}, u32[]{:S(2)}, u32[]{:S(2)}) collective-permute-start(f32[288,128]{1,0:T(8,128)S(1)} %get-tuple-element.39), channel_id=1, source_target_pairs={{0,64},{64,128},{128,192},{192,256},{256,320},{320,384},{384,448},... | collective-permute-start | bytes 442376 | tf_op jit(solution)/shard_map/ppermute | solution.py:81
  56.5 6.5 %collective-permute-start.7 = (f32[288,128]{1,0:T(8,128)S(1)}, f32[288,128]{1,0:T(8,128)S(1)}, u32[]{:S(2)}, u32[]{:S(2)}) collective-permute-start(f32[288,128]{1,0:T(8,128)S(1)} %get-tuple-element.40), channel_id=1, source_target_pairs={{64,0},{128,64},{192,128},{256,192},{320,256},{384,320},{448,384},... | collective-permute-start | bytes 442376 | tf_op jit(solution)/shard_map/ppermute | solution.py:81
  69.9 8.2 %collective-permute-start.8 = (f32[8,16,128]{2,1,0:T(8,128)S(1)}, f32[8,16,128]{2,1,0:T(8,128)S(1)}, u32[]{:S(2)}, u32[]{:S(2)}) collective-permute-start(f32[8,16,128]{2,1,0:T(8,128)S(1)} %get-tuple-element.43), channel_id=1, source_target_pairs={{0,1},{1,2},{2,3},{4,5},{5,6},{6,7},{8,9},{9,10},{10,11},{12,13},{... | collective-permute-start | bytes 196616 | tf_op jit(solution)/shard_map/ppermute | solution.py:81
  76.8 9.3 %collective-permute-start.9 = (f32[8,16,128]{2,1,0:T(8,128)S(1)}, f32[8,16,128]{2,1,0:T(8,128)S(1)}, u32[]{:S(2)}, u32[]{:S(2)}) collective-permute-start(f32[8,16,128]{2,1,0:T(8,128)S(1)} %get-tuple-element.44), channel_id=1, source_target_pairs={{1,0},{2,1},{3,2},{5,4},{6,5},{7,6},{9,8},{10,9},{11,10},{13,12},{... | collective-permute-start | bytes 196616 | tf_op jit(solution)/shard_map/ppermute | solution.py:81
  86.3 5.3 %collective-permute-start.10 = (f32[312,128]{1,0:T(8,128)S(1)}, f32[312,128]{1,0:T(8,128)S(1)}, u32[]{:S(2)}, u32[]{:S(2)}) collective-permute-start(f32[312,128]{1,0:T(8,128)S(1)} %get-tuple-element.45), channel_id=1, source_target_pairs={{0,4},{4,8},{8,12},{12,16},{16,20},{20,24},{24,28},{28,32},{32,36}... | collective-permute-start | bytes 479240 | tf_op jit(solution)/shard_map/ppermute | solution.py:81
  89.3 10.9 %collective-permute-start.11 = (f32[312,128]{1,0:T(8,128)S(1)}, f32[312,128]{1,0:T(8,128)S(1)}, u32[]{:S(2)}, u32[]{:S(2)}) collective-permute-start(f32[312,128]{1,0:T(8,128)S(1)} %get-tuple-element.46), channel_id=1, source_target_pairs={{4,0},{8,4},{12,8},{16,12},{20,16},{24,20},{28,24},{32,28},{36,32}... | collective-permute-start | bytes 479240 | tf_op jit(solution)/shard_map/ppermute | solution.py:81
  100.8 6.2 %collective-permute-start.12 = (f32[96,128]{1,0:T(8,128)S(1)}, f32[96,128]{1,0:T(8,128)S(1)}, u32[]{:S(2)}, u32[]{:S(2)}) collective-permute-start(f32[96,128]{1,0:T(8,128)S(1)} %get-tuple-element.48), channel_id=1, source_target_pairs={{0,64},{64,128},{128,192},{192,256},{256,320},{320,384},{384,448},... | collective-permute-start | bytes 147464 | tf_op jit(solution)/shard_map/ppermute | solution.py:81
  105.1 5.4 %collective-permute-start.13 = (f32[96,128]{1,0:T(8,128)S(1)}, f32[96,128]{1,0:T(8,128)S(1)}, u32[]{:S(2)}, u32[]{:S(2)}) collective-permute-start(f32[96,128]{1,0:T(8,128)S(1)} %get-tuple-element.49), channel_id=1, source_target_pairs={{64,0},{128,64},{192,128},{256,192},{320,256},{384,320},{448,384},... | collective-permute-start | bytes 147464 | tf_op jit(solution)/shard_map/ppermute | solution.py:81

commit v4 on v3

--- a/solution.py
+++ b/solution.py
@@ -63,15 +63,14 @@
 VM = pl.BlockSpec(memory_space=pltpu.VMEM)
 
 
-def run(kernel, outs, args, scratch=(), name=None, mib=16):
+def run(kernel, outs, args, scratch=(), mib=16, space=pltpu.VMEM):
     return pl.pallas_call(
         kernel,
         out_shape=[jax.ShapeDtypeStruct(s, f32) for s in outs],
-        in_specs=[VM] * len(args),
+        in_specs=[pl.BlockSpec(memory_space=space)] * len(args),
         out_specs=[VM] * len(outs),
         scratch_shapes=list(scratch),
         compiler_params=pltpu.CompilerParams(vmem_limit_bytes=mib << 20),
-        name=name,
     )(*args)
 
 
@@ -87,8 +86,16 @@
     return from_below, from_above
 
 
-def pack_block(x_ref, b_ref, k_ref, zdn, zup, ydn, yup):
+def pack_block(x_hbm, b_hbm, k_hbm, zdn, zup, ydn, yup, x_ref, b_ref, k_ref, sems):
     fields = (x_ref, b_ref, k_ref)
+    copies = [
+        pltpu.make_async_copy(src, dst, sems.at[i])
+        for i, (src, dst) in enumerate(zip((x_hbm, b_hbm, k_hbm), fields))
+    ]
+    for copy in copies:
+        copy.start()
+    for copy in copies:
+        copy.wait()
     for f, field in enumerate(fields):
         n = DEPTHS[f] * NY
         at = OFFS[f] * NY
@@ -355,19 +362,21 @@
     return lax.psum(x, "gz")
 
 
-def body(right_side, initial, kappa_sq):
+def solve(right_side, initial, kappa_sq):
     flat = [v.reshape(NZ * NY, NX) for v in (initial, right_side, kappa_sq)]
     zdn, zup, ydn, yup = run(
-        pack_block, [(LAYERS * NY, NX)] * 2 + [(MAIN_ROWS, NX)] * 2, flat, name="pack_block"
+        pack_block,
+        [(LAYERS * NY, NX)] * 2 + [(MAIN_ROWS, NX)] * 2,
+        [pltpu.with_memory_space_constraint(v, pltpu.HBM) for v in flat],
+        scratch=[pltpu.VMEM((NZ * NY, NX), f32)] * 3 + [pltpu.SemaphoreType.DMA((3,))],
+        space=pltpu.HBM,
     )
+    zlo, zhi = exchange(zdn, zup, "gz")
     ylo, yhi = exchange(ydn, yup, "gy")
-    zlo, zhi = exchange(zdn, zup, "gz")
-    down, up = run(pack_corners, [(CORNER_ROWS, NX)] * 2, (zlo, zhi), name="pack_corners")
+    down, up = run(pack_corners, [(CORNER_ROWS, NX)] * 2, (zlo, zhi))
     clo, chi = exchange(down, up, "gy")
     frame_shape = (FZ * FY, NX)
-    xe, be, ke, down, up = run(
-        frame, [frame_shape] * 3 + [(3 * Q_PACK, NX)] * 2, (*flat, zlo, zhi, ylo, yhi, clo, chi), name="frame"
-    )
+    xe, be, ke, down, up = run(frame, [frame_shape] * 3 + [(3 * Q_PACK, NX)] * 2, (*flat, zlo, zhi, ylo, yhi, clo, chi))
     xlo, xhi = exchange(down, up, "gx")
     tile = pltpu.VMEM(frame_shape, f32)
     block = (NZ, NY, NX)
@@ -383,26 +392,24 @@
         [block, block, slab, slab, frame_shape, frame_shape, frame_shape, frame_shape],
         (xe, be, ke, xlo, xhi),
         scratch=[tile] * 7,
-        name="first_stage",
     )
     zlo, zhi = exchange(down, up, "gz")
     w_flat, zlo, zhi = (v.reshape(-1, NX) for v in (w0, zlo, zhi))
-    down, up = run(pack_y2, [(MAIN_ROWS2 + CORNER_ROWS2, NX)] * 2, (w_flat, zlo, zhi), name="pack_y2")
+    down, up = run(pack_y2, [(MAIN_ROWS2 + CORNER_ROWS2, NX)] * 2, (w_flat, zlo, zhi))
     ylo, yhi = exchange(down, up, "gy")
-    we, down, up = run(frame2, [frame_shape, (Q_PACK, NX), (Q_PACK, NX)], (w_flat, zlo, zhi, ylo, yhi), name="frame2")
+    we, down, up = run(frame2, [frame_shape, (Q_PACK, NX), (Q_PACK, NX)], (w_flat, zlo, zhi, ylo, yhi))
     xlo, xhi = exchange(down, up, "gx")
     v1, v2, v3, dots = run(
         second_stage,
         [block, block, block, (G, NX)],
         (we, xlo, xhi, r0, c0, c1, m0, m1),
         scratch=[pltpu.VMEM((4, G, NX), f32)] + [tile] * 7,
-        name="second_stage",
     )
     dots = all_sum(dots)
-    x, r = run(finish, [block, block], (initial, r0, w0, v1, v2, v3, dots), name="finish")
+    x, r = run(finish, [block, block], (initial, r0, w0, v1, v2, v3, dots))
     return x, r
 
 
 def solution(mesh):
     spec = P("gz", "gy", "gx")
-    return jax.shard_map(body, mesh=mesh, in_specs=(spec,) * 3, out_specs=(spec,) * 2, check_vma=False)
+    return jax.shard_map(solve, mesh=mesh, in_specs=(spec,) * 3, out_specs=(spec,) * 2, check_vma=False)

time: 157 us -> 155 us (0.987)
  local copies, waits for them, and re-layouts: 2.87 us -> 0.03 us
    unnamed x10 -> x6, local copies, waits for them, and re-layouts: 2.85 us -> 0.01 us
where the time goes in v4:
time: 155 us; the launch traced here: 153 us
  starting transfers between devices  59.1 us (38%)
  waiting for transfers between devices  38.5 us (25%)
  blocking collectives  34 us (22%)
  Pallas kernels  20.1 us (13%)
    ppermute x14, starting transfers between devices, shift(): return lax.ppermute(x, axis, pairs)  59.1 us
    ppermute x14, waiting for transfers between devices, shift(): return lax.ppermute(x, axis, pairs)  38.5 us
    all_to_all x2, blocking collectives, all_sum(): x = jnp.sum(lax.all_to_all(copies, axis, 0, 0), axis=0)  22.1 us
    pallas_call x8, Pallas kernels, run(): pl.pallas_call(kernel, out_shape=[jax.ShapeDtypeStruct(s, f32) for s in o...  20.1 us
    psum x1, blocking collectives, all_sum(): return lax.psum(x, 'gz')  11.9 us
  transfers between devices with their start and end apart: 14, of which 9 were waited for; matrix products, arithmetic and copies ran while one was open for 0% of the time, Pallas kernels for 0%

profile of v4, /device:TPU:1, one launch (start us, length us, event | category | flops | bytes accessed | tf_op | source)
XLA Modules:
  0.0 152.5 jit_solution(441625229186390132)
XLA Ops:
  0.6 0.0 copy-start.1
  0.6 0.0 copy-start.2
  0.6 1.4 shard_map.50
  2.0 0.0 copy-start
  2.1 4.5 %collective-permute-start.2 = (f32[544,128]{1,0:T(8,128)S(1)}, f32[544,128]{1,0:T(8,128)S(1)}, u32[]{:S(2)}, u32[]{:S(2)}) collective-permute-start(f32[544,128]{1,0:T(8,128)S(1)} %get-tuple-element.32), channel_id=1, source_target_pairs={{0,4},{4,8},{8,12},{12,16},{16,20},{20,24},{24,28},{28,32},{32,36}... | collective-permute-start | bytes 835592 | tf_op jit(solution)/shard_map/ppermute | solution.py:80
  6.6 1.3 collective-permute-start.3
  7.9 8.8 %collective-permute-start = (f32[272,128]{1,0:T(8,128)S(1)}, f32[272,128]{1,0:T(8,128)S(1)}, u32[]{:S(2)}, u32[]{:S(2)}) collective-permute-start(f32[272,128]{1,0:T(8,128)S(1)} %get-tuple-element.30), channel_id=1, source_target_pairs={{0,1},{1,2},{2,3},{4,5},{5,6},{6,7},{8,9},{9,10},{10,11},{12,13},{... | collective-permute-start | bytes 417800 | tf_op jit(solution)/shard_map/ppermute | solution.py:80
  16.7 1.3 collective-permute-start.1
  18.0 0.7 collective-permute-done.lo_ref.zlo
  18.7 8.7 %collective-permute-done.1.hi_ref.zhi = f32[272,128]{1,0:T(8,128)S(1)} collective-permute-done((f32[272,128]{1,0:T(8,128)S(1)}, f32[272,128]{1,0:T(8,128)S(1)}, u32[]{:S(2)}, u32[]{:S(2)}) %collective-permute-start.1) | collective-permute-done | bytes 139296 | tf_op jit(solution)/shard_map/ppermute | solution.py:80
  27.5 15.7 %collective-permute-start.4 = (f32[88,128]{1,0:T(8,128)S(1)}, f32[88,128]{1,0:T(8,128)S(1)}, u32[]{:S(2)}, u32[]{:S(2)}) collective-permute-start(f32[88,128]{1,0:T(8,128)S(1)} %get-tuple-element.34), channel_id=1, source_target_pairs={{0,4},{4,8},{8,12},{12,16},{16,20},{20,24},{24,28},{28,32},{32,36}... | collective-permute-start | bytes 135176 | tf_op jit(solution)/shard_map/ppermute | solution.py:80
  43.1 1.3 collective-permute-start.5
  44.4 0.0 collective-permute-done.4.clo
  44.5 3.5 %collective-permute-done.5.chi = f32[88,128]{1,0:T(8,128)S(1)} collective-permute-done((f32[88,128]{1,0:T(8,128)S(1)}, f32[88,128]{1,0:T(8,128)S(1)}, u32[]{:S(2)}, u32[]{:S(2)}) %collective-permute-start.5) | collective-permute-done | bytes 45088 | tf_op jit(solution)/shard_map/ppermute | solution.py:80
  47.9 0.0 collective-permute-done.2.ylo
  47.9 0.0 collective-permute-done.3.yhi
  47.9 0.0 copy-done.1
  47.9 0.0 copy-done.2
  48.0 0.0 copy-done
  48.0 1.4 shard_map.52
  49.4 5.5 %collective-permute-start.6 = (f32[288,128]{1,0:T(8,128)S(1)}, f32[288,128]{1,0:T(8,128)S(1)}, u32[]{:S(2)}, u32[]{:S(2)}) collective-permute-start(f32[288,128]{1,0:T(8,128)S(1)} %get-tuple-element.39), channel_id=1, source_target_pairs={{0,64},{64,128},{128,192},{192,256},{256,320},{320,384},{384,448},... | collective-permute-start | bytes 442376 | tf_op jit(solution)/shard_map/ppermute | solution.py:80
  54.9 1.9 %collective-permute-start.7 = (f32[288,128]{1,0:T(8,128)S(1)}, f32[288,128]{1,0:T(8,128)S(1)}, u32[]{:S(2)}, u32[]{:S(2)}) collective-permute-start(f32[288,128]{1,0:T(8,128)S(1)} %get-tuple-element.40), channel_id=1, source_target_pairs={{64,0},{128,64},{192,128},{256,192},{320,256},{384,320},{448,384},... | collective-permute-start | bytes 442376 | tf_op jit(solution)/shard_map/ppermute | solution.py:80
  56.8 0.2 collective-permute-done.6.rest_1_
  56.9 4.4 %collective-permute-done.7.rest_2_ = f32[288,128]{1,0:T(8,128)S(1)} collective-permute-done((f32[288,128]{1,0:T(8,128)S(1)}, f32[288,128]{1,0:T(8,128)S(1)}, u32[]{:S(2)}, u32[]{:S(2)}) %collective-permute-start.7) | collective-permute-done | bytes 147488 | tf_op jit(solution)/shard_map/ppermute | solution.py:80
  61.3 7.0 %shard_map.53 = (f32[32,16,128]{2,1,0:T(8,128)S(1)}, f32[32,16,128]{2,1,0:T(8,128)S(1)}, f32[8,16,128]{2,1,0:T(8,128)S(1)}, f32[8,16,128]{2,1,0:T(8,128)S(1)}, f...) custom-call(f32[1536,128]{1,0:T(8,128)S(1)} %get-tuple-element.36.xe, ...), custom_call_target="tpu_custom_call" | custom-call | tf_op jit(solution)/shard_map/pallas_call | solution.py:67
  68.3 6.9 %collective-permute-start.8 = (f32[8,16,128]{2,1,0:T(8,128)S(1)}, f32[8,16,128]{2,1,0:T(8,128)S(1)}, u32[]{:S(2)}, u32[]{:S(2)}) collective-permute-start(f32[8,16,128]{2,1,0:T(8,128)S(1)} %get-tuple-element.43), channel_id=1, source_target_pairs={{0,1},{1,2},{2,3},{4,5},{5,6},{6,7},{8,9},{9,10},{10,11},{12,13},{... | collective-permute-start | bytes 196616 | tf_op jit(solution)/shard_map/ppermute | solution.py:80
  75.2 1.3 collective-permute-start.9
  76.5 0.0 collective-permute-done.8
  76.5 8.0 %collective-permute-done.9 = f32[8,16,128]{2,1,0:T(8,128)S(1)} collective-permute-done((f32[8,16,128]{2,1,0:T(8,128)S(1)}, f32[8,16,128]{2,1,0:T(8,128)S(1)}, u32[]{:S(2)}, u32[]{:S(2)}) %collective-permute-start.9) | collective-permute-done | bytes 65568 | tf_op jit(solution)/shard_map/ppermute | solution.py:80
  84.5 0.1 shard_map.54
  84.6 3.1 %collective-permute-start.10 = (f32[312,128]{1,0:T(8,128)S(1)}, f32[312,128]{1,0:T(8,128)S(1)}, u32[]{:S(2)}, u32[]{:S(2)}) collective-permute-start(f32[312,128]{1,0:T(8,128)S(1)} %get-tuple-element.45), channel_id=1, source_target_pairs={{0,4},{4,8},{8,12},{12,16},{16,20},{20,24},{24,28},{28,32},{32,36}... | collective-permute-start | bytes 479240 | tf_op jit(solution)/shard_map/ppermute | solution.py:80
  87.7 1.3 collective-permute-start.11
  89.0 0.9 collective-permute-done.10.ylo
  89.9 8.7 %collective-permute-done.11.yhi = f32[312,128]{1,0:T(8,128)S(1)} collective-permute-done((f32[312,128]{1,0:T(8,128)S(1)}, f32[312,128]{1,0:T(8,128)S(1)}, u32[]{:S(2)}, u32[]{:S(2)}) %collective-permute-start.11) | collective-permute-done | bytes 159776 | tf_op jit(solution)/shard_map/ppermute | solution.py:80
  98.6 0.6 shard_map.55
  99.2 4.3 %collective-permute-start.12 = (f32[96,128]{1,0:T(8,128)S(1)}, f32[96,128]{1,0:T(8,128)S(1)}, u32[]{:S(2)}, u32[]{:S(2)}) collective-permute-start(f32[96,128]{1,0:T(8,128)S(1)} %get-tuple-element.48), channel_id=1, source_target_pairs={{0,64},{64,128},{128,192},{192,256},{256,320},{320,384},{384,448},... | collective-permute-start | bytes 147464 | tf_op jit(solution)/shard_map/ppermute | solution.py:80
  103.5 1.9 %collective-permute-start.13 = (f32[96,128]{1,0:T(8,128)S(1)}, f32[96,128]{1,0:T(8,128)S(1)}, u32[]{:S(2)}, u32[]{:S(2)}) collective-permute-start(f32[96,128]{1,0:T(8,128)S(1)} %get-tuple-element.49), channel_id=1, source_target_pairs={{64,0},{128,64},{192,128},{256,192},{320,256},{384,320},{448,384},... | collective-permute-start | bytes 147464 | tf_op jit(solution)/shard_map/ppermute | solution.py:80
  105.4 0.0 collective-permute-done.12.lo
  105.4 3.5 %collective-permute-done.13.hi = f32[96,128]{1,0:T(8,128)S(1)} collective-permute-done((f32[96,128]{1,0:T(8,128)S(1)}, f32[96,128]{1,0:T(8,128)S(1)}, u32[]{:S(2)}, u32[]{:S(2)}) %collective-permute-start.13) | collective-permute-done | bytes 49184 | tf_op jit(solution)/shard_map/ppermute | solution.py:80
  108.9 8.7 %shard_map.56 = (f32[32,16,128]{2,1,0:T(8,128)S(1)}, f32[32,16,128]{2,1,0:T(8,128)S(1)}, f32[32,16,128]{2,1,0:T(8,128)S(1)}, f32[8,128]{1,0:T(8,128)S(1)}) custom-call(f32[1536,128]{1,0:T(8,128)S(1)} %get-tuple-element.47.we, f32[96,128]{1,0:T(8,128)S(1)} %collective-permute-done.12.lo, f32[96,128]{1,0:T(8,128)S(1)} %collective-permute-done.13.hi, ...), custom_call_target="tpu_custom_call" | custom-call | tf_op jit(solution)/shard_map/pallas_call | solution.py:67
  117.6 7.8 %all_to_all.10 = f32[8,8,128]{2,1,0:T(8,128)S(1)} all-to-all(f32[8,8,128]{2,1,0:T(8,128)S(1)} %broadcast_in_dim.4), channel_id=1, replica_groups=mesh['gx'=8,'gy'=16,'gz'=4] {'gx'}, dimensions={0} | all-to-all | bytes 65536 | tf_op jit(solution)/shard_map/all_to_all | solution.py:361
  125.4 14.3 %all_to_all.11 = f32[16,8,128]{2,1,0:T(8,128)S(1)} all-to-all(f32[16,8,128]{2,1,0:T(8,128)S(1)} %broadcast_in_dim.5), channel_id=1, replica_groups=mesh['gx'=8,'gy'=16,'gz'=4] {'gy'}, dimensions={0} | all-to-all | bytes 131072 | tf_op jit(solution)/shard_map/all_to_all | solution.py:361
  139.7 11.9 %psum.7.dots = f32[8,128]{1,0:T(8,128)S(1)} all-reduce(f32[8,128]{1,0:T(8,128)S(1)} %reduce_sum.19), channel_id=1, replica_groups=mesh['gx'=8,'gy'=16,'gz'=4] {'gz'}, use_global_device_ids=true, to_apply=%region_2.0 | all-reduce | flops 1024 | bytes 8192 | tf_op jit(solution)/shard_map/psum | solution.py:362
  151.6 1.0 shard_map.57
  (5 shorter events, 0.1 us)
Async XLA Ops:
  0.6 47.3 %copy-start.1 = (f32[32,16,128]{2,1,0:T(8,128)S(1)}, f32[32,16,128]{2,1,0:T(8,128)}, u32[]{:S(2)}) copy-start(f32[32,16,128]{2,1,0:T(8,128)} %param.3) | copy-start | bytes 786436
  0.6 47.3 %copy-start.2 = (f32[32,16,128]{2,1,0:T(8,128)S(1)}, f32[32,16,128]{2,1,0:T(8,128)}, u32[]{:S(2)}) copy-start(f32[32,16,128]{2,1,0:T(8,128)} %param.5) | copy-start | bytes 786436
  2.0 45.9 %copy-start = (f32[32,16,128]{2,1,0:T(8,128)S(1)}, f32[32,16,128]{2,1,0:T(8,128)}, u32[]{:S(2)}) copy-start(f32[32,16,128]{2,1,0:T(8,128)} %x_ref.1) | copy-start | bytes 786436
  2.1 45.9 %collective-permute-start.2 = (f32[544,128]{1,0:T(8,128)S(1)}, f32[544,128]{1,0:T(8,128)S(1)}, u32[]{:S(2)}, u32[]{:S(2)}) collective-permute-start(f32[544,128]{1,0:T(8,128)S(1)} %get-tuple-element.32), channel_id=1, source_target_pairs={{0,4},{4,8},{8,12},{12,16},{16,20},{20,24},{24,28},{28,32},{32,36}... | collective-permute-start | bytes 835592 | tf_op jit(solution)/shard_map/ppermute | solution.py:80
  6.6 41.4 %collective-permute-start.3 = (f32[544,128]{1,0:T(8,128)S(1)}, f32[544,128]{1,0:T(8,128)S(1)}, u32[]{:S(2)}, u32[]{:S(2)}) collective-permute-start(f32[544,128]{1,0:T(8,128)S(1)} %get-tuple-element.33), channel_id=1, source_target_pairs={{4,0},{8,4},{12,8},{16,12},{20,16},{24,20},{28,24},{32,28},{36,32}... | collective-permute-start | bytes 835592 | tf_op jit(solution)/shard_map/ppermute | solution.py:80
  7.9 10.8 %collective-permute-start = (f32[272,128]{1,0:T(8,128)S(1)}, f32[272,128]{1,0:T(8,128)S(1)}, u32[]{:S(2)}, u32[]{:S(2)}) collective-permute-start(f32[272,128]{1,0:T(8,128)S(1)} %get-tuple-element.30), channel_id=1, source_target_pairs={{0,1},{1,2},{2,3},{4,5},{5,6},{6,7},{8,9},{9,10},{10,11},{12,13},{... | collective-permute-start | bytes 417800 | tf_op jit(solution)/shard_map/ppermute | solution.py:80
  16.7 10.7 %collective-permute-start.1 = (f32[272,128]{1,0:T(8,128)S(1)}, f32[272,128]{1,0:T(8,128)S(1)}, u32[]{:S(2)}, u32[]{:S(2)}) collective-permute-start(f32[272,128]{1,0:T(8,128)S(1)} %get-tuple-element.31), channel_id=1, source_target_pairs={{1,0},{2,1},{3,2},{5,4},{6,5},{7,6},{9,8},{10,9},{11,10},{13,12},{... | collective-permute-start | bytes 417800 | tf_op jit(solution)/shard_map/ppermute | solution.py:80
  27.5 17.0 %collective-permute-start.4 = (f32[88,128]{1,0:T(8,128)S(1)}, f32[88,128]{1,0:T(8,128)S(1)}, u32[]{:S(2)}, u32[]{:S(2)}) collective-permute-start(f32[88,128]{1,0:T(8,128)S(1)} %get-tuple-element.34), channel_id=1, source_target_pairs={{0,4},{4,8},{8,12},{12,16},{16,20},{20,24},{24,28},{28,32},{32,36}... | collective-permute-start | bytes 135176 | tf_op jit(solution)/shard_map/ppermute | solution.py:80
  43.1 4.8 %collective-permute-start.5 = (f32[88,128]{1,0:T(8,128)S(1)}, f32[88,128]{1,0:T(8,128)S(1)}, u32[]{:S(2)}, u32[]{:S(2)}) collective-permute-start(f32[88,128]{1,0:T(8,128)S(1)} %get-tuple-element.35), channel_id=1, source_target_pairs={{4,0},{8,4},{12,8},{16,12},{20,16},{24,20},{28,24},{32,28},{36,32}... | collective-permute-start | bytes 135176 | tf_op jit(solution)/shard_map/ppermute | solution.py:80
  49.4 7.6 %collective-permute-start.6 = (f32[288,128]{1,0:T(8,128)S(1)}, f32[288,128]{1,0:T(8,128)S(1)}, u32[]{:S(2)}, u32[]{:S(2)}) collective-permute-start(f32[288,128]{1,0:T(8,128)S(1)} %get-tuple-element.39), channel_id=1, source_target_pairs={{0,64},{64,128},{128,192},{192,256},{256,320},{320,384},{384,448},... | collective-permute-start | bytes 442376 | tf_op jit(solution)/shard_map/ppermute | solution.py:80
  54.9 6.5 %collective-permute-start.7 = (f32[288,128]{1,0:T(8,128)S(1)}, f32[288,128]{1,0:T(8,128)S(1)}, u32[]{:S(2)}, u32[]{:S(2)}) collective-permute-start(f32[288,128]{1,0:T(8,128)S(1)} %get-tuple-element.40), channel_id=1, source_target_pairs={{64,0},{128,64},{192,128},{256,192},{320,256},{384,320},{448,384},... | collective-permute-start | bytes 442376 | tf_op jit(solution)/shard_map/ppermute | solution.py:80
  68.3 8.2 %collective-permute-start.8 = (f32[8,16,128]{2,1,0:T(8,128)S(1)}, f32[8,16,128]{2,1,0:T(8,128)S(1)}, u32[]{:S(2)}, u32[]{:S(2)}) collective-permute-start(f32[8,16,128]{2,1,0:T(8,128)S(1)} %get-tuple-element.43), channel_id=1, source_target_pairs={{0,1},{1,2},{2,3},{4,5},{5,6},{6,7},{8,9},{9,10},{10,11},{12,13},{... | collective-permute-start | bytes 196616 | tf_op jit(solution)/shard_map/ppermute | solution.py:80
  75.2 9.3 %collective-permute-start.9 = (f32[8,16,128]{2,1,0:T(8,128)S(1)}, f32[8,16,128]{2,1,0:T(8,128)S(1)}, u32[]{:S(2)}, u32[]{:S(2)}) collective-permute-start(f32[8,16,128]{2,1,0:T(8,128)S(1)} %get-tuple-element.44), channel_id=1, source_target_pairs={{1,0},{2,1},{3,2},{5,4},{6,5},{7,6},{9,8},{10,9},{11,10},{13,12},{... | collective-permute-start | bytes 196616 | tf_op jit(solution)/shard_map/ppermute | solution.py:80
  84.6 5.3 %collective-permute-start.10 = (f32[312,128]{1,0:T(8,128)S(1)}, f32[312,128]{1,0:T(8,128)S(1)}, u32[]{:S(2)}, u32[]{:S(2)}) collective-permute-start(f32[312,128]{1,0:T(8,128)S(1)} %get-tuple-element.45), channel_id=1, source_target_pairs={{0,4},{4,8},{8,12},{12,16},{16,20},{20,24},{24,28},{28,32},{32,36}... | collective-permute-start | bytes 479240 | tf_op jit(solution)/shard_map/ppermute | solution.py:80
  87.7 10.9 %collective-permute-start.11 = (f32[312,128]{1,0:T(8,128)S(1)}, f32[312,128]{1,0:T(8,128)S(1)}, u32[]{:S(2)}, u32[]{:S(2)}) collective-permute-start(f32[312,128]{1,0:T(8,128)S(1)} %get-tuple-element.46), channel_id=1, source_target_pairs={{4,0},{8,4},{12,8},{16,12},{20,16},{24,20},{28,24},{32,28},{36,32}... | collective-permute-start | bytes 479240 | tf_op jit(solution)/shard_map/ppermute | solution.py:80
  99.2 6.2 %collective-permute-start.12 = (f32[96,128]{1,0:T(8,128)S(1)}, f32[96,128]{1,0:T(8,128)S(1)}, u32[]{:S(2)}, u32[]{:S(2)}) collective-permute-start(f32[96,128]{1,0:T(8,128)S(1)} %get-tuple-element.48), channel_id=1, source_target_pairs={{0,64},{64,128},{128,192},{192,256},{256,320},{320,384},{384,448},... | collective-permute-start | bytes 147464 | tf_op jit(solution)/shard_map/ppermute | solution.py:80
  103.5 5.4 %collective-permute-start.13 = (f32[96,128]{1,0:T(8,128)S(1)}, f32[96,128]{1,0:T(8,128)S(1)}, u32[]{:S(2)}, u32[]{:S(2)}) collective-permute-start(f32[96,128]{1,0:T(8,128)S(1)} %get-tuple-element.49), channel_id=1, source_target_pairs={{64,0},{128,64},{192,128},{256,192},{320,256},{384,320},{448,384},... | collective-permute-start | bytes 147464 | tf_op jit(solution)/shard_map/ppermute | solution.py:80

commit v5 on v4

--- a/solution.py
+++ b/solution.py
@@ -125,22 +125,20 @@
         for g in range(16):
             v = read(16 * q + g)
             a = v if g == 0 else pltpu.roll(v, G * g, 1)
-            b = v if g == 15 else pltpu.roll(v, G * (g + 1), 1)
             dn = jnp.where(group == g, a, dn)
-            up = jnp.where(group == g, b, up)
+            up = jnp.where(group == (g - 1) % 16, a, up)
         dn_ref[base + q * FY : base + (q + 1) * FY, :] = dn
         up_ref[base + q * FY : base + (q + 1) * FY, :] = up
 
 
 def unpack_lanes(lo_ref, hi_ref, base, write):
-    right = lax.broadcasted_iota(jnp.int32, (FY, NX), 1) < NX // 2
+    group = lax.broadcasted_iota(jnp.int32, (FY, NX), 1) // G
     for q in range(FZ // 16):
         lo = lo_ref[base + q * FY : base + (q + 1) * FY, :]
         hi = hi_ref[base + q * FY : base + (q + 1) * FY, :]
         for g in range(16):
-            a = hi if g == 0 else pltpu.roll(hi, NX - G * g, 1)
-            b = lo if g == 15 else pltpu.roll(lo, NX - G - G * g, 1)
-            write(16 * q + g, jnp.where(right, a, b))
+            v = jnp.where(group == g, hi, lo)
+            write(16 * q + g, v if g == 0 else pltpu.roll(v, NX - G * g, 1))
 
 
 def frame(x_ref, b_ref, k_ref, zlo, zhi, ylo, yhi, clo, chi, xe, be, ke, dn_ref, up_ref):
@@ -217,14 +215,18 @@
 
 
 def block_of(v, n):
-    return v.reshape(n, FY, NX)[:, G : G + NY]
+    return v.reshape(n, FY, NX)[:, G : G + NY].reshape(n * NY, NX)
+
+
+def block_rows(z, n):
+    return pl.ds(pl.multiple_of((z - G) * NY, NY), n * NY)
 
 
 def span(radius):
     return G - radius, G + NZ + radius
 
 
-def first_stage(xe, be, ke, lo, hi, r_out, w_out, wdn, wup, c0, c1, m0, m1, x1, b1, p0, p1, q0, q1):
+def first_stage(xe, be, ke, lo, hi, r_out, w_out, zdn, zup, ydn, yup, c0, c1, m0, m1, x1, b1, p0, p1, q0, q1):
     def put(ref):
         def write(z, v):
             ref[z * FY : (z + 1) * FY] = v
@@ -260,27 +262,28 @@
         at = rows_of(z, n)
         r = be[at]
         w = C0 * r + (C1 / SQ) * q0[at] + (C2 / SQ**2) * v0
-        w_out[pl.ds(z - G, n)] = block_of(w, n)
-        r_out[pl.ds(z - G, n)] = block_of(r, n)
+        w_out[block_rows(z, n)] = block_of(w, n)
+        r_out[block_rows(z, n)] = block_of(r, n)
 
     apply_k(p, None, coef, mask, *span(0), finish=to_precond)
-    wdn[...] = w_out[0:G]
-    wup[...] = w_out[NZ - G : NZ]
-
-
-def pack_y2(w_ref, lo_ref, hi_ref, dn_ref, up_ref):
+    zdn[...] = w_out[0 : G * NY]
+    zup[...] = w_out[(NZ - G) * NY : NZ * NY]
     for t in range(1, G + 1):
+        ydn[(t - 1) * NZ : t * NZ, :] = w_out[pl.ds(t - 1, NZ, stride=NY), :]
+        yup[(t - 1) * NZ : t * NZ, :] = w_out[pl.ds(NY - t, NZ, stride=NY), :]
+
+
+def pack_corners2(lo_ref, hi_ref, dn_ref, up_ref):
+    for t in range(1, G):
         n = G - t
         for out, row in ((dn_ref, t - 1), (up_ref, NY - t)):
-            out[(t - 1) * NZ : t * NZ, :] = w_ref[pl.ds(row, NZ, stride=NY), :]
-            if n:
-                at = MAIN_ROWS2 + CORNERS2[0, t, 0]
-                out[at : at + n, :] = lo_ref[pl.ds(t * NY + row, n, stride=NY), :]
-                at = MAIN_ROWS2 + CORNERS2[0, t, 1]
-                out[at : at + n, :] = hi_ref[pl.ds(row, n, stride=NY), :]
-
-
-def frame2(w_ref, zlo, zhi, ylo, yhi, we, dn_ref, up_ref):
+            at = CORNERS2[0, t, 0]
+            out[at : at + n, :] = lo_ref[pl.ds(t * NY + row, n, stride=NY), :]
+            at = CORNERS2[0, t, 1]
+            out[at : at + n, :] = hi_ref[pl.ds(row, n, stride=NY), :]
+
+
+def frame2(w_ref, zlo, zhi, ylo, yhi, clo, chi, we, dn_ref, up_ref):
     for z in range(FZ):
         at = z * FY
         src, k = (zlo, z) if z < G else (w_ref, z - G) if z < G + NZ else (zhi, z - G - NZ)
@@ -290,13 +293,13 @@
             we[at + G + NY : at + FY, :] = jnp.zeros((G, NX), f32)
     for t in range(1, G + 1):
         n = G - t
-        for src, row in ((ylo, G - t), (yhi, G + NY + t - 1)):
+        for src, corner, row in ((ylo, clo, G - t), (yhi, chi, G + NY + t - 1)):
             we[pl.ds(G * FY + row, NZ, stride=FY), :] = src[(t - 1) * NZ : t * NZ, :]
             if n:
-                at = MAIN_ROWS2 + CORNERS2[0, t, 0]
-                we[pl.ds((G - n) * FY + row, n, stride=FY), :] = src[at : at + n, :]
-                at = MAIN_ROWS2 + CORNERS2[0, t, 1]
-                we[pl.ds((G + NZ) * FY + row, n, stride=FY), :] = src[at : at + n, :]
+                at = CORNERS2[0, t, 0]
+                we[pl.ds((G - n) * FY + row, n, stride=FY), :] = corner[at : at + n, :]
+                at = CORNERS2[0, t, 1]
+                we[pl.ds((G + NZ) * FY + row, n, stride=FY), :] = corner[at : at + n, :]
     pack_lanes(lambda z: we[z * FY : (z + 1) * FY, :], dn_ref, up_ref, 0)
 
 
@@ -322,13 +325,13 @@
     acc[...] = jnp.zeros((4, G, NX), f32)
 
     def to_w3(z, n, a0, a1):
-        at, to = rows_of(z, n), pl.ds(z - G, n)
+        at, to = rows_of(z, n), block_rows(z, n)
         w, u1, u2, u3 = (block_of(v, n) for v in (we[at], q0[at], s0[at], a0))
         v1_out[to] = u1
         v2_out[to] = u2
         v3_out[to] = u3
         for i, t in enumerate((r_ref[to] * w, w * u1, u1 * u2, u2 * u3)):
-            acc[i] += jnp.sum(t[:, 0:8] + t[:, 8:16], axis=0)
+            acc[i] += jnp.sum(t.reshape(n * NY // G, G, NX), axis=0)
 
     apply_k(p, None, coef, mask, *span(0), finish=to_w3)
     dots[...] = jnp.zeros((G, NX), f32)
@@ -350,8 +353,8 @@
     a1 = e1 / (beta * beta * g0 - 2.0 * beta * a0 * h + a0 * a0 * k)
     near = a0 + a1 * beta
     far = a1 * a0
-    x_out[...] = x_ref[...] + near[None] * w_ref[...] - (far * (1.0 / SQ))[None] * v2[...]
-    r_out[...] = r_ref[...] - (near * (1.0 / SQ))[None] * v1[...] + (far * (1.0 / SQ**2))[None] * v3[...]
+    x_out[...] = x_ref[...] + near * w_ref[...] - (far * (1.0 / SQ)) * v2[...]
+    r_out[...] = r_ref[...] - (near * (1.0 / SQ)) * v1[...] + (far * (1.0 / SQ**2)) * v3[...]
 
 
 def all_sum(x):
@@ -379,25 +382,25 @@
     xe, be, ke, down, up = run(frame, [frame_shape] * 3 + [(3 * Q_PACK, NX)] * 2, (*flat, zlo, zhi, ylo, yhi, clo, chi))
     xlo, xhi = exchange(down, up, "gx")
     tile = pltpu.VMEM(frame_shape, f32)
-    block = (NZ, NY, NX)
-    slab = (G, NY, NX)
+    block = (NZ * NY, NX)
+    slab = (G * NY, NX)
 
     def stage1(xe, be_in, *rest):
         be = rest[-1]
         be[...] = be_in[...]
         first_stage(xe, be, *rest[:-1])
 
-    r0, w0, down, up, c0, c1, m0, m1 = run(
+    r0, w0, zdn, zup, ydn, yup, c0, c1, m0, m1 = run(
         stage1,
-        [block, block, slab, slab, frame_shape, frame_shape, frame_shape, frame_shape],
+        [block, block, slab, slab, (MAIN_ROWS2, NX), (MAIN_ROWS2, NX), frame_shape, frame_shape, frame_shape, frame_shape],
         (xe, be, ke, xlo, xhi),
         scratch=[tile] * 7,
     )
-    zlo, zhi = exchange(down, up, "gz")
-    w_flat, zlo, zhi = (v.reshape(-1, NX) for v in (w0, zlo, zhi))
-    down, up = run(pack_y2, [(MAIN_ROWS2 + CORNER_ROWS2, NX)] * 2, (w_flat, zlo, zhi))
-    ylo, yhi = exchange(down, up, "gy")
-    we, down, up = run(frame2, [frame_shape, (Q_PACK, NX), (Q_PACK, NX)], (w_flat, zlo, zhi, ylo, yhi))
+    zlo, zhi = exchange(zdn, zup, "gz")
+    ylo, yhi = exchange(ydn, yup, "gy")
+    down, up = run(pack_corners2, [(CORNER_ROWS2, NX)] * 2, (zlo, zhi))
+    clo, chi = exchange(down, up, "gy")
+    we, down, up = run(frame2, [frame_shape, (Q_PACK, NX), (Q_PACK, NX)], (w0, zlo, zhi, ylo, yhi, clo, chi))
     xlo, xhi = exchange(down, up, "gx")
     v1, v2, v3, dots = run(
         second_stage,
@@ -406,8 +409,8 @@
         scratch=[pltpu.VMEM((4, G, NX), f32)] + [tile] * 7,
     )
     dots = all_sum(dots)
-    x, r = run(finish, [block, block], (initial, r0, w0, v1, v2, v3, dots))
-    return x, r
+    x, r = run(finish, [block, block], (flat[0], r0, w0, v1, v2, v3, dots))
+    return x.reshape(NZ, NY, NX), r.reshape(NZ, NY, NX)
 
 
 def solution(mesh):

time: 155 us -> 161 us (1.039)
  starting transfers between devices: 59.1 us -> 65.5 us
  blocking collectives: 34 us -> 37.8 us
  waiting for transfers between devices: 38.5 us -> 35.1 us
    ppermute x14 -> x16, starting transfers between devices: 59.1 us -> 65.5 us  [shift(): return lax.ppermute(x, axis, pairs)]
    all_to_all x2, blocking collectives: 22.1 us -> 27 us  [all_sum(): x = jnp.sum(lax.all_to_all(copies, axis, 0, 0), axis=0)]
    ppermute x14 -> x16, waiting for transfers between devices: 38.5 us -> 35.1 us  [shift(): return lax.ppermute(x, axis, pairs)]
  transfers between devices with their start and end apart: 14 -> 16, of which waited for: 9 -> 8; matrix products, arithmetic and copies ran while one was open for 0% -> 0% of each run, Pallas kernels for 0% -> 0%
where the time goes in v5:
time: 161 us; the launch traced here: 158 us
  starting transfers between devices  65.5 us (41%)
  blocking collectives  37.8 us (23%)
  waiting for transfers between devices  35.1 us (22%)
  Pallas kernels  19 us (12%)
    ppermute x16, starting transfers between devices, shift(): return lax.ppermute(x, axis, pairs)  65.5 us
    ppermute x16, waiting for transfers between devices, shift(): return lax.ppermute(x, axis, pairs)  35.1 us
    all_to_all x2, blocking collectives, all_sum(): x = jnp.sum(lax.all_to_all(copies, axis, 0, 0), axis=0)  27 us
    pallas_call x8, Pallas kernels, run(): pl.pallas_call(kernel, out_shape=[jax.ShapeDtypeStruct(s, f32) for s in o...  19 us
    psum x1, blocking collectives, all_sum(): return lax.psum(x, 'gz')  10.7 us
  transfers between devices with their start and end apart: 16, of which 8 were waited for; matrix products, arithmetic and copies ran while one was open for 0% of the time, Pallas kernels for 0%

profile of v5, /device:TPU:1, one launch (start us, length us, event | category | flops | bytes accessed | tf_op | source)
XLA Modules:
  0.0 158.3 jit_solution(4600901298628733513)
XLA Ops:
  0.6 0.0 copy-start.1
  0.6 0.0 copy-start.2
  0.6 1.4 shard_map.50
  2.0 0.0 copy-start
  2.1 4.5 %collective-permute-start.2 = (f32[544,128]{1,0:T(8,128)S(1)}, f32[544,128]{1,0:T(8,128)S(1)}, u32[]{:S(2)}, u32[]{:S(2)}) collective-permute-start(f32[544,128]{1,0:T(8,128)S(1)} %get-tuple-element.36), channel_id=1, source_target_pairs={{0,4},{4,8},{8,12},{12,16},{16,20},{20,24},{24,28},{28,32},{32,36}... | collective-permute-start | bytes 835592 | tf_op jit(solution)/shard_map/ppermute | solution.py:80
  6.6 1.3 collective-permute-start.3
  7.9 8.8 %collective-permute-start = (f32[272,128]{1,0:T(8,128)S(1)}, f32[272,128]{1,0:T(8,128)S(1)}, u32[]{:S(2)}, u32[]{:S(2)}) collective-permute-start(f32[272,128]{1,0:T(8,128)S(1)} %get-tuple-element.34), channel_id=1, source_target_pairs={{0,1},{1,2},{2,3},{4,5},{5,6},{6,7},{8,9},{9,10},{10,11},{12,13},{... | collective-permute-start | bytes 417800 | tf_op jit(solution)/shard_map/ppermute | solution.py:80
  16.7 1.3 collective-permute-start.1
  18.0 0.7 collective-permute-done.lo_ref.zlo
  18.7 8.7 %collective-permute-done.1.hi_ref.zhi = f32[272,128]{1,0:T(8,128)S(1)} collective-permute-done((f32[272,128]{1,0:T(8,128)S(1)}, f32[272,128]{1,0:T(8,128)S(1)}, u32[]{:S(2)}, u32[]{:S(2)}) %collective-permute-start.1) | collective-permute-done | bytes 139296 | tf_op jit(solution)/shard_map/ppermute | solution.py:80
  27.5 15.7 %collective-permute-start.4 = (f32[88,128]{1,0:T(8,128)S(1)}, f32[88,128]{1,0:T(8,128)S(1)}, u32[]{:S(2)}, u32[]{:S(2)}) collective-permute-start(f32[88,128]{1,0:T(8,128)S(1)} %get-tuple-element.38), channel_id=1, source_target_pairs={{0,4},{4,8},{8,12},{12,16},{16,20},{20,24},{24,28},{28,32},{32,36}... | collective-permute-start | bytes 135176 | tf_op jit(solution)/shard_map/ppermute | solution.py:80
  43.1 1.3 collective-permute-start.5
  44.4 0.0 collective-permute-done.4.clo
  44.5 3.5 %collective-permute-done.5.chi = f32[88,128]{1,0:T(8,128)S(1)} collective-permute-done((f32[88,128]{1,0:T(8,128)S(1)}, f32[88,128]{1,0:T(8,128)S(1)}, u32[]{:S(2)}, u32[]{:S(2)}) %collective-permute-start.5) | collective-permute-done | bytes 45088 | tf_op jit(solution)/shard_map/ppermute | solution.py:80
  47.9 0.0 collective-permute-done.2.ylo
  47.9 0.0 collective-permute-done.3.yhi
  47.9 0.0 copy-done.1
  47.9 0.0 copy-done.2
  48.0 0.0 copy-done
  48.0 0.8 shard_map.52
  48.8 5.5 %collective-permute-start.6 = (f32[288,128]{1,0:T(8,128)S(1)}, f32[288,128]{1,0:T(8,128)S(1)}, u32[]{:S(2)}, u32[]{:S(2)}) collective-permute-start(f32[288,128]{1,0:T(8,128)S(1)} %get-tuple-element.43), channel_id=1, source_target_pairs={{0,64},{64,128},{128,192},{192,256},{256,320},{320,384},{384,448},... | collective-permute-start | bytes 442376 | tf_op jit(solution)/shard_map/ppermute | solution.py:80
  54.3 1.9 %collective-permute-start.7 = (f32[288,128]{1,0:T(8,128)S(1)}, f32[288,128]{1,0:T(8,128)S(1)}, u32[]{:S(2)}, u32[]{:S(2)}) collective-permute-start(f32[288,128]{1,0:T(8,128)S(1)} %get-tuple-element.44), channel_id=1, source_target_pairs={{64,0},{128,64},{192,128},{256,192},{320,256},{384,320},{448,384},... | collective-permute-start | bytes 442376 | tf_op jit(solution)/shard_map/ppermute | solution.py:80
  56.2 0.2 collective-permute-done.6.rest_1_
  56.4 4.4 %collective-permute-done.7.rest_2_ = f32[288,128]{1,0:T(8,128)S(1)} collective-permute-done((f32[288,128]{1,0:T(8,128)S(1)}, f32[288,128]{1,0:T(8,128)S(1)}, u32[]{:S(2)}, u32[]{:S(2)}) %collective-permute-start.7) | collective-permute-done | bytes 147488 | tf_op jit(solution)/shard_map/ppermute | solution.py:80
  60.8 6.7 %shard_map.53 = (f32[512,128]{1,0:T(8,128)S(1)}, f32[512,128]{1,0:T(8,128)S(1)}, f32[128,128]{1,0:T(8,128)S(1)}, f32[128,128]{1,0:T(8,128)S(1)}, f32[256,128]{1,...) custom-call(f32[1536,128]{1,0:T(8,128)S(1)} %get-tuple-element.40.xe, ...), custom_call_target="tpu_custom_call" | custom-call | tf_op jit(solution)/shard_map/pallas_call | solution.py:67
  67.4 2.0 %collective-permute-start.10 = (f32[256,128]{1,0:T(8,128)S(1)}, f32[256,128]{1,0:T(8,128)S(1)}, u32[]{:S(2)}, u32[]{:S(2)}) collective-permute-start(f32[256,128]{1,0:T(8,128)S(1)} %get-tuple-element.49), channel_id=1, source_target_pairs={{0,4},{4,8},{8,12},{12,16},{16,20},{20,24},{24,28},{28,32},{32,36}... | collective-permute-start | bytes 393224 | tf_op jit(solution)/shard_map/ppermute | solution.py:80
  69.4 1.3 collective-permute-start.11
  70.7 7.0 %collective-permute-start.8 = (f32[128,128]{1,0:T(8,128)S(1)}, f32[128,128]{1,0:T(8,128)S(1)}, u32[]{:S(2)}, u32[]{:S(2)}) collective-permute-start(f32[128,128]{1,0:T(8,128)S(1)} %get-tuple-element.47), channel_id=1, source_target_pairs={{0,1},{1,2},{2,3},{4,5},{5,6},{6,7},{8,9},{9,10},{10,11},{12,13},{... | collective-permute-start | bytes 196616 | tf_op jit(solution)/shard_map/ppermute | solution.py:80
  77.7 1.3 collective-permute-start.9
  79.0 0.0 collective-permute-done.8.lo_ref.zlo
  79.0 7.6 %collective-permute-done.9.hi_ref.zhi = f32[128,128]{1,0:T(8,128)S(1)} collective-permute-done((f32[128,128]{1,0:T(8,128)S(1)}, f32[128,128]{1,0:T(8,128)S(1)}, u32[]{:S(2)}, u32[]{:S(2)}) %collective-permute-start.9) | collective-permute-done | bytes 65568 | tf_op jit(solution)/shard_map/ppermute | solution.py:80
  86.7 5.7 %collective-permute-start.12 = (f32[56,128]{1,0:T(8,128)S(1)}, f32[56,128]{1,0:T(8,128)S(1)}, u32[]{:S(2)}, u32[]{:S(2)}) collective-permute-start(f32[56,128]{1,0:T(8,128)S(1)} %get-tuple-element.51), channel_id=1, source_target_pairs={{0,4},{4,8},{8,12},{12,16},{16,20},{20,24},{24,28},{28,32},{32,36}... | collective-permute-start | bytes 86024 | tf_op jit(solution)/shard_map/ppermute | solution.py:80
  92.4 1.3 collective-permute-start.13
  93.7 0.0 collective-permute-done.12.clo
  93.7 6.5 %collective-permute-done.13.chi = f32[56,128]{1,0:T(8,128)S(1)} collective-permute-done((f32[56,128]{1,0:T(8,128)S(1)}, f32[56,128]{1,0:T(8,128)S(1)}, u32[]{:S(2)}, u32[]{:S(2)}) %collective-permute-start.13) | collective-permute-done | bytes 28704 | tf_op jit(solution)/shard_map/ppermute | solution.py:80
  100.2 0.0 collective-permute-done.10.ylo
  100.2 0.0 collective-permute-done.11.yhi
  100.2 0.4 shard_map.55
  100.6 4.8 %collective-permute-start.14 = (f32[96,128]{1,0:T(8,128)S(1)}, f32[96,128]{1,0:T(8,128)S(1)}, u32[]{:S(2)}, u32[]{:S(2)}) collective-permute-start(f32[96,128]{1,0:T(8,128)S(1)} %get-tuple-element.54), channel_id=1, source_target_pairs={{0,64},{64,128},{128,192},{192,256},{256,320},{320,384},{384,448},... | collective-permute-start | bytes 147464 | tf_op jit(solution)/shard_map/ppermute | solution.py:80
  105.4 1.9 %collective-permute-start.15 = (f32[96,128]{1,0:T(8,128)S(1)}, f32[96,128]{1,0:T(8,128)S(1)}, u32[]{:S(2)}, u32[]{:S(2)}) collective-permute-start(f32[96,128]{1,0:T(8,128)S(1)} %get-tuple-element.55), channel_id=1, source_target_pairs={{64,0},{128,64},{192,128},{256,192},{320,256},{384,320},{448,384},... | collective-permute-start | bytes 147464 | tf_op jit(solution)/shard_map/ppermute | solution.py:80
  107.3 0.0 collective-permute-done.14.lo
  107.4 3.5 %collective-permute-done.15.hi = f32[96,128]{1,0:T(8,128)S(1)} collective-permute-done((f32[96,128]{1,0:T(8,128)S(1)}, f32[96,128]{1,0:T(8,128)S(1)}, u32[]{:S(2)}, u32[]{:S(2)}) %collective-permute-start.15) | collective-permute-done | bytes 49184 | tf_op jit(solution)/shard_map/ppermute | solution.py:80
  110.8 8.7 %shard_map.56 = (f32[512,128]{1,0:T(8,128)S(1)}, f32[512,128]{1,0:T(8,128)S(1)}, f32[512,128]{1,0:T(8,128)S(1)}, f32[8,128]{1,0:T(8,128)S(1)}) custom-call(f32[1536,128]{1,0:T(8,128)S(1)} %get-tuple-element.53.we, f32[96,128]{1,0:T(8,128)S(1)} %collective-permute-done.14.lo, f32[96,128]{1,0:T(8,128)S(1)} %collective-permute-done.15.hi, ...), custom_call_target="tpu_custom_call" | custom-call | tf_op jit(solution)/shard_map/pallas_call | solution.py:67
  119.5 8.8 %all_to_all.10 = f32[8,8,128]{2,1,0:T(8,128)S(1)} all-to-all(f32[8,8,128]{2,1,0:T(8,128)S(1)} %broadcast_in_dim.4), channel_id=1, replica_groups=mesh['gx'=8,'gy'=16,'gz'=4] {'gx'}, dimensions={0} | all-to-all | bytes 65536 | tf_op jit(solution)/shard_map/all_to_all | solution.py:364
  128.3 18.2 %all_to_all.11 = f32[16,8,128]{2,1,0:T(8,128)S(1)} all-to-all(f32[16,8,128]{2,1,0:T(8,128)S(1)} %broadcast_in_dim.5), channel_id=1, replica_groups=mesh['gx'=8,'gy'=16,'gz'=4] {'gy'}, dimensions={0} | all-to-all | bytes 131072 | tf_op jit(solution)/shard_map/all_to_all | solution.py:364
  146.6 10.7 %psum.7.dots = f32[8,128]{1,0:T(8,128)S(1)} all-reduce(f32[8,128]{1,0:T(8,128)S(1)} %reduce_sum.19), channel_id=1, replica_groups=mesh['gx'=8,'gy'=16,'gz'=4] {'gz'}, use_global_device_ids=true, to_apply=%region_2.0 | all-reduce | flops 1024 | bytes 8192 | tf_op jit(solution)/shard_map/psum | solution.py:365
  157.3 1.0 shard_map.57
  (6 shorter events, 0.1 us)
Async XLA Ops:
  0.6 47.3 %copy-start.1 = (f32[32,16,128]{2,1,0:T(8,128)S(1)}, f32[32,16,128]{2,1,0:T(8,128)}, u32[]{:S(2)}) copy-start(f32[32,16,128]{2,1,0:T(8,128)} %param.3) | copy-start | bytes 786436
  0.6 47.3 %copy-start.2 = (f32[32,16,128]{2,1,0:T(8,128)S(1)}, f32[32,16,128]{2,1,0:T(8,128)}, u32[]{:S(2)}) copy-start(f32[32,16,128]{2,1,0:T(8,128)} %param.5) | copy-start | bytes 786436
  2.0 45.9 %copy-start = (f32[32,16,128]{2,1,0:T(8,128)S(1)}, f32[32,16,128]{2,1,0:T(8,128)}, u32[]{:S(2)}) copy-start(f32[32,16,128]{2,1,0:T(8,128)} %param.4) | copy-start | bytes 786436
  2.1 45.9 %collective-permute-start.2 = (f32[544,128]{1,0:T(8,128)S(1)}, f32[544,128]{1,0:T(8,128)S(1)}, u32[]{:S(2)}, u32[]{:S(2)}) collective-permute-start(f32[544,128]{1,0:T(8,128)S(1)} %get-tuple-element.36), channel_id=1, source_target_pairs={{0,4},{4,8},{8,12},{12,16},{16,20},{20,24},{24,28},{28,32},{32,36}... | collective-permute-start | bytes 835592 | tf_op jit(solution)/shard_map/ppermute | solution.py:80
  6.6 41.4 %collective-permute-start.3 = (f32[544,128]{1,0:T(8,128)S(1)}, f32[544,128]{1,0:T(8,128)S(1)}, u32[]{:S(2)}, u32[]{:S(2)}) collective-permute-start(f32[544,128]{1,0:T(8,128)S(1)} %get-tuple-element.37), channel_id=1, source_target_pairs={{4,0},{8,4},{12,8},{16,12},{20,16},{24,20},{28,24},{32,28},{36,32}... | collective-permute-start | bytes 835592 | tf_op jit(solution)/shard_map/ppermute | solution.py:80
  7.9 10.8 %collective-permute-start = (f32[272,128]{1,0:T(8,128)S(1)}, f32[272,128]{1,0:T(8,128)S(1)}, u32[]{:S(2)}, u32[]{:S(2)}) collective-permute-start(f32[272,128]{1,0:T(8,128)S(1)} %get-tuple-element.34), channel_id=1, source_target_pairs={{0,1},{1,2},{2,3},{4,5},{5,6},{6,7},{8,9},{9,10},{10,11},{12,13},{... | collective-permute-start | bytes 417800 | tf_op jit(solution)/shard_map/ppermute | solution.py:80
  16.7 10.7 %collective-permute-start.1 = (f32[272,128]{1,0:T(8,128)S(1)}, f32[272,128]{1,0:T(8,128)S(1)}, u32[]{:S(2)}, u32[]{:S(2)}) collective-permute-start(f32[272,128]{1,0:T(8,128)S(1)} %get-tuple-element.35), channel_id=1, source_target_pairs={{1,0},{2,1},{3,2},{5,4},{6,5},{7,6},{9,8},{10,9},{11,10},{13,12},{... | collective-permute-start | bytes 417800 | tf_op jit(solution)/shard_map/ppermute | solution.py:80
  27.5 17.0 %collective-permute-start.4 = (f32[88,128]{1,0:T(8,128)S(1)}, f32[88,128]{1,0:T(8,128)S(1)}, u32[]{:S(2)}, u32[]{:S(2)}) collective-permute-start(f32[88,128]{1,0:T(8,128)S(1)} %get-tuple-element.38), channel_id=1, source_target_pairs={{0,4},{4,8},{8,12},{12,16},{16,20},{20,24},{24,28},{28,32},{32,36}... | collective-permute-start | bytes 135176 | tf_op jit(solution)/shard_map/ppermute | solution.py:80
  43.1 4.8 %collective-permute-start.5 = (f32[88,128]{1,0:T(8,128)S(1)}, f32[88,128]{1,0:T(8,128)S(1)}, u32[]{:S(2)}, u32[]{:S(2)}) collective-permute-start(f32[88,128]{1,0:T(8,128)S(1)} %get-tuple-element.39), channel_id=1, source_target_pairs={{4,0},{8,4},{12,8},{16,12},{20,16},{24,20},{28,24},{32,28},{36,32}... | collective-permute-start | bytes 135176 | tf_op jit(solution)/shard_map/ppermute | solution.py:80
  48.8 7.6 %collective-permute-start.6 = (f32[288,128]{1,0:T(8,128)S(1)}, f32[288,128]{1,0:T(8,128)S(1)}, u32[]{:S(2)}, u32[]{:S(2)}) collective-permute-start(f32[288,128]{1,0:T(8,128)S(1)} %get-tuple-element.43), channel_id=1, source_target_pairs={{0,64},{64,128},{128,192},{192,256},{256,320},{320,384},{384,448},... | collective-permute-start | bytes 442376 | tf_op jit(solution)/shard_map/ppermute | solution.py:80
  54.3 6.5 %collective-permute-start.7 = (f32[288,128]{1,0:T(8,128)S(1)}, f32[288,128]{1,0:T(8,128)S(1)}, u32[]{:S(2)}, u32[]{:S(2)}) collective-permute-start(f32[288,128]{1,0:T(8,128)S(1)} %get-tuple-element.44), channel_id=1, source_target_pairs={{64,0},{128,64},{192,128},{256,192},{320,256},{384,320},{448,384},... | collective-permute-start | bytes 442376 | tf_op jit(solution)/shard_map/ppermute | solution.py:80
  67.4 32.8 %collective-permute-start.10 = (f32[256,128]{1,0:T(8,128)S(1)}, f32[256,128]{1,0:T(8,128)S(1)}, u32[]{:S(2)}, u32[]{:S(2)}) collective-permute-start(f32[256,128]{1,0:T(8,128)S(1)} %get-tuple-element.49), channel_id=1, source_target_pairs={{0,4},{4,8},{8,12},{12,16},{16,20},{20,24},{24,28},{28,32},{32,36}... | collective-permute-start | bytes 393224 | tf_op jit(solution)/shard_map/ppermute | solution.py:80
  69.4 30.8 %collective-permute-start.11 = (f32[256,128]{1,0:T(8,128)S(1)}, f32[256,128]{1,0:T(8,128)S(1)}, u32[]{:S(2)}, u32[]{:S(2)}) collective-permute-start(f32[256,128]{1,0:T(8,128)S(1)} %get-tuple-element.50), channel_id=1, source_target_pairs={{4,0},{8,4},{12,8},{16,12},{20,16},{24,20},{28,24},{32,28},{36,32}... | collective-permute-start | bytes 393224 | tf_op jit(solution)/shard_map/ppermute | solution.py:80
  70.7 8.3 %collective-permute-start.8 = (f32[128,128]{1,0:T(8,128)S(1)}, f32[128,128]{1,0:T(8,128)S(1)}, u32[]{:S(2)}, u32[]{:S(2)}) collective-permute-start(f32[128,128]{1,0:T(8,128)S(1)} %get-tuple-element.47), channel_id=1, source_target_pairs={{0,1},{1,2},{2,3},{4,5},{5,6},{6,7},{8,9},{9,10},{10,11},{12,13},{... | collective-permute-start | bytes 196616 | tf_op jit(solution)/shard_map/ppermute | solution.py:80
  77.7 8.9 %collective-permute-start.9 = (f32[128,128]{1,0:T(8,128)S(1)}, f32[128,128]{1,0:T(8,128)S(1)}, u32[]{:S(2)}, u32[]{:S(2)}) collective-permute-start(f32[128,128]{1,0:T(8,128)S(1)} %get-tuple-element.48), channel_id=1, source_target_pairs={{1,0},{2,1},{3,2},{5,4},{6,5},{7,6},{9,8},{10,9},{11,10},{13,12},{... | collective-permute-start | bytes 196616 | tf_op jit(solution)/shard_map/ppermute | solution.py:80
  86.7 7.0 %collective-permute-start.12 = (f32[56,128]{1,0:T(8,128)S(1)}, f32[56,128]{1,0:T(8,128)S(1)}, u32[]{:S(2)}, u32[]{:S(2)}) collective-permute-start(f32[56,128]{1,0:T(8,128)S(1)} %get-tuple-element.51), channel_id=1, source_target_pairs={{0,4},{4,8},{8,12},{12,16},{16,20},{20,24},{24,28},{28,32},{32,36}... | collective-permute-start | bytes 86024 | tf_op jit(solution)/shard_map/ppermute | solution.py:80
  92.4 7.8 %collective-permute-start.13 = (f32[56,128]{1,0:T(8,128)S(1)}, f32[56,128]{1,0:T(8,128)S(1)}, u32[]{:S(2)}, u32[]{:S(2)}) collective-permute-start(f32[56,128]{1,0:T(8,128)S(1)} %get-tuple-element.52), channel_id=1, source_target_pairs={{4,0},{8,4},{12,8},{16,12},{20,16},{24,20},{28,24},{32,28},{36,32}... | collective-permute-start | bytes 86024 | tf_op jit(solution)/shard_map/ppermute | solution.py:80
  100.6 6.7 %collective-permute-start.14 = (f32[96,128]{1,0:T(8,128)S(1)}, f32[96,128]{1,0:T(8,128)S(1)}, u32[]{:S(2)}, u32[]{:S(2)}) collective-permute-start(f32[96,128]{1,0:T(8,128)S(1)} %get-tuple-element.54), channel_id=1, source_target_pairs={{0,64},{64,128},{128,192},{192,256},{256,320},{320,384},{384,448},... | collective-permute-start | bytes 147464 | tf_op jit(solution)/shard_map/ppermute | solution.py:80
  105.4 5.4 %collective-permute-start.15 = (f32[96,128]{1,0:T(8,128)S(1)}, f32[96,128]{1,0:T(8,128)S(1)}, u32[]{:S(2)}, u32[]{:S(2)}) collective-permute-start(f32[96,128]{1,0:T(8,128)S(1)} %get-tuple-element.55), channel_id=1, source_target_pairs={{64,0},{128,64},{192,128},{256,192},{320,256},{384,320},{448,384},... | collective-permute-start | bytes 147464 | tf_op jit(solution)/shard_map/ppermute | solution.py:80

commit v6 on v5

--- a/solution.py
+++ b/solution.py
@@ -168,62 +168,65 @@
 
 
 PLANES = 8
-
-
-def rows_of(z, n, shift=0):
-    return pl.ds(pl.multiple_of(z * FY, FY) + shift, n * FY)
-
-
-def apply_k(src, dst, coef, mask, first, last, finish=None):
+GROUP = 4
+
+
+class Window:
+    def __init__(self, radius):
+        self.first, self.last = G - radius, G + NZ + radius
+        self.y, self.n = (G, NY) if radius == 0 else (4, 24) if radius <= 4 else (0, FY)
+
+    def at(self, z, shift=0):
+        return pl.ds(pl.multiple_of(z * FY, FY) + (self.y + shift), self.n)
+
+
+def apply_k(src, dst, coef, mask, radius, finish=None):
+    win = Window(radius)
     s0, s1 = src
     c0, c1 = coef
     m0, m1 = mask
 
-    def plane(z):
-        lane = lax.broadcasted_iota(jnp.int32, (FY, NX), 1)
-
-        def around(ref, v, other):
-            x = pltpu.roll(jnp.where(lane == NX - 1, other, v), 1, 1)
-            x = x + pltpu.roll(jnp.where(lane == 0, other, v), NX - 1, 1)
-            y = ref[rows_of(z, 1, -1)] + ref[rows_of(z, 1, 1)]
-            return (y + (ref[rows_of(z, 1, -FY)] + ref[rows_of(z, 1, FY)])) + x
-
-        here = rows_of(z, 1)
-        v0, v1 = s0[here], s1[here]
-        r0 = c0[here] * v0 - m0[here] * around(s0, v0, v1)
-        r1 = c1[here] * v1 - m1[here] * around(s1, v1, v0)
-        if finish is None:
-            dst[0][here] = r0
-            dst[1][here] = r1
-        else:
-            finish(z, 1, r0, r1)
-
-    def planes(z, n):
-        for k in range(n):
-            plane(z + k)
-
-    count = last - first
+    def group(planes):
+        lane = lax.broadcasted_iota(jnp.int32, (win.n, NX), 1)
+        here = [win.at(z) for z in planes]
+        v0, v1 = [s0[at] for at in here], [s1[at] for at in here]
+        left0 = [pltpu.roll(jnp.where(lane == NX - 1, b, a), 1, 1) for a, b in zip(v0, v1)]
+        left1 = [pltpu.roll(jnp.where(lane == NX - 1, a, b), 1, 1) for a, b in zip(v0, v1)]
+        right0 = [pltpu.roll(jnp.where(lane == 0, b, a), NX - 1, 1) for a, b in zip(v0, v1)]
+        right1 = [pltpu.roll(jnp.where(lane == 0, a, b), NX - 1, 1) for a, b in zip(v0, v1)]
+
+        def around(ref, z):
+            y = ref[win.at(z, -1)] + ref[win.at(z, 1)]
+            return y + (ref[win.at(z, -FY)] + ref[win.at(z, FY)])
+
+        for i, z in enumerate(planes):
+            at = here[i]
+            r0 = c0[at] * v0[i] - m0[at] * (around(s0, z) + (left0[i] + right0[i]))
+            r1 = c1[at] * v1[i] - m1[at] * (around(s1, z) + (left1[i] + right1[i]))
+            if finish is None:
+                dst[0][at] = r0
+                dst[1][at] = r1
+            else:
+                finish(z, at, r0, r1)
+
+    def some(z, n):
+        for k in range(0, n, GROUP):
+            group([z + k + i for i in range(min(GROUP, n - k))])
+
+    count = win.last - win.first
     whole = count // PLANES
 
     def step(i, _):
-        planes(first + i * PLANES, PLANES)
+        some(win.first + i * PLANES, PLANES)
         return 0
 
     lax.fori_loop(0, whole, step, 0)
     if count % PLANES:
-        planes(first + whole * PLANES, count % PLANES)
-
-
-def block_of(v, n):
-    return v.reshape(n, FY, NX)[:, G : G + NY].reshape(n * NY, NX)
-
-
-def block_rows(z, n):
-    return pl.ds(pl.multiple_of((z - G) * NY, NY), n * NY)
-
-
-def span(radius):
-    return G - radius, G + NZ + radius
+        some(win.first + whole * PLANES, count % PLANES)
+
+
+def block_rows(z):
+    return pl.ds(pl.multiple_of((z - G) * NY, NY), NY)
 
 
 def first_stage(xe, be, ke, lo, hi, r_out, w_out, zdn, zup, ydn, yup, c0, c1, m0, m1, x1, b1, p0, p1, q0, q1):
@@ -246,26 +249,23 @@
     unpack_lanes(lo, hi, 2 * Q_PACK, put_coef)
     coef, mask, p, q, b = (c0, c1), (m0, m1), (p0, p1), (q0, q1), (be, b1)
 
-    apply_k((xe, x1), p, coef, mask, *span(5))
-
-    def to_residual(z, n, v0, v1):
-        at = rows_of(z, n)
+    apply_k((xe, x1), p, coef, mask, 5)
+
+    def to_residual(z, at, v0, v1):
         be[at] = be[at] - v0 * (1.0 / SQ)
         b1[at] = b1[at] - v1 * (1.0 / SQ)
 
-    apply_k(p, None, coef, mask, *span(4), finish=to_residual)
-    apply_k(b, p, coef, mask, *span(3))
-    apply_k(p, q, coef, mask, *span(2))
-    apply_k(q, p, coef, mask, *span(1))
-
-    def to_precond(z, n, v0, v1):
-        at = rows_of(z, n)
+    apply_k(p, None, coef, mask, 4, finish=to_residual)
+    apply_k(b, p, coef, mask, 3)
+    apply_k(p, q, coef, mask, 2)
+    apply_k(q, p, coef, mask, 1)
+
+    def to_precond(z, at, v0, _):
         r = be[at]
-        w = C0 * r + (C1 / SQ) * q0[at] + (C2 / SQ**2) * v0
-        w_out[block_rows(z, n)] = block_of(w, n)
-        r_out[block_rows(z, n)] = block_of(r, n)
-
-    apply_k(p, None, coef, mask, *span(0), finish=to_precond)
+        w_out[block_rows(z)] = C0 * r + (C1 / SQ) * q0[at] + (C2 / SQ**2) * v0
+        r_out[block_rows(z)] = r
+
+    apply_k(p, None, coef, mask, 0, finish=to_precond)
     zdn[...] = w_out[0 : G * NY]
     zup[...] = w_out[(NZ - G) * NY : NZ * NY]
     for t in range(1, G + 1):
@@ -309,31 +309,30 @@
 
     unpack_lanes(lo, hi, 0, write)
     coef, mask, p, q, s = (c0, c1), (m0, m1), (p0, p1), (q0, q1), (s0, s1)
-    apply_k((we, w1), p, coef, mask, *span(7))
-    apply_k(p, q, coef, mask, *span(6))
-    apply_k(q, p, coef, mask, *span(5))
-    apply_k(p, s, coef, mask, *span(4))
-    apply_k(s, p, coef, mask, *span(3))
-
-    def to_w2(z, n, a0, a1):
-        at = rows_of(z, n)
+    apply_k((we, w1), p, coef, mask, 7)
+    apply_k(p, q, coef, mask, 6)
+    apply_k(q, p, coef, mask, 5)
+    apply_k(p, s, coef, mask, 4)
+    apply_k(s, p, coef, mask, 3)
+
+    def to_w2(z, at, a0, a1):
         s0[at] = C0 * q0[at] + (C1 / SQ) * s0[at] + (C2 / SQ**2) * a0
         s1[at] = C0 * q1[at] + (C1 / SQ) * s1[at] + (C2 / SQ**2) * a1
 
-    apply_k(p, None, coef, mask, *span(2), finish=to_w2)
-    apply_k(s, p, coef, mask, *span(1))
+    apply_k(p, None, coef, mask, 2, finish=to_w2)
+    apply_k(s, p, coef, mask, 1)
     acc[...] = jnp.zeros((4, G, NX), f32)
 
-    def to_w3(z, n, a0, a1):
-        at, to = rows_of(z, n), block_rows(z, n)
-        w, u1, u2, u3 = (block_of(v, n) for v in (we[at], q0[at], s0[at], a0))
+    def to_w3(z, at, u3, _):
+        to = block_rows(z)
+        w, u1, u2 = we[at], q0[at], s0[at]
         v1_out[to] = u1
         v2_out[to] = u2
         v3_out[to] = u3
         for i, t in enumerate((r_ref[to] * w, w * u1, u1 * u2, u2 * u3)):
-            acc[i] += jnp.sum(t.reshape(n * NY // G, G, NX), axis=0)
-
-    apply_k(p, None, coef, mask, *span(0), finish=to_w3)
+            acc[i] += t[:G] + t[G:]
+
+    apply_k(p, None, coef, mask, 0, finish=to_w3)
     dots[...] = jnp.zeros((G, NX), f32)
     for i in range(4):
         dots[i : i + 1, :] = jnp.sum(acc[i], axis=0, keepdims=True)

time: 161 us -> 160 us (level)
  no operation moved by 1% of the time
where the time goes in v6:
time: 160 us; the launch traced here: 157 us
  starting transfers between devices  65.5 us (41%)
  blocking collectives  37.8 us (24%)
  waiting for transfers between devices  35.1 us (22%)
  Pallas kernels  18.2 us (11%)
    ppermute x16, starting transfers between devices, shift(): return lax.ppermute(x, axis, pairs)  65.5 us
    ppermute x16, waiting for transfers between devices, shift(): return lax.ppermute(x, axis, pairs)  35.1 us
    all_to_all x2, blocking collectives, all_sum(): x = jnp.sum(lax.all_to_all(copies, axis, 0, 0), axis=0)  27 us
    pallas_call x8, Pallas kernels, run(): pl.pallas_call(kernel, out_shape=[jax.ShapeDtypeStruct(s, f32) for s in o...  18.2 us
    psum x1, blocking collectives, all_sum(): return lax.psum(x, 'gz')  10.7 us
  transfers between devices with their start and end apart: 16, of which 8 were waited for; matrix products, arithmetic and copies ran while one was open for 0% of the time, Pallas kernels for 0%

profile of v6, /device:TPU:1, one launch (start us, length us, event | category | flops | bytes accessed | tf_op | source)
XLA Modules:
  0.0 157.5 jit_solution(10606866963754691534)
XLA Ops:
  0.6 0.0 copy-start.1
  0.6 0.0 copy-start.2
  0.6 1.4 shard_map.50
  2.0 0.0 copy-start
  2.1 4.5 %collective-permute-start.2 = (f32[544,128]{1,0:T(8,128)S(1)}, f32[544,128]{1,0:T(8,128)S(1)}, u32[]{:S(2)}, u32[]{:S(2)}) collective-permute-start(f32[544,128]{1,0:T(8,128)S(1)} %get-tuple-element.36), channel_id=1, source_target_pairs={{0,4},{4,8},{8,12},{12,16},{16,20},{20,24},{24,28},{28,32},{32,36}... | collective-permute-start | bytes 835592 | tf_op jit(solution)/shard_map/ppermute | solution.py:80
  6.6 1.3 collective-permute-start.3
  7.9 8.8 %collective-permute-start = (f32[272,128]{1,0:T(8,128)S(1)}, f32[272,128]{1,0:T(8,128)S(1)}, u32[]{:S(2)}, u32[]{:S(2)}) collective-permute-start(f32[272,128]{1,0:T(8,128)S(1)} %get-tuple-element.34), channel_id=1, source_target_pairs={{0,1},{1,2},{2,3},{4,5},{5,6},{6,7},{8,9},{9,10},{10,11},{12,13},{... | collective-permute-start | bytes 417800 | tf_op jit(solution)/shard_map/ppermute | solution.py:80
  16.7 1.3 collective-permute-start.1
  18.0 0.7 collective-permute-done.lo_ref.zlo
  18.7 8.7 %collective-permute-done.1.hi_ref.zhi = f32[272,128]{1,0:T(8,128)S(1)} collective-permute-done((f32[272,128]{1,0:T(8,128)S(1)}, f32[272,128]{1,0:T(8,128)S(1)}, u32[]{:S(2)}, u32[]{:S(2)}) %collective-permute-start.1) | collective-permute-done | bytes 139296 | tf_op jit(solution)/shard_map/ppermute | solution.py:80
  27.5 15.7 %collective-permute-start.4 = (f32[88,128]{1,0:T(8,128)S(1)}, f32[88,128]{1,0:T(8,128)S(1)}, u32[]{:S(2)}, u32[]{:S(2)}) collective-permute-start(f32[88,128]{1,0:T(8,128)S(1)} %get-tuple-element.38), channel_id=1, source_target_pairs={{0,4},{4,8},{8,12},{12,16},{16,20},{20,24},{24,28},{28,32},{32,36}... | collective-permute-start | bytes 135176 | tf_op jit(solution)/shard_map/ppermute | solution.py:80
  43.1 1.3 collective-permute-start.5
  44.4 0.0 collective-permute-done.4.clo
  44.5 3.5 %collective-permute-done.5.chi = f32[88,128]{1,0:T(8,128)S(1)} collective-permute-done((f32[88,128]{1,0:T(8,128)S(1)}, f32[88,128]{1,0:T(8,128)S(1)}, u32[]{:S(2)}, u32[]{:S(2)}) %collective-permute-start.5) | collective-permute-done | bytes 45088 | tf_op jit(solution)/shard_map/ppermute | solution.py:80
  47.9 0.0 collective-permute-done.2.ylo
  47.9 0.0 collective-permute-done.3.yhi
  47.9 0.0 copy-done.1
  47.9 0.0 copy-done.2
  48.0 0.0 copy-done
  48.0 0.8 shard_map.52
  48.8 5.5 %collective-permute-start.6 = (f32[288,128]{1,0:T(8,128)S(1)}, f32[288,128]{1,0:T(8,128)S(1)}, u32[]{:S(2)}, u32[]{:S(2)}) collective-permute-start(f32[288,128]{1,0:T(8,128)S(1)} %get-tuple-element.43), channel_id=1, source_target_pairs={{0,64},{64,128},{128,192},{192,256},{256,320},{320,384},{384,448},... | collective-permute-start | bytes 442376 | tf_op jit(solution)/shard_map/ppermute | solution.py:80
  54.3 1.9 %collective-permute-start.7 = (f32[288,128]{1,0:T(8,128)S(1)}, f32[288,128]{1,0:T(8,128)S(1)}, u32[]{:S(2)}, u32[]{:S(2)}) collective-permute-start(f32[288,128]{1,0:T(8,128)S(1)} %get-tuple-element.44), channel_id=1, source_target_pairs={{64,0},{128,64},{192,128},{256,192},{320,256},{384,320},{448,384},... | collective-permute-start | bytes 442376 | tf_op jit(solution)/shard_map/ppermute | solution.py:80
  56.2 0.2 collective-permute-done.6.rest_1_
  56.4 4.4 %collective-permute-done.7.rest_2_ = f32[288,128]{1,0:T(8,128)S(1)} collective-permute-done((f32[288,128]{1,0:T(8,128)S(1)}, f32[288,128]{1,0:T(8,128)S(1)}, u32[]{:S(2)}, u32[]{:S(2)}) %collective-permute-start.7) | collective-permute-done | bytes 147488 | tf_op jit(solution)/shard_map/ppermute | solution.py:80
  60.8 6.1 %shard_map.53 = (f32[512,128]{1,0:T(8,128)S(1)}, f32[512,128]{1,0:T(8,128)S(1)}, f32[128,128]{1,0:T(8,128)S(1)}, f32[128,128]{1,0:T(8,128)S(1)}, f32[256,128]{1,...) custom-call(f32[1536,128]{1,0:T(8,128)S(1)} %get-tuple-element.40.xe, ...), custom_call_target="tpu_custom_call" | custom-call | tf_op jit(solution)/shard_map/pallas_call | solution.py:67
  66.9 2.0 %collective-permute-start.10 = (f32[256,128]{1,0:T(8,128)S(1)}, f32[256,128]{1,0:T(8,128)S(1)}, u32[]{:S(2)}, u32[]{:S(2)}) collective-permute-start(f32[256,128]{1,0:T(8,128)S(1)} %get-tuple-element.49), channel_id=1, source_target_pairs={{0,4},{4,8},{8,12},{12,16},{16,20},{20,24},{24,28},{28,32},{32,36}... | collective-permute-start | bytes 393224 | tf_op jit(solution)/shard_map/ppermute | solution.py:80
  68.9 1.3 collective-permute-start.11
  70.2 7.0 %collective-permute-start.8 = (f32[128,128]{1,0:T(8,128)S(1)}, f32[128,128]{1,0:T(8,128)S(1)}, u32[]{:S(2)}, u32[]{:S(2)}) collective-permute-start(f32[128,128]{1,0:T(8,128)S(1)} %get-tuple-element.47), channel_id=1, source_target_pairs={{0,1},{1,2},{2,3},{4,5},{5,6},{6,7},{8,9},{9,10},{10,11},{12,13},{... | collective-permute-start | bytes 196616 | tf_op jit(solution)/shard_map/ppermute | solution.py:80
  77.2 1.3 collective-permute-start.9
  78.5 0.0 collective-permute-done.8.lo_ref.zlo
  78.5 7.6 %collective-permute-done.9.hi_ref.zhi = f32[128,128]{1,0:T(8,128)S(1)} collective-permute-done((f32[128,128]{1,0:T(8,128)S(1)}, f32[128,128]{1,0:T(8,128)S(1)}, u32[]{:S(2)}, u32[]{:S(2)}) %collective-permute-start.9) | collective-permute-done | bytes 65568 | tf_op jit(solution)/shard_map/ppermute | solution.py:80
  86.2 5.7 %collective-permute-start.12 = (f32[56,128]{1,0:T(8,128)S(1)}, f32[56,128]{1,0:T(8,128)S(1)}, u32[]{:S(2)}, u32[]{:S(2)}) collective-permute-start(f32[56,128]{1,0:T(8,128)S(1)} %get-tuple-element.51), channel_id=1, source_target_pairs={{0,4},{4,8},{8,12},{12,16},{16,20},{20,24},{24,28},{28,32},{32,36}... | collective-permute-start | bytes 86024 | tf_op jit(solution)/shard_map/ppermute | solution.py:80
  91.9 1.3 collective-permute-start.13
  93.2 0.0 collective-permute-done.12.clo
  93.2 6.5 %collective-permute-done.13.chi = f32[56,128]{1,0:T(8,128)S(1)} collective-permute-done((f32[56,128]{1,0:T(8,128)S(1)}, f32[56,128]{1,0:T(8,128)S(1)}, u32[]{:S(2)}, u32[]{:S(2)}) %collective-permute-start.13) | collective-permute-done | bytes 28704 | tf_op jit(solution)/shard_map/ppermute | solution.py:80
  99.7 0.0 collective-permute-done.10.ylo
  99.7 0.0 collective-permute-done.11.yhi
  99.7 0.4 shard_map.55
  100.1 4.8 %collective-permute-start.14 = (f32[96,128]{1,0:T(8,128)S(1)}, f32[96,128]{1,0:T(8,128)S(1)}, u32[]{:S(2)}, u32[]{:S(2)}) collective-permute-start(f32[96,128]{1,0:T(8,128)S(1)} %get-tuple-element.54), channel_id=1, source_target_pairs={{0,64},{64,128},{128,192},{192,256},{256,320},{320,384},{384,448},... | collective-permute-start | bytes 147464 | tf_op jit(solution)/shard_map/ppermute | solution.py:80
  104.9 1.9 %collective-permute-start.15 = (f32[96,128]{1,0:T(8,128)S(1)}, f32[96,128]{1,0:T(8,128)S(1)}, u32[]{:S(2)}, u32[]{:S(2)}) collective-permute-start(f32[96,128]{1,0:T(8,128)S(1)} %get-tuple-element.55), channel_id=1, source_target_pairs={{64,0},{128,64},{192,128},{256,192},{320,256},{384,320},{448,384},... | collective-permute-start | bytes 147464 | tf_op jit(solution)/shard_map/ppermute | solution.py:80
  106.8 0.0 collective-permute-done.14.lo
  106.8 3.5 %collective-permute-done.15.hi = f32[96,128]{1,0:T(8,128)S(1)} collective-permute-done((f32[96,128]{1,0:T(8,128)S(1)}, f32[96,128]{1,0:T(8,128)S(1)}, u32[]{:S(2)}, u32[]{:S(2)}) %collective-permute-start.15) | collective-permute-done | bytes 49184 | tf_op jit(solution)/shard_map/ppermute | solution.py:80
  110.3 8.4 %shard_map.56 = (f32[512,128]{1,0:T(8,128)S(1)}, f32[512,128]{1,0:T(8,128)S(1)}, f32[512,128]{1,0:T(8,128)S(1)}, f32[8,128]{1,0:T(8,128)S(1)}) custom-call(f32[1536,128]{1,0:T(8,128)S(1)} %get-tuple-element.53.we, f32[96,128]{1,0:T(8,128)S(1)} %collective-permute-done.14.lo, f32[96,128]{1,0:T(8,128)S(1)} %collective-permute-done.15.hi, ...), custom_call_target="tpu_custom_call" | custom-call | tf_op jit(solution)/shard_map/pallas_call | solution.py:67
  118.7 8.8 %all_to_all.10 = f32[8,8,128]{2,1,0:T(8,128)S(1)} all-to-all(f32[8,8,128]{2,1,0:T(8,128)S(1)} %broadcast_in_dim.4), channel_id=1, replica_groups=mesh['gx'=8,'gy'=16,'gz'=4] {'gx'}, dimensions={0} | all-to-all | bytes 65536 | tf_op jit(solution)/shard_map/all_to_all | solution.py:363
  127.5 18.2 %all_to_all.11 = f32[16,8,128]{2,1,0:T(8,128)S(1)} all-to-all(f32[16,8,128]{2,1,0:T(8,128)S(1)} %broadcast_in_dim.5), channel_id=1, replica_groups=mesh['gx'=8,'gy'=16,'gz'=4] {'gy'}, dimensions={0} | all-to-all | bytes 131072 | tf_op jit(solution)/shard_map/all_to_all | solution.py:363
  145.8 10.7 %psum.7.dots = f32[8,128]{1,0:T(8,128)S(1)} all-reduce(f32[8,128]{1,0:T(8,128)S(1)} %reduce_sum.19), channel_id=1, replica_groups=mesh['gx'=8,'gy'=16,'gz'=4] {'gz'}, use_global_device_ids=true, to_apply=%region_2.0 | all-reduce | flops 1024 | bytes 8192 | tf_op jit(solution)/shard_map/psum | solution.py:364
  156.5 1.0 shard_map.57
  (6 shorter events, 0.1 us)
Async XLA Ops:
  0.6 47.3 %copy-start.1 = (f32[32,16,128]{2,1,0:T(8,128)S(1)}, f32[32,16,128]{2,1,0:T(8,128)}, u32[]{:S(2)}) copy-start(f32[32,16,128]{2,1,0:T(8,128)} %param.3) | copy-start | bytes 786436
  0.6 47.3 %copy-start.2 = (f32[32,16,128]{2,1,0:T(8,128)S(1)}, f32[32,16,128]{2,1,0:T(8,128)}, u32[]{:S(2)}) copy-start(f32[32,16,128]{2,1,0:T(8,128)} %param.5) | copy-start | bytes 786436
  2.0 45.9 %copy-start = (f32[32,16,128]{2,1,0:T(8,128)S(1)}, f32[32,16,128]{2,1,0:T(8,128)}, u32[]{:S(2)}) copy-start(f32[32,16,128]{2,1,0:T(8,128)} %param.4) | copy-start | bytes 786436
  2.1 45.9 %collective-permute-start.2 = (f32[544,128]{1,0:T(8,128)S(1)}, f32[544,128]{1,0:T(8,128)S(1)}, u32[]{:S(2)}, u32[]{:S(2)}) collective-permute-start(f32[544,128]{1,0:T(8,128)S(1)} %get-tuple-element.36), channel_id=1, source_target_pairs={{0,4},{4,8},{8,12},{12,16},{16,20},{20,24},{24,28},{28,32},{32,36}... | collective-permute-start | bytes 835592 | tf_op jit(solution)/shard_map/ppermute | solution.py:80
  6.6 41.4 %collective-permute-start.3 = (f32[544,128]{1,0:T(8,128)S(1)}, f32[544,128]{1,0:T(8,128)S(1)}, u32[]{:S(2)}, u32[]{:S(2)}) collective-permute-start(f32[544,128]{1,0:T(8,128)S(1)} %get-tuple-element.37), channel_id=1, source_target_pairs={{4,0},{8,4},{12,8},{16,12},{20,16},{24,20},{28,24},{32,28},{36,32}... | collective-permute-start | bytes 835592 | tf_op jit(solution)/shard_map/ppermute | solution.py:80
  7.9 10.8 %collective-permute-start = (f32[272,128]{1,0:T(8,128)S(1)}, f32[272,128]{1,0:T(8,128)S(1)}, u32[]{:S(2)}, u32[]{:S(2)}) collective-permute-start(f32[272,128]{1,0:T(8,128)S(1)} %get-tuple-element.34), channel_id=1, source_target_pairs={{0,1},{1,2},{2,3},{4,5},{5,6},{6,7},{8,9},{9,10},{10,11},{12,13},{... | collective-permute-start | bytes 417800 | tf_op jit(solution)/shard_map/ppermute | solution.py:80
  16.7 10.7 %collective-permute-start.1 = (f32[272,128]{1,0:T(8,128)S(1)}, f32[272,128]{1,0:T(8,128)S(1)}, u32[]{:S(2)}, u32[]{:S(2)}) collective-permute-start(f32[272,128]{1,0:T(8,128)S(1)} %get-tuple-element.35), channel_id=1, source_target_pairs={{1,0},{2,1},{3,2},{5,4},{6,5},{7,6},{9,8},{10,9},{11,10},{13,12},{... | collective-permute-start | bytes 417800 | tf_op jit(solution)/shard_map/ppermute | solution.py:80
  27.5 17.0 %collective-permute-start.4 = (f32[88,128]{1,0:T(8,128)S(1)}, f32[88,128]{1,0:T(8,128)S(1)}, u32[]{:S(2)}, u32[]{:S(2)}) collective-permute-start(f32[88,128]{1,0:T(8,128)S(1)} %get-tuple-element.38), channel_id=1, source_target_pairs={{0,4},{4,8},{8,12},{12,16},{16,20},{20,24},{24,28},{28,32},{32,36}... | collective-permute-start | bytes 135176 | tf_op jit(solution)/shard_map/ppermute | solution.py:80
  43.1 4.8 %collective-permute-start.5 = (f32[88,128]{1,0:T(8,128)S(1)}, f32[88,128]{1,0:T(8,128)S(1)}, u32[]{:S(2)}, u32[]{:S(2)}) collective-permute-start(f32[88,128]{1,0:T(8,128)S(1)} %get-tuple-element.39), channel_id=1, source_target_pairs={{4,0},{8,4},{12,8},{16,12},{20,16},{24,20},{28,24},{32,28},{36,32}... | collective-permute-start | bytes 135176 | tf_op jit(solution)/shard_map/ppermute | solution.py:80
  48.8 7.6 %collective-permute-start.6 = (f32[288,128]{1,0:T(8,128)S(1)}, f32[288,128]{1,0:T(8,128)S(1)}, u32[]{:S(2)}, u32[]{:S(2)}) collective-permute-start(f32[288,128]{1,0:T(8,128)S(1)} %get-tuple-element.43), channel_id=1, source_target_pairs={{0,64},{64,128},{128,192},{192,256},{256,320},{320,384},{384,448},... | collective-permute-start | bytes 442376 | tf_op jit(solution)/shard_map/ppermute | solution.py:80
  54.3 6.5 %collective-permute-start.7 = (f32[288,128]{1,0:T(8,128)S(1)}, f32[288,128]{1,0:T(8,128)S(1)}, u32[]{:S(2)}, u32[]{:S(2)}) collective-permute-start(f32[288,128]{1,0:T(8,128)S(1)} %get-tuple-element.44), channel_id=1, source_target_pairs={{64,0},{128,64},{192,128},{256,192},{320,256},{384,320},{448,384},... | collective-permute-start | bytes 442376 | tf_op jit(solution)/shard_map/ppermute | solution.py:80
  66.9 32.8 %collective-permute-start.10 = (f32[256,128]{1,0:T(8,128)S(1)}, f32[256,128]{1,0:T(8,128)S(1)}, u32[]{:S(2)}, u32[]{:S(2)}) collective-permute-start(f32[256,128]{1,0:T(8,128)S(1)} %get-tuple-element.49), channel_id=1, source_target_pairs={{0,4},{4,8},{8,12},{12,16},{16,20},{20,24},{24,28},{28,32},{32,36}... | collective-permute-start | bytes 393224 | tf_op jit(solution)/shard_map/ppermute | solution.py:80
  68.9 30.8 %collective-permute-start.11 = (f32[256,128]{1,0:T(8,128)S(1)}, f32[256,128]{1,0:T(8,128)S(1)}, u32[]{:S(2)}, u32[]{:S(2)}) collective-permute-start(f32[256,128]{1,0:T(8,128)S(1)} %get-tuple-element.50), channel_id=1, source_target_pairs={{4,0},{8,4},{12,8},{16,12},{20,16},{24,20},{28,24},{32,28},{36,32}... | collective-permute-start | bytes 393224 | tf_op jit(solution)/shard_map/ppermute | solution.py:80
  70.2 8.3 %collective-permute-start.8 = (f32[128,128]{1,0:T(8,128)S(1)}, f32[128,128]{1,0:T(8,128)S(1)}, u32[]{:S(2)}, u32[]{:S(2)}) collective-permute-start(f32[128,128]{1,0:T(8,128)S(1)} %get-tuple-element.47), channel_id=1, source_target_pairs={{0,1},{1,2},{2,3},{4,5},{5,6},{6,7},{8,9},{9,10},{10,11},{12,13},{... | collective-permute-start | bytes 196616 | tf_op jit(solution)/shard_map/ppermute | solution.py:80
  77.2 8.9 %collective-permute-start.9 = (f32[128,128]{1,0:T(8,128)S(1)}, f32[128,128]{1,0:T(8,128)S(1)}, u32[]{:S(2)}, u32[]{:S(2)}) collective-permute-start(f32[128,128]{1,0:T(8,128)S(1)} %get-tuple-element.48), channel_id=1, source_target_pairs={{1,0},{2,1},{3,2},{5,4},{6,5},{7,6},{9,8},{10,9},{11,10},{13,12},{... | collective-permute-start | bytes 196616 | tf_op jit(solution)/shard_map/ppermute | solution.py:80
  86.2 7.0 %collective-permute-start.12 = (f32[56,128]{1,0:T(8,128)S(1)}, f32[56,128]{1,0:T(8,128)S(1)}, u32[]{:S(2)}, u32[]{:S(2)}) collective-permute-start(f32[56,128]{1,0:T(8,128)S(1)} %get-tuple-element.51), channel_id=1, source_target_pairs={{0,4},{4,8},{8,12},{12,16},{16,20},{20,24},{24,28},{28,32},{32,36}... | collective-permute-start | bytes 86024 | tf_op jit(solution)/shard_map/ppermute | solution.py:80
  91.9 7.8 %collective-permute-start.13 = (f32[56,128]{1,0:T(8,128)S(1)}, f32[56,128]{1,0:T(8,128)S(1)}, u32[]{:S(2)}, u32[]{:S(2)}) collective-permute-start(f32[56,128]{1,0:T(8,128)S(1)} %get-tuple-element.52), channel_id=1, source_target_pairs={{4,0},{8,4},{12,8},{16,12},{20,16},{24,20},{28,24},{32,28},{36,32}... | collective-permute-start | bytes 86024 | tf_op jit(solution)/shard_map/ppermute | solution.py:80
  100.1 6.7 %collective-permute-start.14 = (f32[96,128]{1,0:T(8,128)S(1)}, f32[96,128]{1,0:T(8,128)S(1)}, u32[]{:S(2)}, u32[]{:S(2)}) collective-permute-start(f32[96,128]{1,0:T(8,128)S(1)} %get-tuple-element.54), channel_id=1, source_target_pairs={{0,64},{64,128},{128,192},{192,256},{256,320},{320,384},{384,448},... | collective-permute-start | bytes 147464 | tf_op jit(solution)/shard_map/ppermute | solution.py:80
  104.9 5.4 %collective-permute-start.15 = (f32[96,128]{1,0:T(8,128)S(1)}, f32[96,128]{1,0:T(8,128)S(1)}, u32[]{:S(2)}, u32[]{:S(2)}) collective-permute-start(f32[96,128]{1,0:T(8,128)S(1)} %get-tuple-element.55), channel_id=1, source_target_pairs={{64,0},{128,64},{192,128},{256,192},{320,256},{384,320},{448,384},... | collective-permute-start | bytes 147464 | tf_op jit(solution)/shard_map/ppermute | solution.py:80

commit v7 on v6

--- a/solution.py
+++ b/solution.py
@@ -86,7 +86,26 @@
     return from_below, from_above
 
 
-def pack_block(x_hbm, b_hbm, k_hbm, zdn, zup, ydn, yup, x_ref, b_ref, k_ref, sems):
+def swap(mine_a, mine_b, axis):
+    n = lax.axis_size(axis)
+    a = lax.ppermute(mine_a, axis, [(i, i ^ 1) for i in range(n)])
+    b = lax.ppermute(mine_b, axis, [(i, i + 1 if i % 2 else i - 1) for i in range(1, n - 1)])
+    return a, b
+
+
+def is_even(axis):
+    return lax.axis_index(axis) % 2 == 0
+
+
+def place(even, dn, up):
+    return jnp.where(even, up, dn), jnp.where(even, dn, up)
+
+
+def sides(even, a, b):
+    return jnp.where(even, b, a), jnp.where(even, a, b)
+
+
+def pack_block(x_hbm, b_hbm, k_hbm, zdn, zup, ya, yb, x_ref, b_ref, k_ref, sems):
     fields = (x_ref, b_ref, k_ref)
     copies = [
         pltpu.make_async_copy(src, dst, sems.at[i])
@@ -101,23 +120,24 @@
         at = OFFS[f] * NY
         zdn[at : at + n, :] = field[0:n, :]
         zup[at : at + n, :] = field[NZ * NY - n : NZ * NY, :]
+    even = is_even("gy")
     for i, (f, t) in enumerate(PIECES):
-        for out, row in ((ydn, t - 1), (yup, NY - t)):
-            out[i * NZ : (i + 1) * NZ, :] = fields[f][pl.ds(row, NZ, stride=NY), :]
-
-
-def pack_corners(lo_ref, hi_ref, dn_ref, up_ref):
+        dn, up = (fields[f][pl.ds(row, NZ, stride=NY), :] for row in (t - 1, NY - t))
+        ya[i * NZ : (i + 1) * NZ, :], yb[i * NZ : (i + 1) * NZ, :] = place(even, dn, up)
+
+
+def pack_corners(lo_ref, hi_ref, a_ref, b_ref):
+    even = is_even("gy")
     for f, t in PIECES:
         d, n = DEPTHS[f], DEPTHS[f] - t
-        for out, row in ((dn_ref, t - 1), (up_ref, NY - t)):
+        for side, ref, first in ((0, lo_ref, OFFS[f] + d - n), (1, hi_ref, OFFS[f])):
             if n:
-                at = CORNERS[f, t, 0]
-                out[at : at + n, :] = lo_ref[pl.ds((OFFS[f] + d - n) * NY + row, n, stride=NY), :]
-                at = CORNERS[f, t, 1]
-                out[at : at + n, :] = hi_ref[pl.ds(OFFS[f] * NY + row, n, stride=NY), :]
-
-
-def pack_lanes(read, dn_ref, up_ref, base):
+                at = CORNERS[f, t, side]
+                dn, up = (ref[pl.ds(first * NY + row, n, stride=NY), :] for row in (t - 1, NY - t))
+                a_ref[at : at + n, :], b_ref[at : at + n, :] = place(even, dn, up)
+
+
+def pack_lanes(read, a_ref, b_ref, base):
     group = lax.broadcasted_iota(jnp.int32, (FY, NX), 1) // G
     for q in range(FZ // 16):
         dn = jnp.zeros((FY, NX), f32)
@@ -127,21 +147,27 @@
             a = v if g == 0 else pltpu.roll(v, G * g, 1)
             dn = jnp.where(group == g, a, dn)
             up = jnp.where(group == (g - 1) % 16, a, up)
-        dn_ref[base + q * FY : base + (q + 1) * FY, :] = dn
-        up_ref[base + q * FY : base + (q + 1) * FY, :] = up
-
-
-def unpack_lanes(lo_ref, hi_ref, base, write):
+        at = slice(base + q * FY, base + (q + 1) * FY)
+        a_ref[at, :], b_ref[at, :] = place(is_even("gx"), dn, up)
+
+
+def unpack_lanes(a_ref, b_ref, base, write):
     group = lax.broadcasted_iota(jnp.int32, (FY, NX), 1) // G
     for q in range(FZ // 16):
-        lo = lo_ref[base + q * FY : base + (q + 1) * FY, :]
-        hi = hi_ref[base + q * FY : base + (q + 1) * FY, :]
+        at = slice(base + q * FY, base + (q + 1) * FY)
+        lo, hi = sides(is_even("gx"), a_ref[at, :], b_ref[at, :])
         for g in range(16):
             v = jnp.where(group == g, hi, lo)
             write(16 * q + g, v if g == 0 else pltpu.roll(v, NX - G * g, 1))
 
 
-def frame(x_ref, b_ref, k_ref, zlo, zhi, ylo, yhi, clo, chi, xe, be, ke, dn_ref, up_ref):
+def put_rows(out, t, first, n, lo_hi):
+    for rows, row in zip(lo_hi, (G - t, G + NY + t - 1)):
+        out[pl.ds(first * FY + row, n, stride=FY), :] = rows
+
+
+def frame(x_ref, b_ref, k_ref, zlo, zhi, ya, yb, ca, cb, xe, be, ke, dn_ref, up_ref):
+    even = is_even("gy")
     fields = (x_ref, b_ref, k_ref)
     for f, out in enumerate((xe, be, ke)):
         d = DEPTHS[f]
@@ -157,13 +183,11 @@
             out[at : at + NY, :] = zhi[src : src + NY, :]
         for t in range(1, d + 1):
             i, n = OFFS[f] + t - 1, d - t
-            for src, corner, row in ((ylo, clo, G - t), (yhi, chi, G + NY + t - 1)):
-                out[pl.ds(G * FY + row, NZ, stride=FY), :] = src[i * NZ : (i + 1) * NZ, :]
+            put_rows(out, t, G, NZ, sides(even, ya[i * NZ : (i + 1) * NZ, :], yb[i * NZ : (i + 1) * NZ, :]))
+            for side, first in ((0, G - n), (1, G + NZ)):
                 if n:
-                    at = CORNERS[f, t, 0]
-                    out[pl.ds((G - n) * FY + row, n, stride=FY), :] = corner[at : at + n, :]
-                    at = CORNERS[f, t, 1]
-                    out[pl.ds((G + NZ) * FY + row, n, stride=FY), :] = corner[at : at + n, :]
+                    at = CORNERS[f, t, side]
+                    put_rows(out, t, first, n, sides(even, ca[at : at + n, :], cb[at : at + n, :]))
         pack_lanes(lambda z: out[z * FY : (z + 1) * FY, :], dn_ref, up_ref, f * Q_PACK)
 
 
@@ -229,7 +253,7 @@
     return pl.ds(pl.multiple_of((z - G) * NY, NY), NY)
 
 
-def first_stage(xe, be, ke, lo, hi, r_out, w_out, zdn, zup, ydn, yup, c0, c1, m0, m1, x1, b1, p0, p1, q0, q1):
+def first_stage(xe, be, ke, lo, hi, r_out, w_out, zdn, zup, ya, yb, c0, c1, m0, m1, x1, b1, p0, p1, q0, q1):
     def put(ref):
         def write(z, v):
             ref[z * FY : (z + 1) * FY] = v
@@ -269,21 +293,22 @@
     zdn[...] = w_out[0 : G * NY]
     zup[...] = w_out[(NZ - G) * NY : NZ * NY]
     for t in range(1, G + 1):
-        ydn[(t - 1) * NZ : t * NZ, :] = w_out[pl.ds(t - 1, NZ, stride=NY), :]
-        yup[(t - 1) * NZ : t * NZ, :] = w_out[pl.ds(NY - t, NZ, stride=NY), :]
-
-
-def pack_corners2(lo_ref, hi_ref, dn_ref, up_ref):
+        dn, up = (w_out[pl.ds(row, NZ, stride=NY), :] for row in (t - 1, NY - t))
+        ya[(t - 1) * NZ : t * NZ, :], yb[(t - 1) * NZ : t * NZ, :] = place(is_even("gy"), dn, up)
+
+
+def pack_corners2(lo_ref, hi_ref, a_ref, b_ref):
+    even = is_even("gy")
     for t in range(1, G):
         n = G - t
-        for out, row in ((dn_ref, t - 1), (up_ref, NY - t)):
-            at = CORNERS2[0, t, 0]
-            out[at : at + n, :] = lo_ref[pl.ds(t * NY + row, n, stride=NY), :]
-            at = CORNERS2[0, t, 1]
-            out[at : at + n, :] = hi_ref[pl.ds(row, n, stride=NY), :]
-
-
-def frame2(w_ref, zlo, zhi, ylo, yhi, clo, chi, we, dn_ref, up_ref):
+        for side, ref, first in ((0, lo_ref, t), (1, hi_ref, 0)):
+            at = CORNERS2[0, t, side]
+            dn, up = (ref[pl.ds(first * NY + row, n, stride=NY), :] for row in (t - 1, NY - t))
+            a_ref[at : at + n, :], b_ref[at : at + n, :] = place(even, dn, up)
+
+
+def frame2(w_ref, zlo, zhi, ya, yb, ca, cb, we, dn_ref, up_ref):
+    even = is_even("gy")
     for z in range(FZ):
         at = z * FY
         src, k = (zlo, z) if z < G else (w_ref, z - G) if z < G + NZ else (zhi, z - G - NZ)
@@ -293,13 +318,11 @@
             we[at + G + NY : at + FY, :] = jnp.zeros((G, NX), f32)
     for t in range(1, G + 1):
         n = G - t
-        for src, corner, row in ((ylo, clo, G - t), (yhi, chi, G + NY + t - 1)):
-            we[pl.ds(G * FY + row, NZ, stride=FY), :] = src[(t - 1) * NZ : t * NZ, :]
+        put_rows(we, t, G, NZ, sides(even, ya[(t - 1) * NZ : t * NZ, :], yb[(t - 1) * NZ : t * NZ, :]))
+        for side, first in ((0, G - n), (1, G + NZ)):
             if n:
-                at = CORNERS2[0, t, 0]
-                we[pl.ds((G - n) * FY + row, n, stride=FY), :] = corner[at : at + n, :]
-                at = CORNERS2[0, t, 1]
-                we[pl.ds((G + NZ) * FY + row, n, stride=FY), :] = corner[at : at + n, :]
+                at = CORNERS2[0, t, side]
+                put_rows(we, t, first, n, sides(even, ca[at : at + n, :], cb[at : at + n, :]))
     pack_lanes(lambda z: we[z * FY : (z + 1) * FY, :], dn_ref, up_ref, 0)
 
 
@@ -366,7 +389,7 @@
 
 def solve(right_side, initial, kappa_sq):
     flat = [v.reshape(NZ * NY, NX) for v in (initial, right_side, kappa_sq)]
-    zdn, zup, ydn, yup = run(
+    zdn, zup, ya, yb = run(
         pack_block,
         [(LAYERS * NY, NX)] * 2 + [(MAIN_ROWS, NX)] * 2,
         [pltpu.with_memory_space_constraint(v, pltpu.HBM) for v in flat],
@@ -374,12 +397,12 @@
         space=pltpu.HBM,
     )
     zlo, zhi = exchange(zdn, zup, "gz")
-    ylo, yhi = exchange(ydn, yup, "gy")
-    down, up = run(pack_corners, [(CORNER_ROWS, NX)] * 2, (zlo, zhi))
-    clo, chi = exchange(down, up, "gy")
+    ya, yb = swap(ya, yb, "gy")
+    a, b = run(pack_corners, [(CORNER_ROWS, NX)] * 2, (zlo, zhi))
+    ca, cb = swap(a, b, "gy")
     frame_shape = (FZ * FY, NX)
-    xe, be, ke, down, up = run(frame, [frame_shape] * 3 + [(3 * Q_PACK, NX)] * 2, (*flat, zlo, zhi, ylo, yhi, clo, chi))
-    xlo, xhi = exchange(down, up, "gx")
+    xe, be, ke, a, b = run(frame, [frame_shape] * 3 + [(3 * Q_PACK, NX)] * 2, (*flat, zlo, zhi, ya, yb, ca, cb))
+    xa, xb = swap(a, b, "gx")
     tile = pltpu.VMEM(frame_shape, f32)
     block = (NZ * NY, NX)
     slab = (G * NY, NX)
@@ -389,22 +412,22 @@
         be[...] = be_in[...]
         first_stage(xe, be, *rest[:-1])
 
-    r0, w0, zdn, zup, ydn, yup, c0, c1, m0, m1 = run(
+    r0, w0, zdn, zup, ya, yb, c0, c1, m0, m1 = run(
         stage1,
         [block, block, slab, slab, (MAIN_ROWS2, NX), (MAIN_ROWS2, NX), frame_shape, frame_shape, frame_shape, frame_shape],
-        (xe, be, ke, xlo, xhi),
+        (xe, be, ke, xa, xb),
         scratch=[tile] * 7,
     )
     zlo, zhi = exchange(zdn, zup, "gz")
-    ylo, yhi = exchange(ydn, yup, "gy")
-    down, up = run(pack_corners2, [(CORNER_ROWS2, NX)] * 2, (zlo, zhi))
-    clo, chi = exchange(down, up, "gy")
-    we, down, up = run(frame2, [frame_shape, (Q_PACK, NX), (Q_PACK, NX)], (w0, zlo, zhi, ylo, yhi, clo, chi))
-    xlo, xhi = exchange(down, up, "gx")
+    ya, yb = swap(ya, yb, "gy")
+    a, b = run(pack_corners2, [(CORNER_ROWS2, NX)] * 2, (zlo, zhi))
+    ca, cb = swap(a, b, "gy")
+    we, a, b = run(frame2, [frame_shape, (Q_PACK, NX), (Q_PACK, NX)], (w0, zlo, zhi, ya, yb, ca, cb))
+    xa, xb = swap(a, b, "gx")
     v1, v2, v3, dots = run(
         second_stage,
         [block, block, block, (G, NX)],
-        (we, xlo, xhi, r0, c0, c1, m0, m1),
+        (we, xa, xb, r0, c0, c1, m0, m1),
         scratch=[pltpu.VMEM((4, G, NX), f32)] + [tile] * 7,
     )
     dots = all_sum(dots)

time: 160 us -> 158 us (0.988)
  waiting for transfers between devices: 35.1 us -> 23.5 us
  starting transfers between devices: 65.5 us -> 71.8 us
  blocking collectives: 37.8 us -> 41.6 us
    ppermute x0 -> x12, starting transfers between devices: none -> 53.7 us  [the longest x6 41.8 us: swap(): a = lax.ppermute(mine_a, axis, [(i, i ^ 1) for i in range(n)])]
    ppermute x16 -> x4, starting transfers between devices: 65.5 us -> 18.1 us  [shift(): return lax.ppermute(x, axis, pairs)]
    ppermute x16 -> x4, waiting for transfers between devices: 35.1 us -> 17 us  [shift(): return lax.ppermute(x, axis, pairs)]
    ppermute x0 -> x12, waiting for transfers between devices: none -> 6.43 us  [the longest x6 5.1 us: swap(): lax.ppermute(mine_b, axis, [(i, i + 1 if i % 2 else i - 1) for i in range...]
    all_to_all x2, blocking collectives: 27 us -> 30.9 us  [all_sum(): x = jnp.sum(lax.all_to_all(copies, axis, 0, 0), axis=0)]
  transfers between devices with their start and end apart: 16 -> 16, of which waited for: 8 -> 7; matrix products, arithmetic and copies ran while one was open for 0% -> 0% of each run, Pallas kernels for 0% -> 0%
where the time goes in v7:
time: 158 us; the launch traced here: 156 us
  starting transfers between devices  71.8 us (45%)
  blocking collectives  41.6 us (26%)
  waiting for transfers between devices  23.5 us (15%)
  Pallas kernels  18.3 us (12%)
    ppermute x6, starting transfers between devices, swap(): a = lax.ppermute(mine_a, axis, [(i, i ^ 1) for i in range(n)])  41.8 us
    all_to_all x2, blocking collectives, all_sum(): x = jnp.sum(lax.all_to_all(copies, axis, 0, 0), axis=0)  30.9 us
    pallas_call x8, Pallas kernels, run(): pl.pallas_call(kernel, out_shape=[jax.ShapeDtypeStruct(s, f32) for s in o...  18.3 us
    ppermute x4, starting transfers between devices, shift(): return lax.ppermute(x, axis, pairs)  18.1 us
    ppermute x4, waiting for transfers between devices, shift(): return lax.ppermute(x, axis, pairs)  17 us
    ppermute x6, starting transfers between devices, swap(): lax.ppermute(mine_b, axis, [(i, i + 1 if i % 2 else i - 1) for i in range...  11.8 us
    psum x1, blocking collectives, all_sum(): return lax.psum(x, 'gz')  10.7 us
    ppermute x6, waiting for transfers between devices, swap(): lax.ppermute(mine_b, axis, [(i, i + 1 if i % 2 else i - 1) for i in range...  5.1 us
  transfers between devices with their start and end apart: 16, of which 7 were waited for; matrix products, arithmetic and copies ran while one was open for 0% of the time, Pallas kernels for 0%

profile of v7, /device:TPU:1, one launch (start us, length us, event | category | flops | bytes accessed | tf_op | source)
XLA Modules:
  0.0 156.0 jit_solution(14444787390041703899)
XLA Ops:
  0.6 0.0 copy-start.1
  0.6 0.0 copy-start.2
  0.6 1.4 shard_map.50
  2.0 0.0 copy-start
  2.0 4.5 %collective-permute-start.2 = (f32[544,128]{1,0:T(8,128)S(1)}, f32[544,128]{1,0:T(8,128)S(1)}, u32[]{:S(2)}, u32[]{:S(2)}) collective-permute-start(f32[544,128]{1,0:T(8,128)S(1)} %get-tuple-element.36), channel_id=1, source_target_pairs={{0,4},{4,0},{8,12},{12,8},{16,20},{20,16},{24,28},{28,24},{32,36},... | collective-permute-start | bytes 835592 | tf_op jit(solution)/shard_map/ppermute | solution.py:91
  6.5 0.7 collective-permute-start.3
  7.2 8.8 %collective-permute-start = (f32[272,128]{1,0:T(8,128)S(1)}, f32[272,128]{1,0:T(8,128)S(1)}, u32[]{:S(2)}, u32[]{:S(2)}) collective-permute-start(f32[272,128]{1,0:T(8,128)S(1)} %get-tuple-element.34), channel_id=1, source_target_pairs={{0,1},{1,2},{2,3},{4,5},{5,6},{6,7},{8,9},{9,10},{10,11},{12,13},{... | collective-permute-start | bytes 417800 | tf_op jit(solution)/shard_map/ppermute | solution.py:80
  16.1 1.3 collective-permute-start.1
  17.4 0.7 collective-permute-done.lo_ref.zlo
  18.1 8.7 %collective-permute-done.1.hi_ref.zhi = f32[272,128]{1,0:T(8,128)S(1)} collective-permute-done((f32[272,128]{1,0:T(8,128)S(1)}, f32[272,128]{1,0:T(8,128)S(1)}, u32[]{:S(2)}, u32[]{:S(2)}) %collective-permute-start.1) | collective-permute-done | bytes 139296 | tf_op jit(solution)/shard_map/ppermute | solution.py:80
  26.8 11.9 %collective-permute-start.4 = (f32[88,128]{1,0:T(8,128)S(1)}, f32[88,128]{1,0:T(8,128)S(1)}, u32[]{:S(2)}, u32[]{:S(2)}) collective-permute-start(f32[88,128]{1,0:T(8,128)S(1)} %get-tuple-element.38), channel_id=1, source_target_pairs={{0,4},{4,0},{8,12},{12,8},{16,20},{20,16},{24,28},{28,24},{32,36},... | collective-permute-start | bytes 135176 | tf_op jit(solution)/shard_map/ppermute | solution.py:91
  38.7 0.7 collective-permute-start.5
  39.4 0.7 collective-permute-done.4.ca
  40.2 0.0 collective-permute-done.5.cb
  40.2 0.0 collective-permute-done.2.ya
  40.2 0.0 collective-permute-done.3.yb
  40.2 0.0 copy-done.1
  40.2 0.0 copy-done.2
  40.2 0.0 copy-done
  40.2 0.9 shard_map.52
  41.1 4.3 %collective-permute-start.6 = (f32[288,128]{1,0:T(8,128)S(1)}, f32[288,128]{1,0:T(8,128)S(1)}, u32[]{:S(2)}, u32[]{:S(2)}) collective-permute-start(f32[288,128]{1,0:T(8,128)S(1)} %get-tuple-element.43), channel_id=1, source_target_pairs={{0,64},{64,0},{128,192},{192,128},{256,320},{320,256},{384,448},{4... | collective-permute-start | bytes 442376 | tf_op jit(solution)/shard_map/ppermute | solution.py:91
  45.5 3.1 %collective-permute-start.7 = (f32[288,128]{1,0:T(8,128)S(1)}, f32[288,128]{1,0:T(8,128)S(1)}, u32[]{:S(2)}, u32[]{:S(2)}) collective-permute-start(f32[288,128]{1,0:T(8,128)S(1)} %get-tuple-element.44), channel_id=1, source_target_pairs={{64,128},{128,64},{192,256},{256,192},{320,384},{384,320},{65,129}... | collective-permute-start | bytes 442376 | tf_op jit(solution)/shard_map/ppermute | solution.py:92
  48.6 0.0 collective-permute-done.6.rest_1_
  48.6 3.3 %collective-permute-done.7.rest_2_ = f32[288,128]{1,0:T(8,128)S(1)} collective-permute-done((f32[288,128]{1,0:T(8,128)S(1)}, f32[288,128]{1,0:T(8,128)S(1)}, u32[]{:S(2)}, u32[]{:S(2)}) %collective-permute-start.7) | collective-permute-done | bytes 147488 | tf_op jit(solution)/shard_map/ppermute | solution.py:92
  52.0 6.1 %shard_map.53 = (f32[512,128]{1,0:T(8,128)S(1)}, f32[512,128]{1,0:T(8,128)S(1)}, f32[128,128]{1,0:T(8,128)S(1)}, f32[128,128]{1,0:T(8,128)S(1)}, f32[256,128]{1,...) custom-call(f32[1536,128]{1,0:T(8,128)S(1)} %get-tuple-element.40.xe, ...), custom_call_target="tpu_custom_call" | custom-call | tf_op jit(solution)/shard_map/pallas_call | solution.py:67
  58.1 9.8 %collective-permute-start.10 = (f32[256,128]{1,0:T(8,128)S(1)}, f32[256,128]{1,0:T(8,128)S(1)}, u32[]{:S(2)}, u32[]{:S(2)}) collective-permute-start(f32[256,128]{1,0:T(8,128)S(1)} %get-tuple-element.49), channel_id=1, source_target_pairs={{0,4},{4,0},{8,12},{12,8},{16,20},{20,16},{24,28},{28,24},{32,36},... | collective-permute-start | bytes 393224 | tf_op jit(solution)/shard_map/ppermute | solution.py:91
  67.9 0.7 collective-permute-start.11
  68.6 6.7 %collective-permute-start.8 = (f32[128,128]{1,0:T(8,128)S(1)}, f32[128,128]{1,0:T(8,128)S(1)}, u32[]{:S(2)}, u32[]{:S(2)}) collective-permute-start(f32[128,128]{1,0:T(8,128)S(1)} %get-tuple-element.47), channel_id=1, source_target_pairs={{0,1},{1,2},{2,3},{4,5},{5,6},{6,7},{8,9},{9,10},{10,11},{12,13},{... | collective-permute-start | bytes 196616 | tf_op jit(solution)/shard_map/ppermute | solution.py:80
  75.3 1.3 collective-permute-start.9
  76.6 0.0 collective-permute-done.8.lo_ref.zlo
  76.6 7.6 %collective-permute-done.9.hi_ref.zhi = f32[128,128]{1,0:T(8,128)S(1)} collective-permute-done((f32[128,128]{1,0:T(8,128)S(1)}, f32[128,128]{1,0:T(8,128)S(1)}, u32[]{:S(2)}, u32[]{:S(2)}) %collective-permute-start.9) | collective-permute-done | bytes 65568 | tf_op jit(solution)/shard_map/ppermute | solution.py:80
  84.3 9.3 %collective-permute-start.12 = (f32[56,128]{1,0:T(8,128)S(1)}, f32[56,128]{1,0:T(8,128)S(1)}, u32[]{:S(2)}, u32[]{:S(2)}) collective-permute-start(f32[56,128]{1,0:T(8,128)S(1)} %get-tuple-element.51), channel_id=1, source_target_pairs={{0,4},{4,0},{8,12},{12,8},{16,20},{20,16},{24,28},{28,24},{32,36},... | collective-permute-start | bytes 86024 | tf_op jit(solution)/shard_map/ppermute | solution.py:91
  93.6 0.7 collective-permute-start.13
  94.3 0.6 collective-permute-done.12.ca
  94.9 0.0 collective-permute-done.13.cb
  94.9 0.0 collective-permute-done.10.ya
  94.9 0.0 collective-permute-done.11.yb
  94.9 0.4 shard_map.55
  95.3 1.9 %collective-permute-start.14 = (f32[96,128]{1,0:T(8,128)S(1)}, f32[96,128]{1,0:T(8,128)S(1)}, u32[]{:S(2)}, u32[]{:S(2)}) collective-permute-start(f32[96,128]{1,0:T(8,128)S(1)} %get-tuple-element.54), channel_id=1, source_target_pairs={{0,64},{64,0},{128,192},{192,128},{256,320},{320,256},{384,448},{4... | collective-permute-start | bytes 147464 | tf_op jit(solution)/shard_map/ppermute | solution.py:91
  97.2 6.1 %collective-permute-start.15 = (f32[96,128]{1,0:T(8,128)S(1)}, f32[96,128]{1,0:T(8,128)S(1)}, u32[]{:S(2)}, u32[]{:S(2)}) collective-permute-start(f32[96,128]{1,0:T(8,128)S(1)} %get-tuple-element.55), channel_id=1, source_target_pairs={{64,128},{128,64},{192,256},{256,192},{320,384},{384,320},{65,129}... | collective-permute-start | bytes 147464 | tf_op jit(solution)/shard_map/ppermute | solution.py:92
  103.3 0.0 collective-permute-done.14.lo
  103.3 1.7 %collective-permute-done.15.hi = f32[96,128]{1,0:T(8,128)S(1)} collective-permute-done((f32[96,128]{1,0:T(8,128)S(1)}, f32[96,128]{1,0:T(8,128)S(1)}, u32[]{:S(2)}, u32[]{:S(2)}) %collective-permute-start.15) | collective-permute-done | bytes 49184 | tf_op jit(solution)/shard_map/ppermute | solution.py:92
  105.0 8.4 %shard_map.56 = (f32[512,128]{1,0:T(8,128)S(1)}, f32[512,128]{1,0:T(8,128)S(1)}, f32[512,128]{1,0:T(8,128)S(1)}, f32[8,128]{1,0:T(8,128)S(1)}) custom-call(f32[1536,128]{1,0:T(8,128)S(1)} %get-tuple-element.53.we, f32[96,128]{1,0:T(8,128)S(1)} %collective-permute-done.14.lo, f32[96,128]{1,0:T(8,128)S(1)} %collective-permute-done.15.hi, ...), custom_call_target="tpu_custom_call" | custom-call | tf_op jit(solution)/shard_map/pallas_call | solution.py:67
  113.5 10.2 %all_to_all.10 = f32[8,8,128]{2,1,0:T(8,128)S(1)} all-to-all(f32[8,8,128]{2,1,0:T(8,128)S(1)} %broadcast_in_dim.4), channel_id=1, replica_groups=mesh['gx'=8,'gy'=16,'gz'=4] {'gx'}, dimensions={0} | all-to-all | bytes 65536 | tf_op jit(solution)/shard_map/all_to_all | solution.py:386
  123.6 20.7 %all_to_all.11 = f32[16,8,128]{2,1,0:T(8,128)S(1)} all-to-all(f32[16,8,128]{2,1,0:T(8,128)S(1)} %broadcast_in_dim.5), channel_id=1, replica_groups=mesh['gx'=8,'gy'=16,'gz'=4] {'gy'}, dimensions={0} | all-to-all | bytes 131072 | tf_op jit(solution)/shard_map/all_to_all | solution.py:386
  144.4 10.7 %psum.7.dots = f32[8,128]{1,0:T(8,128)S(1)} all-reduce(f32[8,128]{1,0:T(8,128)S(1)} %reduce_sum.19), channel_id=1, replica_groups=mesh['gx'=8,'gy'=16,'gz'=4] {'gz'}, use_global_device_ids=true, to_apply=%region_2.0 | all-reduce | flops 1024 | bytes 8192 | tf_op jit(solution)/shard_map/psum | solution.py:387
  155.1 1.0 shard_map.57
  (6 shorter events, 0.1 us)
Async XLA Ops:
  0.6 39.6 %copy-start.1 = (f32[32,16,128]{2,1,0:T(8,128)S(1)}, f32[32,16,128]{2,1,0:T(8,128)}, u32[]{:S(2)}) copy-start(f32[32,16,128]{2,1,0:T(8,128)} %param.3) | copy-start | bytes 786436
  0.6 39.6 %copy-start.2 = (f32[32,16,128]{2,1,0:T(8,128)S(1)}, f32[32,16,128]{2,1,0:T(8,128)}, u32[]{:S(2)}) copy-start(f32[32,16,128]{2,1,0:T(8,128)} %param.5) | copy-start | bytes 786436
  2.0 38.2 %copy-start = (f32[32,16,128]{2,1,0:T(8,128)S(1)}, f32[32,16,128]{2,1,0:T(8,128)}, u32[]{:S(2)}) copy-start(f32[32,16,128]{2,1,0:T(8,128)} %param.4) | copy-start | bytes 786436
  2.0 38.1 %collective-permute-start.2 = (f32[544,128]{1,0:T(8,128)S(1)}, f32[544,128]{1,0:T(8,128)S(1)}, u32[]{:S(2)}, u32[]{:S(2)}) collective-permute-start(f32[544,128]{1,0:T(8,128)S(1)} %get-tuple-element.36), channel_id=1, source_target_pairs={{0,4},{4,0},{8,12},{12,8},{16,20},{20,16},{24,28},{28,24},{32,36},... | collective-permute-start | bytes 835592 | tf_op jit(solution)/shard_map/ppermute | solution.py:91
  6.5 33.6 %collective-permute-start.3 = (f32[544,128]{1,0:T(8,128)S(1)}, f32[544,128]{1,0:T(8,128)S(1)}, u32[]{:S(2)}, u32[]{:S(2)}) collective-permute-start(f32[544,128]{1,0:T(8,128)S(1)} %get-tuple-element.37), channel_id=1, source_target_pairs={{4,8},{8,4},{12,16},{16,12},{20,24},{24,20},{28,32},{32,28},{36,40... | collective-permute-start | bytes 835592 | tf_op jit(solution)/shard_map/ppermute | solution.py:92
  7.2 10.8 %collective-permute-start = (f32[272,128]{1,0:T(8,128)S(1)}, f32[272,128]{1,0:T(8,128)S(1)}, u32[]{:S(2)}, u32[]{:S(2)}) collective-permute-start(f32[272,128]{1,0:T(8,128)S(1)} %get-tuple-element.34), channel_id=1, source_target_pairs={{0,1},{1,2},{2,3},{4,5},{5,6},{6,7},{8,9},{9,10},{10,11},{12,13},{... | collective-permute-start | bytes 417800 | tf_op jit(solution)/shard_map/ppermute | solution.py:80
  16.1 10.7 %collective-permute-start.1 = (f32[272,128]{1,0:T(8,128)S(1)}, f32[272,128]{1,0:T(8,128)S(1)}, u32[]{:S(2)}, u32[]{:S(2)}) collective-permute-start(f32[272,128]{1,0:T(8,128)S(1)} %get-tuple-element.35), channel_id=1, source_target_pairs={{1,0},{2,1},{3,2},{5,4},{6,5},{7,6},{9,8},{10,9},{11,10},{13,12},{... | collective-permute-start | bytes 417800 | tf_op jit(solution)/shard_map/ppermute | solution.py:80
  26.8 13.3 %collective-permute-start.4 = (f32[88,128]{1,0:T(8,128)S(1)}, f32[88,128]{1,0:T(8,128)S(1)}, u32[]{:S(2)}, u32[]{:S(2)}) collective-permute-start(f32[88,128]{1,0:T(8,128)S(1)} %get-tuple-element.38), channel_id=1, source_target_pairs={{0,4},{4,0},{8,12},{12,8},{16,20},{20,16},{24,28},{28,24},{32,36},... | collective-permute-start | bytes 135176 | tf_op jit(solution)/shard_map/ppermute | solution.py:91
  38.7 1.4 collective-permute-start.5
  41.1 7.5 %collective-permute-start.6 = (f32[288,128]{1,0:T(8,128)S(1)}, f32[288,128]{1,0:T(8,128)S(1)}, u32[]{:S(2)}, u32[]{:S(2)}) collective-permute-start(f32[288,128]{1,0:T(8,128)S(1)} %get-tuple-element.43), channel_id=1, source_target_pairs={{0,64},{64,0},{128,192},{192,128},{256,320},{320,256},{384,448},{4... | collective-permute-start | bytes 442376 | tf_op jit(solution)/shard_map/ppermute | solution.py:91
  45.5 6.5 %collective-permute-start.7 = (f32[288,128]{1,0:T(8,128)S(1)}, f32[288,128]{1,0:T(8,128)S(1)}, u32[]{:S(2)}, u32[]{:S(2)}) collective-permute-start(f32[288,128]{1,0:T(8,128)S(1)} %get-tuple-element.44), channel_id=1, source_target_pairs={{64,128},{128,64},{192,256},{256,192},{320,384},{384,320},{65,129}... | collective-permute-start | bytes 442376 | tf_op jit(solution)/shard_map/ppermute | solution.py:92
  58.1 36.8 %collective-permute-start.10 = (f32[256,128]{1,0:T(8,128)S(1)}, f32[256,128]{1,0:T(8,128)S(1)}, u32[]{:S(2)}, u32[]{:S(2)}) collective-permute-start(f32[256,128]{1,0:T(8,128)S(1)} %get-tuple-element.49), channel_id=1, source_target_pairs={{0,4},{4,0},{8,12},{12,8},{16,20},{20,16},{24,28},{28,24},{32,36},... | collective-permute-start | bytes 393224 | tf_op jit(solution)/shard_map/ppermute | solution.py:91
  67.9 26.9 %collective-permute-start.11 = (f32[256,128]{1,0:T(8,128)S(1)}, f32[256,128]{1,0:T(8,128)S(1)}, u32[]{:S(2)}, u32[]{:S(2)}) collective-permute-start(f32[256,128]{1,0:T(8,128)S(1)} %get-tuple-element.50), channel_id=1, source_target_pairs={{4,8},{8,4},{12,16},{16,12},{20,24},{24,20},{28,32},{32,28},{36,40... | collective-permute-start | bytes 393224 | tf_op jit(solution)/shard_map/ppermute | solution.py:92
  68.6 8.0 %collective-permute-start.8 = (f32[128,128]{1,0:T(8,128)S(1)}, f32[128,128]{1,0:T(8,128)S(1)}, u32[]{:S(2)}, u32[]{:S(2)}) collective-permute-start(f32[128,128]{1,0:T(8,128)S(1)} %get-tuple-element.47), channel_id=1, source_target_pairs={{0,1},{1,2},{2,3},{4,5},{5,6},{6,7},{8,9},{9,10},{10,11},{12,13},{... | collective-permute-start | bytes 196616 | tf_op jit(solution)/shard_map/ppermute | solution.py:80
  75.3 8.9 %collective-permute-start.9 = (f32[128,128]{1,0:T(8,128)S(1)}, f32[128,128]{1,0:T(8,128)S(1)}, u32[]{:S(2)}, u32[]{:S(2)}) collective-permute-start(f32[128,128]{1,0:T(8,128)S(1)} %get-tuple-element.48), channel_id=1, source_target_pairs={{1,0},{2,1},{3,2},{5,4},{6,5},{7,6},{9,8},{10,9},{11,10},{13,12},{... | collective-permute-start | bytes 196616 | tf_op jit(solution)/shard_map/ppermute | solution.py:80
  84.3 10.6 %collective-permute-start.12 = (f32[56,128]{1,0:T(8,128)S(1)}, f32[56,128]{1,0:T(8,128)S(1)}, u32[]{:S(2)}, u32[]{:S(2)}) collective-permute-start(f32[56,128]{1,0:T(8,128)S(1)} %get-tuple-element.51), channel_id=1, source_target_pairs={{0,4},{4,0},{8,12},{12,8},{16,20},{20,16},{24,28},{28,24},{32,36},... | collective-permute-start | bytes 86024 | tf_op jit(solution)/shard_map/ppermute | solution.py:91
  93.6 1.2 collective-permute-start.13
  95.3 8.0 %collective-permute-start.14 = (f32[96,128]{1,0:T(8,128)S(1)}, f32[96,128]{1,0:T(8,128)S(1)}, u32[]{:S(2)}, u32[]{:S(2)}) collective-permute-start(f32[96,128]{1,0:T(8,128)S(1)} %get-tuple-element.54), channel_id=1, source_target_pairs={{0,64},{64,0},{128,192},{192,128},{256,320},{320,256},{384,448},{4... | collective-permute-start | bytes 147464 | tf_op jit(solution)/shard_map/ppermute | solution.py:91
  97.2 7.8 %collective-permute-start.15 = (f32[96,128]{1,0:T(8,128)S(1)}, f32[96,128]{1,0:T(8,128)S(1)}, u32[]{:S(2)}, u32[]{:S(2)}) collective-permute-start(f32[96,128]{1,0:T(8,128)S(1)} %get-tuple-element.55), channel_id=1, source_target_pairs={{64,128},{128,64},{192,256},{256,192},{320,384},{384,320},{65,129}... | collective-permute-start | bytes 147464 | tf_op jit(solution)/shard_map/ppermute | solution.py:92

commit v8 on v7

--- a/solution.py
+++ b/solution.py
@@ -191,8 +191,8 @@
         pack_lanes(lambda z: out[z * FY : (z + 1) * FY, :], dn_ref, up_ref, f * Q_PACK)
 
 
-PLANES = 8
-GROUP = 4
+TRIPS = 1
+GROUP = 1
 
 
 class Window:
@@ -237,16 +237,13 @@
         for k in range(0, n, GROUP):
             group([z + k + i for i in range(min(GROUP, n - k))])
 
-    count = win.last - win.first
-    whole = count // PLANES
+    planes = (win.last - win.first) // TRIPS
 
     def step(i, _):
-        some(win.first + i * PLANES, PLANES)
+        some(win.first + i * planes, planes)
         return 0
 
-    lax.fori_loop(0, whole, step, 0)
-    if count % PLANES:
-        some(win.first + whole * PLANES, count % PLANES)
+    lax.fori_loop(0, TRIPS, step, 0)
 
 
 def block_rows(z):
@@ -362,17 +359,18 @@
 
 
 def finish(x_ref, r_ref, w_ref, v1, v2, v3, dots, x_out, r_out):
-    def total(i, scale):
-        return jnp.sum(dots[i : i + 1, :], axis=1, keepdims=True) * (1.0 / scale)
-
-    e0 = total(0, 1.0)
-    g0 = total(1, SQ)
-    h = total(2, SQ**2)
-    k = total(3, SQ**3)
-    a0 = e0 / g0
-    e1 = a0 * a0 * h - e0
+    def lanes(i, scale):
+        return dots[i : i + 1, :] * (1.0 / scale)
+
+    def total(v):
+        return jnp.sum(v, axis=1, keepdims=True)
+
+    e, g, h, k = (lanes(i, SQ**i) for i in range(4))
+    e0 = total(e)
+    a0 = e0 / total(g)
+    e1 = total(e - a0 * (2.0 * g - a0 * h))
     beta = 1.0 + e1 / e0
-    a1 = e1 / (beta * beta * g0 - 2.0 * beta * a0 * h + a0 * a0 * k)
+    a1 = e1 / total(beta * beta * g - a0 * (2.0 * beta * h - a0 * k))
     near = a0 + a1 * beta
     far = a1 * a0
     x_out[...] = x_ref[...] + near * w_ref[...] - (far * (1.0 / SQ)) * v2[...]

time: 158 us -> 153 us (0.968)
  Pallas kernels: 18.3 us -> 13 us
    pallas_call x8, Pallas kernels: 18.3 us -> 13 us  [run(): pl.pallas_call(kernel, out_shape=[jax.ShapeDtypeStruct(s, f32) for s in o...]
where the time goes in v8:
time: 153 us; the launch traced here: 151 us
  starting transfers between devices  71.8 us (47%)
  blocking collectives  41.6 us (27%)
  waiting for transfers between devices  23.5 us (15%)
  Pallas kernels  13 us (8%)
    ppermute x6, starting transfers between devices, swap(): a = lax.ppermute(mine_a, axis, [(i, i ^ 1) for i in range(n)])  41.8 us
    all_to_all x2, blocking collectives, all_sum(): x = jnp.sum(lax.all_to_all(copies, axis, 0, 0), axis=0)  30.9 us
    ppermute x4, starting transfers between devices, shift(): return lax.ppermute(x, axis, pairs)  18.1 us
    ppermute x4, waiting for transfers between devices, shift(): return lax.ppermute(x, axis, pairs)  17 us
    pallas_call x8, Pallas kernels, run(): pl.pallas_call(kernel, out_shape=[jax.ShapeDtypeStruct(s, f32) for s in o...  13 us
    ppermute x6, starting transfers between devices, swap(): lax.ppermute(mine_b, axis, [(i, i + 1 if i % 2 else i - 1) for i in range...  11.8 us
    psum x1, blocking collectives, all_sum(): return lax.psum(x, 'gz')  10.7 us
    ppermute x6, waiting for transfers between devices, swap(): lax.ppermute(mine_b, axis, [(i, i + 1 if i % 2 else i - 1) for i in range...  5.1 us
  transfers between devices with their start and end apart: 16, of which 7 were waited for; matrix products, arithmetic and copies ran while one was open for 0% of the time, Pallas kernels for 0%

profile of v8, /device:TPU:1, one launch (start us, length us, event | category | flops | bytes accessed | tf_op | source)
XLA Modules:
  0.0 150.8 jit_solution(11502054461405762965)
XLA Ops:
  0.6 0.0 copy-start.1
  0.6 0.0 copy-start.2
  0.6 1.4 shard_map.50
  2.0 0.0 copy-start
  2.0 4.5 %collective-permute-start.2 = (f32[544,128]{1,0:T(8,128)S(1)}, f32[544,128]{1,0:T(8,128)S(1)}, u32[]{:S(2)}, u32[]{:S(2)}) collective-permute-start(f32[544,128]{1,0:T(8,128)S(1)} %get-tuple-element.36), channel_id=1, source_target_pairs={{0,4},{4,0},{8,12},{12,8},{16,20},{20,16},{24,28},{28,24},{32,36},... | collective-permute-start | bytes 835592 | tf_op jit(solution)/shard_map/ppermute | solution.py:91
  6.5 0.7 collective-permute-start.3
  7.2 8.8 %collective-permute-start = (f32[272,128]{1,0:T(8,128)S(1)}, f32[272,128]{1,0:T(8,128)S(1)}, u32[]{:S(2)}, u32[]{:S(2)}) collective-permute-start(f32[272,128]{1,0:T(8,128)S(1)} %get-tuple-element.34), channel_id=1, source_target_pairs={{0,1},{1,2},{2,3},{4,5},{5,6},{6,7},{8,9},{9,10},{10,11},{12,13},{... | collective-permute-start | bytes 417800 | tf_op jit(solution)/shard_map/ppermute | solution.py:80
  16.1 1.3 collective-permute-start.1
  17.4 0.7 collective-permute-done.lo_ref.zlo
  18.1 8.7 %collective-permute-done.1.hi_ref.zhi = f32[272,128]{1,0:T(8,128)S(1)} collective-permute-done((f32[272,128]{1,0:T(8,128)S(1)}, f32[272,128]{1,0:T(8,128)S(1)}, u32[]{:S(2)}, u32[]{:S(2)}) %collective-permute-start.1) | collective-permute-done | bytes 139296 | tf_op jit(solution)/shard_map/ppermute | solution.py:80
  26.8 11.9 %collective-permute-start.4 = (f32[88,128]{1,0:T(8,128)S(1)}, f32[88,128]{1,0:T(8,128)S(1)}, u32[]{:S(2)}, u32[]{:S(2)}) collective-permute-start(f32[88,128]{1,0:T(8,128)S(1)} %get-tuple-element.38), channel_id=1, source_target_pairs={{0,4},{4,0},{8,12},{12,8},{16,20},{20,16},{24,28},{28,24},{32,36},... | collective-permute-start | bytes 135176 | tf_op jit(solution)/shard_map/ppermute | solution.py:91
  38.7 0.7 collective-permute-start.5
  39.4 0.7 collective-permute-done.4.ca
  40.2 0.0 collective-permute-done.5.cb
  40.2 0.0 collective-permute-done.2.ya
  40.2 0.0 collective-permute-done.3.yb
  40.2 0.0 copy-done.1
  40.2 0.0 copy-done.2
  40.2 0.0 copy-done
  40.2 0.9 shard_map.52
  41.1 4.3 %collective-permute-start.6 = (f32[288,128]{1,0:T(8,128)S(1)}, f32[288,128]{1,0:T(8,128)S(1)}, u32[]{:S(2)}, u32[]{:S(2)}) collective-permute-start(f32[288,128]{1,0:T(8,128)S(1)} %get-tuple-element.43), channel_id=1, source_target_pairs={{0,64},{64,0},{128,192},{192,128},{256,320},{320,256},{384,448},{4... | collective-permute-start | bytes 442376 | tf_op jit(solution)/shard_map/ppermute | solution.py:91
  45.5 3.1 %collective-permute-start.7 = (f32[288,128]{1,0:T(8,128)S(1)}, f32[288,128]{1,0:T(8,128)S(1)}, u32[]{:S(2)}, u32[]{:S(2)}) collective-permute-start(f32[288,128]{1,0:T(8,128)S(1)} %get-tuple-element.44), channel_id=1, source_target_pairs={{64,128},{128,64},{192,256},{256,192},{320,384},{384,320},{65,129}... | collective-permute-start | bytes 442376 | tf_op jit(solution)/shard_map/ppermute | solution.py:92
  48.6 0.0 collective-permute-done.6.rest_1_
  48.6 3.3 %collective-permute-done.7.rest_2_ = f32[288,128]{1,0:T(8,128)S(1)} collective-permute-done((f32[288,128]{1,0:T(8,128)S(1)}, f32[288,128]{1,0:T(8,128)S(1)}, u32[]{:S(2)}, u32[]{:S(2)}) %collective-permute-start.7) | collective-permute-done | bytes 147488 | tf_op jit(solution)/shard_map/ppermute | solution.py:92
  52.0 3.8 %shard_map.53 = (f32[512,128]{1,0:T(8,128)S(1)}, f32[512,128]{1,0:T(8,128)S(1)}, f32[128,128]{1,0:T(8,128)S(1)}, f32[128,128]{1,0:T(8,128)S(1)}, f32[256,128]{1,...) custom-call(f32[1536,128]{1,0:T(8,128)S(1)} %get-tuple-element.40.xe, ...), custom_call_target="tpu_custom_call" | custom-call | tf_op jit(solution)/shard_map/pallas_call | solution.py:67
  55.8 9.8 %collective-permute-start.10 = (f32[256,128]{1,0:T(8,128)S(1)}, f32[256,128]{1,0:T(8,128)S(1)}, u32[]{:S(2)}, u32[]{:S(2)}) collective-permute-start(f32[256,128]{1,0:T(8,128)S(1)} %get-tuple-element.49), channel_id=1, source_target_pairs={{0,4},{4,0},{8,12},{12,8},{16,20},{20,16},{24,28},{28,24},{32,36},... | collective-permute-start | bytes 393224 | tf_op jit(solution)/shard_map/ppermute | solution.py:91
  65.6 0.7 collective-permute-start.11
  66.3 6.7 %collective-permute-start.8 = (f32[128,128]{1,0:T(8,128)S(1)}, f32[128,128]{1,0:T(8,128)S(1)}, u32[]{:S(2)}, u32[]{:S(2)}) collective-permute-start(f32[128,128]{1,0:T(8,128)S(1)} %get-tuple-element.47), channel_id=1, source_target_pairs={{0,1},{1,2},{2,3},{4,5},{5,6},{6,7},{8,9},{9,10},{10,11},{12,13},{... | collective-permute-start | bytes 196616 | tf_op jit(solution)/shard_map/ppermute | solution.py:80
  73.0 1.3 collective-permute-start.9
  74.3 0.0 collective-permute-done.8.lo_ref.zlo
  74.3 7.6 %collective-permute-done.9.hi_ref.zhi = f32[128,128]{1,0:T(8,128)S(1)} collective-permute-done((f32[128,128]{1,0:T(8,128)S(1)}, f32[128,128]{1,0:T(8,128)S(1)}, u32[]{:S(2)}, u32[]{:S(2)}) %collective-permute-start.9) | collective-permute-done | bytes 65568 | tf_op jit(solution)/shard_map/ppermute | solution.py:80
  81.9 9.3 %collective-permute-start.12 = (f32[56,128]{1,0:T(8,128)S(1)}, f32[56,128]{1,0:T(8,128)S(1)}, u32[]{:S(2)}, u32[]{:S(2)}) collective-permute-start(f32[56,128]{1,0:T(8,128)S(1)} %get-tuple-element.51), channel_id=1, source_target_pairs={{0,4},{4,0},{8,12},{12,8},{16,20},{20,16},{24,28},{28,24},{32,36},... | collective-permute-start | bytes 86024 | tf_op jit(solution)/shard_map/ppermute | solution.py:91
  91.3 0.7 collective-permute-start.13
  91.9 0.6 collective-permute-done.12.ca
  92.5 0.0 collective-permute-done.13.cb
  92.5 0.0 collective-permute-done.10.ya
  92.5 0.0 collective-permute-done.11.yb
  92.5 0.4 shard_map.55
  92.9 1.9 %collective-permute-start.14 = (f32[96,128]{1,0:T(8,128)S(1)}, f32[96,128]{1,0:T(8,128)S(1)}, u32[]{:S(2)}, u32[]{:S(2)}) collective-permute-start(f32[96,128]{1,0:T(8,128)S(1)} %get-tuple-element.54), channel_id=1, source_target_pairs={{0,64},{64,0},{128,192},{192,128},{256,320},{320,256},{384,448},{4... | collective-permute-start | bytes 147464 | tf_op jit(solution)/shard_map/ppermute | solution.py:91
  94.9 6.1 %collective-permute-start.15 = (f32[96,128]{1,0:T(8,128)S(1)}, f32[96,128]{1,0:T(8,128)S(1)}, u32[]{:S(2)}, u32[]{:S(2)}) collective-permute-start(f32[96,128]{1,0:T(8,128)S(1)} %get-tuple-element.55), channel_id=1, source_target_pairs={{64,128},{128,64},{192,256},{256,192},{320,384},{384,320},{65,129}... | collective-permute-start | bytes 147464 | tf_op jit(solution)/shard_map/ppermute | solution.py:92
  100.9 0.0 collective-permute-done.14.lo
  101.0 1.7 %collective-permute-done.15.hi = f32[96,128]{1,0:T(8,128)S(1)} collective-permute-done((f32[96,128]{1,0:T(8,128)S(1)}, f32[96,128]{1,0:T(8,128)S(1)}, u32[]{:S(2)}, u32[]{:S(2)}) %collective-permute-start.15) | collective-permute-done | bytes 49184 | tf_op jit(solution)/shard_map/ppermute | solution.py:92
  102.7 5.3 %shard_map.56 = (f32[512,128]{1,0:T(8,128)S(1)}, f32[512,128]{1,0:T(8,128)S(1)}, f32[512,128]{1,0:T(8,128)S(1)}, f32[8,128]{1,0:T(8,128)S(1)}) custom-call(f32[1536,128]{1,0:T(8,128)S(1)} %get-tuple-element.53.we, f32[96,128]{1,0:T(8,128)S(1)} %collective-permute-done.14.lo, f32[96,128]{1,0:T(8,128)S(1)} %collective-permute-done.15.hi, ...), custom_call_target="tpu_custom_call" | custom-call | tf_op jit(solution)/shard_map/pallas_call | solution.py:67
  108.1 10.2 %all_to_all.10 = f32[8,8,128]{2,1,0:T(8,128)S(1)} all-to-all(f32[8,8,128]{2,1,0:T(8,128)S(1)} %broadcast_in_dim.4), channel_id=1, replica_groups=mesh['gx'=8,'gy'=16,'gz'=4] {'gx'}, dimensions={0} | all-to-all | bytes 65536 | tf_op jit(solution)/shard_map/all_to_all | solution.py:384
  118.2 20.7 %all_to_all.11 = f32[16,8,128]{2,1,0:T(8,128)S(1)} all-to-all(f32[16,8,128]{2,1,0:T(8,128)S(1)} %broadcast_in_dim.5), channel_id=1, replica_groups=mesh['gx'=8,'gy'=16,'gz'=4] {'gy'}, dimensions={0} | all-to-all | bytes 131072 | tf_op jit(solution)/shard_map/all_to_all | solution.py:384
  139.0 10.7 %psum.7.dots = f32[8,128]{1,0:T(8,128)S(1)} all-reduce(f32[8,128]{1,0:T(8,128)S(1)} %reduce_sum.19), channel_id=1, replica_groups=mesh['gx'=8,'gy'=16,'gz'=4] {'gz'}, use_global_device_ids=true, to_apply=%region_2.0 | all-reduce | flops 1024 | bytes 8192 | tf_op jit(solution)/shard_map/psum | solution.py:385
  149.7 1.1 shard_map.57
  (6 shorter events, 0.1 us)
Async XLA Ops:
  0.6 39.6 %copy-start.1 = (f32[32,16,128]{2,1,0:T(8,128)S(1)}, f32[32,16,128]{2,1,0:T(8,128)}, u32[]{:S(2)}) copy-start(f32[32,16,128]{2,1,0:T(8,128)} %param.3) | copy-start | bytes 786436
  0.6 39.6 %copy-start.2 = (f32[32,16,128]{2,1,0:T(8,128)S(1)}, f32[32,16,128]{2,1,0:T(8,128)}, u32[]{:S(2)}) copy-start(f32[32,16,128]{2,1,0:T(8,128)} %param.5) | copy-start | bytes 786436
  2.0 38.2 %copy-start = (f32[32,16,128]{2,1,0:T(8,128)S(1)}, f32[32,16,128]{2,1,0:T(8,128)}, u32[]{:S(2)}) copy-start(f32[32,16,128]{2,1,0:T(8,128)} %param.4) | copy-start | bytes 786436
  2.0 38.1 %collective-permute-start.2 = (f32[544,128]{1,0:T(8,128)S(1)}, f32[544,128]{1,0:T(8,128)S(1)}, u32[]{:S(2)}, u32[]{:S(2)}) collective-permute-start(f32[544,128]{1,0:T(8,128)S(1)} %get-tuple-element.36), channel_id=1, source_target_pairs={{0,4},{4,0},{8,12},{12,8},{16,20},{20,16},{24,28},{28,24},{32,36},... | collective-permute-start | bytes 835592 | tf_op jit(solution)/shard_map/ppermute | solution.py:91
  6.5 33.6 %collective-permute-start.3 = (f32[544,128]{1,0:T(8,128)S(1)}, f32[544,128]{1,0:T(8,128)S(1)}, u32[]{:S(2)}, u32[]{:S(2)}) collective-permute-start(f32[544,128]{1,0:T(8,128)S(1)} %get-tuple-element.37), channel_id=1, source_target_pairs={{4,8},{8,4},{12,16},{16,12},{20,24},{24,20},{28,32},{32,28},{36,40... | collective-permute-start | bytes 835592 | tf_op jit(solution)/shard_map/ppermute | solution.py:92
  7.2 10.8 %collective-permute-start = (f32[272,128]{1,0:T(8,128)S(1)}, f32[272,128]{1,0:T(8,128)S(1)}, u32[]{:S(2)}, u32[]{:S(2)}) collective-permute-start(f32[272,128]{1,0:T(8,128)S(1)} %get-tuple-element.34), channel_id=1, source_target_pairs={{0,1},{1,2},{2,3},{4,5},{5,6},{6,7},{8,9},{9,10},{10,11},{12,13},{... | collective-permute-start | bytes 417800 | tf_op jit(solution)/shard_map/ppermute | solution.py:80
  16.1 10.7 %collective-permute-start.1 = (f32[272,128]{1,0:T(8,128)S(1)}, f32[272,128]{1,0:T(8,128)S(1)}, u32[]{:S(2)}, u32[]{:S(2)}) collective-permute-start(f32[272,128]{1,0:T(8,128)S(1)} %get-tuple-element.35), channel_id=1, source_target_pairs={{1,0},{2,1},{3,2},{5,4},{6,5},{7,6},{9,8},{10,9},{11,10},{13,12},{... | collective-permute-start | bytes 417800 | tf_op jit(solution)/shard_map/ppermute | solution.py:80
  26.8 13.3 %collective-permute-start.4 = (f32[88,128]{1,0:T(8,128)S(1)}, f32[88,128]{1,0:T(8,128)S(1)}, u32[]{:S(2)}, u32[]{:S(2)}) collective-permute-start(f32[88,128]{1,0:T(8,128)S(1)} %get-tuple-element.38), channel_id=1, source_target_pairs={{0,4},{4,0},{8,12},{12,8},{16,20},{20,16},{24,28},{28,24},{32,36},... | collective-permute-start | bytes 135176 | tf_op jit(solution)/shard_map/ppermute | solution.py:91
  38.7 1.4 collective-permute-start.5
  41.1 7.5 %collective-permute-start.6 = (f32[288,128]{1,0:T(8,128)S(1)}, f32[288,128]{1,0:T(8,128)S(1)}, u32[]{:S(2)}, u32[]{:S(2)}) collective-permute-start(f32[288,128]{1,0:T(8,128)S(1)} %get-tuple-element.43), channel_id=1, source_target_pairs={{0,64},{64,0},{128,192},{192,128},{256,320},{320,256},{384,448},{4... | collective-permute-start | bytes 442376 | tf_op jit(solution)/shard_map/ppermute | solution.py:91
  45.5 6.5 %collective-permute-start.7 = (f32[288,128]{1,0:T(8,128)S(1)}, f32[288,128]{1,0:T(8,128)S(1)}, u32[]{:S(2)}, u32[]{:S(2)}) collective-permute-start(f32[288,128]{1,0:T(8,128)S(1)} %get-tuple-element.44), channel_id=1, source_target_pairs={{64,128},{128,64},{192,256},{256,192},{320,384},{384,320},{65,129}... | collective-permute-start | bytes 442376 | tf_op jit(solution)/shard_map/ppermute | solution.py:92
  55.8 36.8 %collective-permute-start.10 = (f32[256,128]{1,0:T(8,128)S(1)}, f32[256,128]{1,0:T(8,128)S(1)}, u32[]{:S(2)}, u32[]{:S(2)}) collective-permute-start(f32[256,128]{1,0:T(8,128)S(1)} %get-tuple-element.49), channel_id=1, source_target_pairs={{0,4},{4,0},{8,12},{12,8},{16,20},{20,16},{24,28},{28,24},{32,36},... | collective-permute-start | bytes 393224 | tf_op jit(solution)/shard_map/ppermute | solution.py:91
  65.6 26.9 %collective-permute-start.11 = (f32[256,128]{1,0:T(8,128)S(1)}, f32[256,128]{1,0:T(8,128)S(1)}, u32[]{:S(2)}, u32[]{:S(2)}) collective-permute-start(f32[256,128]{1,0:T(8,128)S(1)} %get-tuple-element.50), channel_id=1, source_target_pairs={{4,8},{8,4},{12,16},{16,12},{20,24},{24,20},{28,32},{32,28},{36,40... | collective-permute-start | bytes 393224 | tf_op jit(solution)/shard_map/ppermute | solution.py:92
  66.3 8.0 %collective-permute-start.8 = (f32[128,128]{1,0:T(8,128)S(1)}, f32[128,128]{1,0:T(8,128)S(1)}, u32[]{:S(2)}, u32[]{:S(2)}) collective-permute-start(f32[128,128]{1,0:T(8,128)S(1)} %get-tuple-element.47), channel_id=1, source_target_pairs={{0,1},{1,2},{2,3},{4,5},{5,6},{6,7},{8,9},{9,10},{10,11},{12,13},{... | collective-permute-start | bytes 196616 | tf_op jit(solution)/shard_map/ppermute | solution.py:80
  73.0 8.9 %collective-permute-start.9 = (f32[128,128]{1,0:T(8,128)S(1)}, f32[128,128]{1,0:T(8,128)S(1)}, u32[]{:S(2)}, u32[]{:S(2)}) collective-permute-start(f32[128,128]{1,0:T(8,128)S(1)} %get-tuple-element.48), channel_id=1, source_target_pairs={{1,0},{2,1},{3,2},{5,4},{6,5},{7,6},{9,8},{10,9},{11,10},{13,12},{... | collective-permute-start | bytes 196616 | tf_op jit(solution)/shard_map/ppermute | solution.py:80
  81.9 10.6 %collective-permute-start.12 = (f32[56,128]{1,0:T(8,128)S(1)}, f32[56,128]{1,0:T(8,128)S(1)}, u32[]{:S(2)}, u32[]{:S(2)}) collective-permute-start(f32[56,128]{1,0:T(8,128)S(1)} %get-tuple-element.51), channel_id=1, source_target_pairs={{0,4},{4,0},{8,12},{12,8},{16,20},{20,16},{24,28},{28,24},{32,36},... | collective-permute-start | bytes 86024 | tf_op jit(solution)/shard_map/ppermute | solution.py:91
  91.3 1.2 collective-permute-start.13
  92.9 8.0 %collective-permute-start.14 = (f32[96,128]{1,0:T(8,128)S(1)}, f32[96,128]{1,0:T(8,128)S(1)}, u32[]{:S(2)}, u32[]{:S(2)}) collective-permute-start(f32[96,128]{1,0:T(8,128)S(1)} %get-tuple-element.54), channel_id=1, source_target_pairs={{0,64},{64,0},{128,192},{192,128},{256,320},{320,256},{384,448},{4... | collective-permute-start | bytes 147464 | tf_op jit(solution)/shard_map/ppermute | solution.py:91
  94.9 7.8 %collective-permute-start.15 = (f32[96,128]{1,0:T(8,128)S(1)}, f32[96,128]{1,0:T(8,128)S(1)}, u32[]{:S(2)}, u32[]{:S(2)}) collective-permute-start(f32[96,128]{1,0:T(8,128)S(1)} %get-tuple-element.55), channel_id=1, source_target_pairs={{64,128},{128,64},{192,256},{256,192},{320,384},{384,320},{65,129}... | collective-permute-start | bytes 147464 | tf_op jit(solution)/shard_map/ppermute | solution.py:92
